TPU v7x, 32 devices: a whole 2x2x4 slice. The times are simulated.
32 devices in a mesh: dp: 16 (over z, x, core), tensor: 2 (over y).
Axes of the slice: x: 2, y: 2, z: 4, core: 2. Of those that a mesh axis runs over, the one named last changes fastest.
Arguments:
- x_in: bfloat16 [16384, 2048], P('dp'), may hold values from -6 to 6
- norm_gain: float32 [2048], replicated, may hold values from 0.5 to 1.5
- w_zx: bfloat16 [2048, 2, 4096], P(None, None, 'tensor'), may hold values from -0.125 to 0.125
- w_bc: bfloat16 [2048, 256], replicated, may hold values from -0.125 to 0.125
- w_dt: bfloat16 [2048, 64], P(None, 'tensor'), may hold values from -0.125 to 0.125
- conv_x: float32 [5, 4096], P(None, 'tensor'), may hold values from -3 to 3
- conv_bc: float32 [5, 256], replicated, may hold values from -3 to 3
- dt_bias: float32 [64], P('tensor'), may hold values from -4 to -1
- a_log: float32 [64], P('tensor'), may hold values from -3 to 1.5
- d_skip: float32 [64], P('tensor'), may hold values from 0.5 to 1.5
- gate_gain: float32 [4096], P('tensor'), may hold values from 0.5 to 1.5
- w_out: bfloat16 [4096, 2048], P('tensor'), may hold values from -0.09375 to 0.09375
- cotangent: bfloat16 [16384, 2048], P('dp'), may hold values from -6 to 6
- block_parent: int32 [128], P('dp'), may hold values from -1 to 6, as said below
Outputs:
- mixed: bfloat16 [16384, 2048], P('dp')
- input_grad: bfloat16 [16384, 2048], P('dp')
- norm_gain_grad: float32 [2048], replicated
- w_zx_grad: float32 [2048, 2, 4096], P('dp', None, 'tensor')
- w_bc_grad: float32 [2048, 256], replicated
- w_dt_grad: float32 [2048, 64], P('dp', 'tensor')
- conv_x_grad: float32 [5, 4096], P(None, 'tensor')
- conv_bc_grad: float32 [5, 256], replicated
- dt_bias_grad: float32 [64], P('tensor')
- a_log_grad: float32 [64], P('tensor')
- d_skip_grad: float32 [64], P('tensor')
- gate_gain_grad: float32 [4096], P('tensor')
- w_out_grad: float32 [4096, 2048], P('tensor', 'dp')
Inputs may be any that keep to these rules, and one draw needn't show every extreme that they name: `block_parent`: each device's 8 blocks hold one tree. A block's entry is the index, among its device's blocks, of an earlier block whose last token precedes its first token, or -1 at the root; the first half of the blocks or more form a chain from the root, and the last block continues the block before it.
All inputs are finite; a program needn't handle non-finite values.
Results may differ from a plain program's by a relative error of at most 0.014.
Values may be sent and summed in bfloat16 or wider, within the bound.
No kernel may reach another device: no remote copies, remote signals or barrier semaphores. Data moves between devices by JAX's collectives and lax.ppermute only.
A program may use at most 320 MiB of HBM per device.

v0:
```python
import jax
import jax.numpy as jnp
from jax import lax
from jax.sharding import PartitionSpec as P

epsilon = 1e-05
highest = lax.Precision.HIGHEST


def conv_path(inputs, kernel, parent):
    blocks = parent.shape[0]
    tokens, channels = inputs.shape
    window = kernel.shape[0] - 1
    block_len = tokens // blocks
    blocked = inputs.reshape(blocks, block_len, channels)
    trailing = blocked[:, block_len - (window - 1) :, :]
    context = jnp.take(trailing, jnp.maximum(parent, 0), axis=0)
    context = jnp.where((parent >= 0)[:, None, None], context, jnp.zeros_like(context))
    padded = jnp.concatenate([context, blocked], axis=1)
    summed = kernel[window][None, None, :] + jnp.zeros_like(blocked)
    for offset in range(window):
        summed = summed + kernel[offset][None, None, :] * padded[:, offset : offset + block_len, :]
    return jax.nn.silu(summed).reshape(tokens, channels)


def decay_paths(block_decay, parent):
    blocks = parent.shape[0]
    n_heads = block_decay.shape[1]
    parent_map = (parent[:, None] == jnp.arange(blocks, dtype=jnp.int32)[None, :]).astype(
        jnp.float32
    )
    identity = jnp.eye(blocks, dtype=jnp.float32)

    def advance(turn, paths):
        return identity[None] + jnp.einsum(
            "hb,bp,hpa->hba", block_decay.T, parent_map, paths, precision=highest
        )

    paths = lax.fori_loop(0, blocks, advance, jnp.broadcast_to(identity, (n_heads, blocks, blocks)))
    return (paths, parent_map)


def ssd_mix(x_heads, b_rows, c_rows, dt_raw, dt_bias, a_log, d_skip, parent):
    tokens, n_heads, head_dim = x_heads.shape
    blocks = parent.shape[0]
    block_len = tokens // blocks
    dt_values = jax.nn.softplus(dt_raw + dt_bias)
    log_rate = dt_values * -jnp.exp(a_log)
    x_blocks = x_heads.reshape(blocks, block_len, n_heads, head_dim)
    b_blocks = b_rows.reshape(blocks, block_len, -1)
    c_blocks = c_rows.reshape(blocks, block_len, -1)
    dt_blocks = dt_values.reshape(blocks, block_len, n_heads)
    cumulant = jnp.cumsum(log_rate.reshape(blocks, block_len, n_heads), axis=1)
    scores = jnp.einsum("bin,bjn->bij", c_blocks, b_blocks, precision=highest)
    rows_idx = jnp.arange(block_len, dtype=jnp.int32)
    causal = (rows_idx[:, None] >= rows_idx[None, :])[None, :, :, None]
    log_gap = cumulant[:, :, None, :] - cumulant[:, None, :, :]
    decays = jnp.where(causal, jnp.exp(jnp.where(causal, log_gap, 0.0)), 0.0)
    weights = scores[..., None] * decays * dt_blocks[:, None, :, :]
    within = jnp.einsum("bijh,bjhp->bihp", weights, x_blocks, precision=highest)
    to_end = jnp.exp(cumulant[:, -1:, :] - cumulant) * dt_blocks
    local_states = jnp.einsum("bjh,bjhp,bjn->bhpn", to_end, x_blocks, b_blocks, precision=highest)
    paths, parent_map = decay_paths(jnp.exp(cumulant[:, -1, :]), parent)
    end_states = jnp.einsum("hba,ahpn->bhpn", paths, local_states, precision=highest)
    start_states = jnp.einsum("bq,qhpn->bhpn", parent_map, end_states, precision=highest)
    carried = jnp.exp(cumulant)[..., None] * jnp.einsum(
        "bin,bhpn->bihp", c_blocks, start_states, precision=highest
    )
    result = within + carried + d_skip[None, None, :, None] * x_blocks
    return result.reshape(tokens, n_heads * head_dim)


def gated_mix(x_heads, bc_rows, dt_raw, dt_bias, a_log, d_skip, z_gate, parent):
    half = bc_rows.shape[1] // 2
    mixed_heads = ssd_mix(
        x_heads, bc_rows[:, :half], bc_rows[:, half:], dt_raw, dt_bias, a_log, d_skip, parent
    )
    return mixed_heads * jax.nn.silu(z_gate)


def over_tokens(left, right):
    return lax.dot_general(
        left, right, (((0,), (0,)), ((), ())), preferred_element_type=jnp.float32
    )


def over_columns(left, right):
    return lax.dot_general(
        left, right, (((1,), (1,)), ((), ())), preferred_element_type=jnp.float32
    )


def rounded(value):
    return lax.optimization_barrier(value.astype(jnp.bfloat16)).astype(jnp.float32)


def local(
    x_in,
    norm_gain,
    w_zx,
    w_bc,
    w_dt,
    conv_x,
    conv_bc,
    dt_bias,
    a_log,
    d_skip,
    gate_gain,
    w_out,
    cotangent,
    block_parent,
):
    tokens, features = x_in.shape
    local_heads = w_dt.shape[1]
    inner_width = w_zx.shape[2]
    head_dim = inner_width // local_heads
    full_width = inner_width * lax.axis_size("tensor")
    x_float = x_in.astype(jnp.float32)
    inv_rms = lax.rsqrt(jnp.mean(x_float * x_float, axis=-1) + epsilon)
    normed = (x_float * inv_rms[:, None] * norm_gain).astype(jnp.bfloat16)
    z_gate = jnp.dot(normed, w_zx[:, 0, :], preferred_element_type=jnp.float32)
    x_pre = jnp.dot(normed, w_zx[:, 1, :], preferred_element_type=jnp.float32)
    bc_pre = jnp.dot(normed, w_bc, preferred_element_type=jnp.float32)
    dt_raw = jnp.dot(normed, w_dt, preferred_element_type=jnp.float32)

    def x_piece(values, kernel):
        return conv_path(values, kernel, block_parent)

    x_conv, x_pull = jax.vjp(x_piece, x_pre, conv_x)
    bc_conv, bc_pull = jax.vjp(x_piece, bc_pre, conv_bc)
    x_round = rounded(x_conv)
    bc_round = rounded(bc_conv)

    def mixer(x_values, bc_values, dt_values, bias_values, log_values, skip_values, gate_values):
        return gated_mix(
            x_values.reshape(tokens, local_heads, head_dim),
            bc_values,
            dt_values,
            bias_values,
            log_values,
            skip_values,
            gate_values,
            block_parent,
        )

    gated, mix_pull = jax.vjp(mixer, x_round, bc_round, dt_raw, dt_bias, a_log, d_skip, z_gate)
    squares = lax.psum(jnp.sum(gated * gated, axis=-1), "tensor")
    inv_gate = lax.rsqrt(squares / full_width + epsilon)
    gate_normed = (gated * inv_gate[:, None] * gate_gain).astype(jnp.bfloat16)
    partial_out = jnp.dot(gate_normed, w_out, preferred_element_type=jnp.float32)
    share = tokens // lax.axis_size("tensor")
    first_row = lax.axis_index("tensor") * share
    x_rows = lax.dynamic_slice_in_dim(x_float, first_row, share, 0)
    mixed = (
        x_float + lax.psum(partial_out.astype(jnp.bfloat16), "tensor").astype(jnp.float32)
    ).astype(jnp.bfloat16)
    d_gate_normed = over_columns(cotangent, w_out)
    w_out_part = over_tokens(gate_normed, cotangent)
    gate_gain_part = jnp.sum(d_gate_normed * gated * inv_gate[:, None], axis=0)
    scaled = d_gate_normed * gate_gain
    cross = lax.psum(jnp.sum(scaled * gated, axis=-1), "tensor")
    d_gated = (
        inv_gate[:, None] * scaled
        - gated * (inv_gate * inv_gate * inv_gate * cross / full_width)[:, None]
    )
    d_x_round, d_bc_round, d_dt_raw, dt_bias_part, a_log_part, d_skip_part, d_z_gate = mix_pull(
        d_gated
    )
    d_x_pre, conv_x_part = x_pull(d_x_round)
    d_bc_pre, conv_bc_part = bc_pull(d_bc_round)
    z_low = d_z_gate.astype(jnp.bfloat16)
    x_low = d_x_pre.astype(jnp.bfloat16)
    bc_low = d_bc_pre.astype(jnp.bfloat16)
    dt_low = d_dt_raw.astype(jnp.bfloat16)
    w_zx_part = jnp.stack([over_tokens(normed, z_low), over_tokens(normed, x_low)], axis=1)
    w_bc_part = over_tokens(normed, bc_low)
    w_dt_part = over_tokens(normed, dt_low)
    d_normed = over_columns(z_low, w_zx[:, 0, :]) + over_columns(x_low, w_zx[:, 1, :])
    d_normed = d_normed + over_columns(bc_low, w_bc) + over_columns(dt_low, w_dt)
    norm_gain_part = jnp.sum(d_normed * x_float * inv_rms[:, None], axis=0)
    d_rows = lax.psum_scatter(
        d_normed.astype(jnp.bfloat16), "tensor", scatter_dimension=0, tiled=True
    ).astype(jnp.float32)
    rms_rows = lax.dynamic_slice_in_dim(inv_rms, first_row, share, 0)
    cot_rows = lax.dynamic_slice_in_dim(cotangent, first_row, share, 0).astype(jnp.float32)
    gained = d_rows * norm_gain
    spread = rms_rows * rms_rows * rms_rows * jnp.sum(gained * x_rows, axis=-1) / features
    d_input = cot_rows + rms_rows[:, None] * gained - x_rows * spread[:, None]
    input_grad = lax.all_gather(d_input.astype(jnp.bfloat16), "tensor", axis=0, tiled=True)
    w_zx_grad, w_dt_grad, w_out_grad = (
        lax.psum_scatter(
            w_zx_part.astype(jnp.bfloat16), "dp", scatter_dimension=0, tiled=True
        ).astype(jnp.float32),
        lax.psum_scatter(
            w_dt_part.astype(jnp.bfloat16), "dp", scatter_dimension=0, tiled=True
        ).astype(jnp.float32),
        lax.psum_scatter(
            w_out_part.astype(jnp.bfloat16), "dp", scatter_dimension=1, tiled=True
        ).astype(jnp.float32),
    )
    conv_x_grad, dt_bias_grad, a_log_grad, d_skip_grad, gate_gain_grad = lax.psum(
        (conv_x_part, dt_bias_part, a_log_part, d_skip_part, gate_gain_part), "dp"
    )
    norm_gain_grad, w_bc_grad, conv_bc_grad = lax.psum(
        (norm_gain_part, w_bc_part, conv_bc_part), ("dp", "tensor")
    )
    return (
        mixed,
        input_grad,
        norm_gain_grad,
        w_zx_grad,
        w_bc_grad,
        w_dt_grad,
        conv_x_grad,
        conv_bc_grad,
        dt_bias_grad,
        a_log_grad,
        d_skip_grad,
        gate_gain_grad,
        w_out_grad,
    )


def solution(mesh):
    return jax.shard_map(
        local,
        mesh=mesh,
        in_specs=(
            P("dp", None),
            P(),
            P(None, None, "tensor"),
            P(),
            P(None, "tensor"),
            P(None, "tensor"),
            P(),
            P("tensor"),
            P("tensor"),
            P("tensor"),
            P("tensor"),
            P("tensor", None),
            P("dp", None),
            P("dp"),
        ),
        out_specs=(
            P("dp", None),
            P("dp", None),
            P(),
            P("dp", None, "tensor"),
            P(),
            P("dp", "tensor"),
            P(None, "tensor"),
            P(),
            P("tensor"),
            P("tensor"),
            P("tensor"),
            P("tensor"),
            P("tensor", "dp"),
        ),
        check_vma=False,
    )
```

profile of v0, /device:TPU:1, one launch (start us, length us, event | category | flops | bytes accessed | tf_op | source)
XLA Modules:
  0.0 1176.0 jit_solution(15319442505596880165)
XLA Ops:
  12.6 32.8 %fusion.165 = (bf16[2048,1,2048]{2,1,0:T(2,128)(2,1)}, bf16[2048,1,2048]{2,1,0:T(2,128)(2,1)}) fusion(bf16[2048,2,2048]{2,1,0:T(2,128)(2,1)} %param.20), kind=kLoop, calls=%fused_computation.254 | loop fusion | bytes 33554432 | tf_op jit(solution)/shard_map/slice | solution.py:121
  64.3 16.3 %multiply_convert_fusion.1 = (bf16[8,128,2048]{2,1,0:T(8,128)(2,1)}, f32[8,128,2048]{2,1,0:T(8,128)}) fusion(f32[8,128,2048]{2,1,0:T(8,128)} %copy-done.7, f32[2048]{0:T(1024)S(1)} %bitcast.305, f32[8,3,2048]{2,1,0:T(4,128)S(1)} %select_select_fusion, f32[2048]{0:T(1024)S(1)} %bitcast.307, f32[2048]{0:T(1024)S(1)} %bitcast.301, f32[2048]{0:T(1024)S(1)} %bitcast.303, ...), kind=kLoop, calls=%fused_computation.101 | loop fusion | flops 33554432 | bytes 21209088 | tf_op jit(solution)/shard_map/convert_element_type | solution.py:94
  104.8 23.3 %fusion.171 = f32[8,128,32]{2,0,1:T(8,128)S(1)} fusion(f32[8,128,32]{2,0,1:T(8,128)S(1)} %copy.143), kind=kOutput, calls=%fused_computation.260 | output fusion | flops 4161536 | bytes 262144 | tf_op jit(solution)/shard_map/jvp(jit(cumsum))/reduce_window_sum | solution.py:53
  211.2 21.9 %fusion.39 = f32[8,128,32,64]{1,3,2,0:T(8,128)} fusion(f32[8,128,32,64]{1,3,2,0:T(8,128)} %copy.158, f32[8,128,32,64]{1,3,2,0:T(8,128)S(1)} %fusion.69, f32[32]{0:T(128)S(1)} %copy-done.90, f32[8,128,32]{1,2,0:T(8,128)S(1)} %copy.148, f32[8,128,32]{1,2,0:T(8,128)S(1)} %bitcast.298, f32[8,128,32]{1,2,0:T(8,128)S(1)} %copy-done.36, ...), kind=kOutput, calls=%fused_computation.62 | convolution fusion | flops 3250585600 | bytes 30294144 | tf_op jit(solution)/shard_map/jvp(bijh,bjhp->bihp)/dot_general | solution.py:60
  233.2 16.2 %copy.215 = f32[8,128,32,64]{3,2,1,0:T(8,128)} copy(f32[8,128,32,64]{1,3,2,0:T(8,128)} %fusion.39) | data formatting | bytes 16777216 | tf_op jit(solution)/shard_map/jvp()/reshape | solution.py:70
  264.2 19.5 %multiply_reduce_fusion.11 = (f32[1024]{0:T(1024)S(1)}, f32[1024,2048]{1,0:T(8,128)}, f32[1024,2048]{1,0:T(8,128)}) fusion(f32[1024,2048]{1,0:T(8,128)} %reshape.284, bf16[1024,2048]{1,0:T(8,128)(2,1)} %copy-done.2, bf16[2048,1,2048]{2,1,0:T(2,128)(2,1)} %get-tuple-element.379), kind=kOutput, calls=%fused_computation.85 | convolution fusion | flops 8604613632 | bytes 37752832 | tf_op jit(solution)/shard_map/dot_general | solution.py:121
  303.5 17.2 %multiply_reduce_fusion.2 = (f32[2048]{0:T(1024)}, f32[1024]{0:T(1024)S(1)}, f32[1024,2048]{1,0:T(8,128)}) fusion(f32[1024,2048]{1,0:T(8,128)} %get-tuple-element.373, f32[1024]{0:T(1024)S(1)} %add_rsqrt_fusion, f32[2048]{0:T(1024)S(1)} %copy-done.73, bf16[1024,2048]{1,0:T(8,128)(2,1)} %param.30, bf16[2048,2048]{1,0:T(8,128)(2,1)} %param.29), kind=kOutput, calls=%fused_computation.70 | convolution fusion | flops 8602514432 | bytes 29384704 | tf_op jit(solution)/shard_map/dot_general | solution.py:88
  325.0 20.7 %multiply_reduce_fusion.3 = (f32[2048]{0:T(1024)}, f32[1024,2048]{1,0:T(8,128)}, bf16[1024,2048]{1,0:T(8,128)(2,1)}) fusion(bf16[1024,2048]{1,0:T(8,128)(2,1)} %bitcast.262, f32[1024,2048]{1,0:T(8,128)} %get-tuple-element.413, f32[1024,2048]{1,0:T(8,128)} %get-tuple-element.373, f32[1024]{0:T(1024)S(1)} %fusion.141, f32[1024,2048]{1,0:T(8,128)} %get-tuple-element.414, ...), kind=kLoop, calls=%fused_computation.71 | loop fusion | flops 41940992 | bytes 50356224 | tf_op jit(solution)/shard_map/transpose(jvp())/reduce_sum | solution.py:69
  389.1 21.6 %fusion.106 = f32[32,8,8]{2,1,0:T(8,128)S(1)} fusion(f32[32,64,128,8]{2,3,1,0:T(8,128)S(1)} %fusion.44, f32[8,32,64,128]{3,2,1,0:T(8,128)S(1)} %bitcast.259), kind=kOutput, calls=%fused_computation.159 | convolution fusion | flops 201326592 | bytes 16785408 | tf_op jit(solution)/shard_map/transpose(jvp(hba,ahpn->bhpn))/dot_general | solution.py:64
  427.9 18.0 %fusion.103 = f32[8,128,128]{2,1,0:T(8,128)S(1)} fusion(f32[8,32,64,128]{3,0,2,1:T(8,128)} %convolution_bitcast_fusion.1, f32[8,128,32]{1,2,0:T(8,128)S(1)} %copy-done.29, bf16[8,128,32,64]{1,0,3,2:T(8,128)(2,1)S(1)} %bitcast.266), kind=kOutput, calls=%fused_computation.156 | convolution fusion | flops 3225419776 | bytes 13238272 | tf_op jit(solution)/shard_map/transpose(jvp(bjh,bjhp,bjn->bhpn))/dot_general | solution.py:62
  445.9 16.0 %fusion.98 = f32[8,128,128]{2,1,0:T(8,128)S(1)} fusion(f32[8,32,64,128]{3,0,2,1:T(8,128)S(1)} %bitcast.257, f32[8,128,32,64]{1,0,3,2:T(8,128)S(1)} %bitcast.252, f32[8,128,32]{1,2,0:T(8,128)S(1)} %copy.148), kind=kOutput, calls=%fused_computation.155 | convolution fusion | flops 3223322624 | bytes 17432576 | tf_op jit(solution)/shard_map/transpose(jvp(bin,bhpn->bihp))/dot_general | solution.py:66
  462.0 28.9 %fusion.28 = (f32[8,128,32]{1,2,0:T(8,128)}, f32[8,128,32]{1,2,0:T(8,128)S(1)}, f32[8,128,32]{1,2,0:T(8,128)}, f32[8,128,128]{2,1,0:T(8,128)S(1)}) fusion(f32[8,128,32]{1,2,0:T(8,128)S(1)} %bitcast.299, f32[8,128,32]{1,2,0:T(8,128)S(1)} %copy-done.37, f32[8,128,128]{2,1,0:T(8,128)S(1)} %copy-done.31, pred[128,128]{1,0:T(8,128)(4,1)S(1)} %copy-done.64, ...), kind=kOutput, calls=%fused_computation.44 | convolution fusion | flops 3283910656 | bytes 14303232 | tf_op jit(solution)/shard_map/transpose(jvp(bijh,bjhp->bihp))/dot_general | solution.py:60
  506.7 23.6 %bitcast_add_fusion = f32[8,128,32,64]{1,3,2,0:T(8,128)} fusion(f32[8,128,32,64]{1,3,2,0:T(8,128)} %fusion.65, f32[8,128,32,64]{1,0,3,2:T(8,128)S(1)} %bitcast.255, f32[32]{0:T(128)S(1)} %copy-done.91, f32[8,128,32]{1,2,0:T(8,128)S(1)} %copy-done.29, f32[8,128,32]{1,2,0:T(8,128)S(1)} %bitcast.300, f32[8,128,32]{1,2,0:T(8,128)S(1)} %copy-done.37, ...), kind=kOutput, calls=%fused_computation.58 | convolution fusion | flops 3250585600 | bytes 34488448 | tf_op jit(solution)/shard_map/transpose(jvp(bijh,bjhp->bihp))/dot_general | solution.py:60
  534.7 36.3 %while.31 = (s32[]{:T(128)}, f32[8,32]{1,0:T(8,128)}, f32[32,8,8]{2,1,0:T(8,128)S(1)}, f32[8,32,8,8]{3,2,1,0:T(8,128)}, s32[8]{0:T(128)}, /*index=5*/f32[8,32]{0...) while((s32[]{:T(128)}, f32[8,32]{1,0:T(8,128)}, f32[32,8,8]{2,1,0:T(8,128)S(1)}, ...), condition=%wide.region_15.16_spmd.clone, body=%wide.region_14.15_spmd.clone.sunk | while | flops 420484 | bytes 210855 | solution.py:39
  588.8 18.6 %multiply_reduce_fusion.6 = (f32[2048]{0:T(1024)}, f32[2048]{0:T(1024)}, f32[2048]{0:T(1024)}, f32[2048]{0:T(1024)}, f32[2048]{0:T(1024)}, /*index=5*/f32[8,128,2048]{2,1,0:T(8,128)S(1)}) fusion(f32[8,128,2048]{2,1,0:T(8,128)} %copy-done.7, f32[8,3,2048]{2,1,0:T(4,128)S(1)} %copy-done.19, f32[8,128,2048]{2,1,0:T(8,128)} %get-tuple-element.377, ...), kind=kLoop, calls=%fused_computation.74 | loop fusion | flops 44029952 | bytes 33792000 | tf_op jit(solution)/shard_map/transpose(jvp())/reduce_sum | solution.py:22
  648.6 15.7 %fusion.87 = f32[1024,2048]{1,0:T(8,128)} fusion(bf16[1024,2048]{1,0:T(8,128)(2,1)S(1)} %copy-done.15, bf16[2048,1,2048]{2,1,0:T(2,128)(2,1)} %get-tuple-element.379), kind=kOutput, calls=%fused_computation.142 | convolution fusion | flops 8589934592 | bytes 20971520 | tf_op jit(solution)/shard_map/dot_general | solution.py:88
  664.3 24.1 %multiply_reduce_fusion.8 = (f32[2048]{0:T(1024)S(1)}, bf16[1024,2048]{1,0:T(8,128)(2,1)}, bf16[1024,2048]{1,0:T(8,128)(2,1)}) fusion(bf16[1024,2048]{1,0:T(8,128)(2,1)} %param.18, f32[1024]{0:T(1024)S(1)} %copy-done.59, bf16[1024,2048]{1,0:T(8,128)(2,1)} %all-reduce.29.cloned.1.call-done, f32[1024,2048]{1,0:T(8,128)} %fusion.138, ...), kind=kOutput, calls=%fused_computation.78 | convolution fusion | flops 8613001216 | bytes 54538240 | tf_op jit(solution)/shard_map/dot_general | solution.py:88
  692.6 15.4 %convolution_convert_fusion = bf16[2048,2048]{1,0:T(8,128)(2,1)} fusion(bf16[1024,2048]{1,0:T(8,128)(2,1)} %param.30, f32[1024,2048]{1,0:T(8,128)} %get-tuple-element.373, f32[2048]{0:T(1024)S(1)} %copy-done.74, f32[1024]{0:T(1024)S(1)} %copy-done.62), kind=kOutput, calls=%fused_computation.125 | convolution fusion | flops 8600420352 | bytes 20983808 | tf_op jit(solution)/shard_map/dot_general | solution.py:82
  727.0 18.6 %reduce-scatter.9.cloned.1.call-done = bf16[512,2048]{1,0:T(8,128)(2,1)} async-done(((bf16[1024,2048]{1,0:T(8,128)(2,1)}), bf16[512,2048]{1,0:T(8,128)(2,1)}) %reduce-scatter.9.cloned.1.call-update) | async-done | bytes 2097168 | tf_op jit(solution)/shard_map/reduce_scatter | solution.py:181
  789.8 59.2 %all-reduce.25 = (f32[5,2048]{1,0:T(8,128)}, f32[32]{0:T(128)}, f32[32]{0:T(128)}, f32[32]{0:T(128)}, f32[2048]{0:T(1024)}) all-reduce(f32[5,2048]{1,0:T(8,128)S(1)} %pad_add_fusion.3, f32[32]{0:T(128)S(1)} %get-tuple-element.364, f32[32]{0:T(128)S(1)} %negate_multiply_fusion, ...), channel_id=1, replica_groups=mesh['dp'=16,'tensor'=2] {'dp'}, use_global_device_ids=true, to_apply=%region_32.33 | all-reduce | flops 12384 | bytes 99072 | tf_op jit(solution)/shard_map/psum | solution.py:201
  850.5 44.1 %all-reduce.24 = (f32[2048]{0:T(1024)}, f32[5,256]{1,0:T(8,128)}) all-reduce(f32[2048]{0:T(1024)S(1)} %get-tuple-element.381, f32[5,256]{1,0:T(8,128)S(1)} %pad_add_fusion.4), channel_id=1, replica_groups=mesh['dp'=16,'tensor'=2] {'dp','tensor'}, use_global_device_ids=true, to_apply=%region_23.24 | all-reduce | flops 3328 | bytes 26624 | tf_op jit(solution)/shard_map/psum | solution.py:204
  894.6 21.8 %reduce-scatter.15.cloned.1.call-done = bf16[128,2048]{1,0:T(8,128)(2,1)} async-done(((bf16[2048,2048]{1,0:T(8,128)(2,1)}), bf16[128,2048]{1,0:T(8,128)(2,1)}) %reduce-scatter.15.cloned.1.call-update) | async-done | bytes 524304
  918.7 56.4 %all-gather.2.cloned.1.call-done = bf16[1024,2048]{1,0:T(8,128)(2,1)} async-done(((bf16[512,2048]{1,0:T(8,128)(2,1)}), bf16[1024,2048]{1,0:T(8,128)(2,1)}) %all-gather.2.cloned.1.call-update) | async-done | bytes 4194320 | tf_op jit(solution)/shard_map/all_gather | solution.py:189
  975.1 183.4 %reduce-scatter.11.cloned.1.call-done = bf16[128,2,2048]{2,0,1:T(8,128)(2,1)} async-done(((bf16[2048,2,2048]{2,0,1:T(8,128)(2,1)}), bf16[128,2,2048]{2,0,1:T(8,128)(2,1)}) %reduce-scatter.11.cloned.1.call-update) | async-done | bytes 1048592 | tf_op jit(solution)/shard_map/reduce_scatter | solution.py:191
  (419 shorter events, 434.0 us)
Async XLA Ops:
  8.0 137.0 %copy-start = (bf16[2048,256]{1,0:T(8,128)(2,1)S(1)}, bf16[2048,256]{1,0:T(8,128)(2,1)}, u32[]{:S(2)}) copy-start(bf16[2048,256]{1,0:T(8,128)(2,1)} %param.21) | copy-start | bytes 3145732
  8.0 656.3 %all-reduce.29.cloned.1.call-start = ((), (), s32[]{:S(2)}) async-start(), calls=%async_computation.4 | async-start | bytes 8388608 | tf_op jit(solution)/shard_map/psum | solution.py:155
  8.8 51.4 %copy-start.79 = (s32[8]{0:T(128)}, s32[8]{0:T(128)S(1)}, u32[]{:S(2)}) copy-start(s32[8]{0:T(128)S(1)} %broadcast_maximum_fusion) | copy-start | bytes 100
  9.5 139.6 %copy-start.76 = (pred[8]{0:T(512)(128)(4,1)}, pred[8]{0:T(512)(128)(4,1)S(1)}, u32[]{:S(2)}) copy-start(pred[8]{0:T(512)(128)(4,1)S(1)} %get-tuple-element.411) | copy-start | bytes 28
  12.6 32.9 %copy-start.58 = (f32[1024]{0:T(1024)}, f32[1024]{0:T(1024)S(1)}, u32[]{:S(2)}) copy-start(f32[1024]{0:T(1024)S(1)} %add_rsqrt_fusion.1) | copy-start | bytes 12292
  12.6 32.8 %copy-start.60 = (f32[5,2048]{1,0:T(8,128)S(1)}, f32[5,2048]{1,0:T(8,128)}, u32[]{:S(2)}) copy-start(f32[5,2048]{1,0:T(8,128)} %param.23) | copy-start | bytes 122884
  12.6 32.9 %copy-start.6 = (bf16[1024,2048]{1,0:T(8,128)(2,1)S(1)}, bf16[1024,2048]{1,0:T(8,128)(2,1)}, u32[]{:S(2)}) copy-start(bf16[1024,2048]{1,0:T(8,128)(2,1)} %param.18) | copy-start | bytes 12582916
  12.6 32.9 %copy-start.48 = (f32[2048]{0:T(1024)S(1)}, f32[2048]{0:T(1024)}, u32[]{:S(2)}) copy-start(f32[2048]{0:T(1024)} %param.19) | copy-start | bytes 24580
  93.9 35.0 %copy-start.51 = (s32[8]{0:T(128)S(1)}, s32[8]{0:T(128)}, u32[]{:S(2)}) copy-start(s32[8]{0:T(128)} %param.31) | copy-start | bytes 100
  128.8 32.6 %copy-start.34 = (f32[8,8]{0,1:T(8,128)}, f32[8,8]{0,1:T(8,128)S(1)}, u32[]{:S(2)}) copy-start(f32[8,8]{0,1:T(8,128)S(1)} %fusion.143) | copy-start | bytes 772
  288.1 36.8 %copy-start.61 = (f32[1024]{0:T(1024)}, f32[1024]{0:T(1024)S(1)}, u32[]{:S(2)}) copy-start(f32[1024]{0:T(1024)S(1)} %add_rsqrt_fusion) | copy-start | bytes 12292
  303.4 442.2 %reduce-scatter.9.cloned.1.call-start = ((), (), s32[]{:S(2)}) async-start(), calls=%async_computation.5 | async-start | bytes 6291456 | tf_op jit(solution)/shard_map/reduce_scatter | solution.py:181
  530.3 40.7 %copy-start.10 = (f32[8,128,32]{2,0,1:T(8,128)S(1)}, f32[8,128,32]{2,0,1:T(8,128)}, u32[]{:S(2)}) copy-start(f32[8,128,32]{2,0,1:T(8,128)} %copy-done.9) | copy-start | bytes 393220
  530.3 43.3 %copy-start.13 = (f32[8,128,32]{2,0,1:T(8,128)S(1)}, f32[8,128,32]{2,0,1:T(8,128)}, u32[]{:S(2)}) copy-start(f32[8,128,32]{2,0,1:T(8,128)} %copy.149) | copy-start | bytes 393220
  688.4 160.6 %reduce-scatter.13.cloned.1.call-start = ((), (), s32[]{:S(2)}) async-start(), calls=%async_computation.9 | async-start | bytes 557056
  692.5 223.8 %reduce-scatter.15.cloned.1.call-start = ((), (), s32[]{:S(2)}) async-start(), calls=%async_computation.10 | async-start | bytes 8912896
  720.5 254.6 %all-gather.2.cloned.1.call-start = ((), (), s32[]{:S(2)}) async-start(), calls=%async_computation.6 | async-start | bytes 6291456 | tf_op jit(solution)/shard_map/all_gather | solution.py:189
  755.0 403.5 %reduce-scatter.11.cloned.1.call-start = ((), (), s32[]{:S(2)}) async-start(), calls=%async_computation.7 | async-start | bytes 17825792 | tf_op jit(solution)/shard_map/reduce_scatter | solution.py:191
  784.5 64.5 %copy-start.81 = (f32[256]{0:T(256)S(1)}, f32[256]{0:T(256)}, u32[]{:S(2)}) copy-start(f32[256]{0:T(256)} %get-tuple-element.326) | copy-start | bytes 3076
  784.5 64.4 %copy-start.82 = (f32[256]{0:T(256)S(1)}, f32[256]{0:T(256)}, u32[]{:S(2)}) copy-start(f32[256]{0:T(256)} %get-tuple-element.327) | copy-start | bytes 3076
  784.5 64.4 %copy-start.83 = (f32[256]{0:T(256)S(1)}, f32[256]{0:T(256)}, u32[]{:S(2)}) copy-start(f32[256]{0:T(256)} %get-tuple-element.328) | copy-start | bytes 3076
  784.5 64.4 %copy-start.84 = (f32[256]{0:T(256)S(1)}, f32[256]{0:T(256)}, u32[]{:S(2)}) copy-start(f32[256]{0:T(256)} %get-tuple-element.329) | copy-start | bytes 3076
  784.6 64.4 %copy-start.85 = (f32[256]{0:T(256)S(1)}, f32[256]{0:T(256)}, u32[]{:S(2)}) copy-start(f32[256]{0:T(256)} %get-tuple-element.330) | copy-start | bytes 3076
  784.6 377.6 %all-reduce.31.cloned.1.call-start = ((), (), s32[]{:S(2)}) async-start(), calls=%async_computation.8 | async-start | bytes 4194304 | tf_op jit(solution)/shard_map/psum | solution.py:204
  (81 other events, 997.4 us)
Sparse Core Ops, SparseCore 0:
  303.5 110.5 all-reduce.28
  688.5 57.0 reduce-scatter.8
  749.8 54.8 reduce-scatter.12
  809.1 107.1 reduce-scatter.14
  918.4 56.6 all-gather.1
  979.6 178.8 reduce-scatter.10
Sparse Core Ops, SparseCore 1:
  791.8 204.3 all-reduce.30
where the time goes:
time: 1190 us; the launch traced here: 1180 us
  matrix products  397 us (33%)
  waiting for transfers between devices  280 us (24%)
  other arithmetic  188 us (16%)
  local copies, waits for them, and re-layouts  181 us (15%)
  blocking collectives  112 us (9%)
  between operations  17.3 us (1%)
    reduce_scatter x1, waiting for transfers between devices, local(): lax.psum_scatter(w_zx_part.astype(jnp.bfloat16), 'dp', scatter_dimension=...  183 us
    dot_general x3, matrix products, ssd_mix(): within = jnp.einsum('bijh,bjhp->bihp', weights, x_blocks, precision=highest)  74.5 us
    dot_general x5, matrix products, over_columns(): lax.dot_general(left, right, (((1,), (1,)), ((), ())), preferred_element_...  66 us
    psum x1, blocking collectives, local(): lax.psum((conv_x_part, dt_bias_part, a_log_part, d_skip_part, gate_gain_p...  59.2 us
    all_gather x1, waiting for transfers between devices, local(): lax.all_gather(d_input.astype(jnp.bfloat16), 'tensor', axis=0, tiled=True)  56.4 us
    dot_general x5, matrix products, over_tokens(): lax.dot_general(left, right, (((0,), (0,)), ((), ())), preferred_element_...  45.7 us
    dot_general x3, matrix products, ssd_mix(): jnp.einsum('hba,ahpn->bhpn', paths, local_states, precision=highest)  44.6 us
    unnamed x209, local copies, waits for them, and re-layouts  44.2 us
  transfers between devices with their start and end apart: 7, of which 4 were waited for; matrix products, arithmetic and copies ran while one was open for 38% of the time, Pallas kernels for 0%

commit v1 on v0

v1 whole, which is shorter than its diff:
```python
import functools

import jax
import jax.numpy as jnp
from jax import lax
from jax.experimental import pallas as pl
from jax.experimental.pallas import tpu as pltpu
from jax.sharding import PartitionSpec as P

epsilon = 1e-05
f32 = jnp.float32
bf16 = jnp.bfloat16
VMEM_LIMIT = 60 * 1024 * 1024
LIGHT = pl.CostEstimate(flops=1000, bytes_accessed=1000, transcendentals=0)


def sigmoid(v):
    return 0.5 * jnp.tanh(0.5 * v) + 0.5


def dot(a, b, dims=((1,), (0,)), precision=None):
    return lax.dot_general(a, b, (dims, ((), ())), precision=precision, preferred_element_type=f32)


NN = ((1,), (0,))
NT = ((1,), (1,))
TN = ((0,), (0,))
highest = lax.Precision.HIGHEST


def split_low(v):
    hi = v.astype(bf16)
    lo = (v - hi.astype(f32)).astype(bf16)
    return hi, lo


def head_masks(length, head_dim):
    lane = lax.broadcasted_iota(jnp.int32, (length, 2 * head_dim), 1)
    return lane < head_dim


def pair_stack(v, first):
    zero = jnp.zeros_like(v)
    return jnp.concatenate([jnp.where(first, v, zero), jnp.where(first, zero, v)], axis=0)


def tri_mask(length):
    row = lax.broadcasted_iota(jnp.int32, (length, length), 0)
    col = lax.broadcasted_iota(jnp.int32, (length, length), 1)
    return row, col


def step_values(dtr_ref, bias_ref, alog_ref, length):
    row, col = tri_mask(length)
    dtr = dtr_ref[...] + bias_ref[...]
    dt = jnp.maximum(dtr, 0.0) + jnp.log1p(jnp.exp(-jnp.abs(dtr)))
    rate = -jnp.exp(alog_ref[...])
    tri = (row >= col).astype(f32)
    cum = dot(tri, dt * rate, NN, highest)
    last = cum[length - 1 : length, :]
    return dtr, dt, rate, cum, jnp.exp(cum), jnp.exp(jnp.minimum(last - cum, 0.0))


def store_columns(cum, cum_s, cumt_s, heads):
    cum_s[:, :heads] = cum
    cumt_s[...] = jnp.transpose(cum_s[...])


def conv_rows(ext, kern, length, window):
    base = ext.shape[0] - length - (window - 1)
    total = kern[window : window + 1, :] + kern[window - 1 : window, :] * ext[ext.shape[0] - length :, :]
    for offset in range(window - 1):
        total = total + kern[offset : offset + 1, :] * ext[base + offset : base + offset + length, :]
    return total


def forward_kernel(
    sizes,
    par_ref,
    bc_ref,
    dtr_ref,
    z_ref,
    xp_ref,
    kx_ref,
    kbc_ref,
    bias_ref,
    alog_ref,
    skip_ref,
    gain_ref,
    sel_ref,
    y_ref,
    xc_ref,
    pre_ref,
    gg_ref,
    bcc_ref,
    bcp_ref,
    hs_ref,
    sq_ref,
    h_end,
    tail_x,
    tail_bc,
    lhs_s,
    cum_s,
    cumt_s,
    score_s,
    acc_s,
):
    length, inner, heads, head_dim, lanes, blocks, window = sizes
    state = bcc_ref.shape[1] // 2
    b = pl.program_id(0)
    par = par_ref[b]
    slot = jnp.where(par >= 0, par, blocks)

    @pl.when(b == 0)
    def _():
        h_end[blocks] = jnp.zeros(h_end.shape[1:], f32)
        tail_x[blocks] = jnp.zeros(tail_x.shape[1:], f32)
        tail_bc[blocks] = jnp.zeros(tail_bc.shape[1:], f32)
        cum_s[...] = jnp.zeros_like(cum_s)

    bcv = bc_ref[...]
    pre = conv_rows(jnp.concatenate([tail_bc[slot], bcv], axis=0), kbc_ref[...], length, window)
    tail_bc[b] = bcv[length - 8 :, :]
    bcc = (pre * sigmoid(pre)).astype(bf16)
    bcc_ref[...] = bcc
    bcp_ref[...] = pre
    c_rows = bcc[:, state:]
    b_rows = bcc[:, :state]
    row, col = tri_mask(length)
    score_s[...] = jnp.where(row >= col, dot(c_rows, b_rows, NT), 0.0)

    _, dt, _, cum, from_start, to_end = step_values(dtr_ref, bias_ref, alog_ref, length)
    hi, lo = split_low(jnp.concatenate([dt, from_start, to_end], axis=0))
    lhs_s[...] = jnp.concatenate([hi, lo], axis=1)
    store_columns(cum, cum_s, cumt_s, heads)
    acc_s[...] = jnp.zeros_like(acc_s)
    first = head_masks(length, head_dim)
    group = lanes // head_dim
    pair = 2 * head_dim

    def body(g, carry):
        sl = pl.ds(pl.multiple_of(g * lanes, lanes), lanes)
        xpv = xp_ref[:, sl].astype(f32)
        ext = jnp.concatenate([tail_x[slot, :, sl], xpv], axis=0)
        pre_x = conv_rows(ext, kx_ref[:, sl], length, window)
        tail_x[b, :, sl] = xpv[length - 8 :, :]
        xc = (pre_x * sigmoid(pre_x)).astype(bf16)
        pre_ref[:, sl] = pre_x.astype(bf16)
        xc_ref[:, sl] = xc
        wide = dot(lhs_s[...], sel_ref[:, sl])
        dt_l = wide[:length]
        start_l = wide[length : 2 * length]
        end_l = wide[2 * length :]
        xcf = xc.astype(f32)
        xd = dt_l * xcf
        xdb = xd.astype(bf16)
        gx = (end_l * xd).astype(bf16)
        h = h_end[slot, :, sl]
        hb = h.astype(bf16)
        hs_ref[0, :, sl] = hb
        carried = start_l * dot(c_rows, hb)
        h_end[b, :, sl] = start_l[length - 1 : length, :] * h + dot(b_rows, gx, TN)
        cols = pltpu.roll(cum_s[...], cum_s.shape[1] - g * group, 1)
        rows = cumt_s[pl.ds(pl.multiple_of(g * group, 8), max(group, 8)), :]
        score = score_s[...]
        skip = skip_ref[:, sl]
        gain = gain_ref[:, sl]
        zv = z_ref[:, sl].astype(f32)
        gate = zv * sigmoid(zv)
        acc = acc_s[...]
        for q in range(lanes // pair):
            at = slice(q * pair, (q + 1) * pair)
            weights = []
            for h_at in (2 * q, 2 * q + 1):
                gap = jnp.minimum(cols[:, h_at : h_at + 1] - rows[h_at : h_at + 1, :], 0.0)
                weights.append((score * jnp.exp(gap)).astype(bf16))
            within = dot(jnp.concatenate(weights, axis=1), pair_stack(xdb[:, at], first))
            y = (within + carried[:, at] + skip[:, at] * xcf[:, at]).astype(bf16)
            out = pl.ds(pl.multiple_of(g * lanes + q * pair, pair), pair)
            y_ref[:, out] = y
            gated = y.astype(f32) * gate[:, at]
            gained = gated * gain[:, at]
            gg_ref[:, out] = gained.astype(bf16)
            acc = acc + gated * gated
        acc_s[...] = acc
        return carry

    lax.fori_loop(0, inner // lanes, body, 0)
    sq_ref[0] = dot(jnp.ones((8, pair), f32), acc_s[...], NT, highest)


def run_forward(parent, bc_pre, dt_raw, zx, conv_x, conv_bc, dt_bias, a_log, skip_l, gate_gain, sel):
    tokens = zx.shape[0]
    inner = conv_x.shape[1]
    heads = dt_raw.shape[1]
    head_dim = inner // heads
    blocks = parent.shape[0]
    length = tokens // blocks
    window = conv_x.shape[0] - 1
    wide = bc_pre.shape[1]
    state = wide // 2
    lanes = min(512, inner)
    sizes = (length, inner, heads, head_dim, lanes, blocks, window)
    whole = lambda shape: pl.BlockSpec(shape, lambda b, *_: (0,) * len(shape))
    rows = lambda width: pl.BlockSpec((length, width), lambda b, *_: (b, 0))
    block = lambda shape: pl.BlockSpec((1,) + shape, lambda b, *_: (b, 0, 0))
    grid_spec = pltpu.PrefetchScalarGridSpec(
        num_scalar_prefetch=1,
        grid=(blocks,),
        in_specs=[
            rows(wide),
            rows(heads),
            rows(inner),
            pl.BlockSpec((length, inner), lambda b, *_: (b, 1)),
            whole(conv_x.shape),
            whole(conv_bc.shape),
            whole((1, heads)),
            whole((1, heads)),
            whole((1, inner)),
            whole((1, inner)),
            whole(sel.shape),
        ],
        out_specs=[
            rows(inner),
            rows(inner),
            rows(inner),
            rows(inner),
            rows(wide),
            rows(wide),
            block((state, inner)),
            block((8, length)),
        ],
        scratch_shapes=[
            pltpu.VMEM((blocks + 1, state, inner), f32),
            pltpu.VMEM((blocks + 1, 8, inner), f32),
            pltpu.VMEM((blocks + 1, 8, wide), f32),
            pltpu.VMEM((3 * length, 2 * heads), bf16),
            pltpu.VMEM((length, length), f32),
            pltpu.VMEM((length, length), f32),
            pltpu.VMEM((length, length), f32),
            pltpu.VMEM((length, 2 * head_dim), f32),
        ],
    )
    return pl.pallas_call(
        functools.partial(forward_kernel, sizes),
        grid_spec=grid_spec,
        out_shape=[jax.ShapeDtypeStruct((tokens, inner), bf16)] * 4
        + [
            jax.ShapeDtypeStruct((tokens, wide), bf16),
            jax.ShapeDtypeStruct((tokens, wide), f32),
            jax.ShapeDtypeStruct((blocks, state, inner), bf16),
            jax.ShapeDtypeStruct((blocks, 8, length), f32),
        ],
        compiler_params=pltpu.CompilerParams(vmem_limit_bytes=VMEM_LIMIT),
        cost_estimate=LIGHT,
        name="ssd_forward",
    )(parent, bc_pre, dt_raw, zx, zx, conv_x, conv_bc, dt_bias[None], a_log[None], skip_l, gate_gain[None], sel)


def token_column(row_ref, at, length):
    row = row_ref[pl.ds(at, 1), :]
    return jnp.transpose(jnp.broadcast_to(row, (length, length)))


def ungate_kernel(sizes, sq_ref, cross_ref, y_ref, z_ref, dgn_ref, gain_ref, dz_ref, dy_ref, grad_ref):
    length, inner, lanes, full = sizes
    b = pl.program_id(0)
    inv = lax.rsqrt(token_column(sq_ref, b, length) / full + epsilon)
    coef = inv * token_column(cross_ref, b, length) / full

    @pl.when(b == 0)
    def _():
        grad_ref[...] = jnp.zeros_like(grad_ref)

    def body(g, carry):
        sl = pl.ds(pl.multiple_of(g * length, length), length)
        zv = z_ref[:, sl].astype(f32)
        sig = sigmoid(zv)
        gate = zv * sig
        gain = gain_ref[:, sl]
        y = y_ref[:, sl].astype(f32) * inv
        scaled = y * gate
        dgn = dgn_ref[:, sl].astype(f32)
        grad_ref[:, sl] += jnp.sum(dgn * scaled, axis=0, keepdims=True)
        d_scaled = dgn * gain - scaled * coef
        dz_ref[:, sl] = (d_scaled * y * (sig + gate * (1.0 - sig))).astype(bf16)
        dy_ref[:, sl] = (d_scaled * inv * gate).astype(bf16)
        return carry

    lax.fori_loop(0, inner // length, body, 0, unroll=2)


def run_ungate(squares, cross, y, zx, dgn, gate_gain, full):
    tokens, inner = y.shape
    blocks, length = squares.shape
    rows = pl.BlockSpec((length, inner), lambda b: (b, 0))
    one = pl.BlockSpec((1, inner), lambda b: (0, 0))
    small = pl.BlockSpec((blocks, length), lambda b: (0, 0))
    return pl.pallas_call(
        functools.partial(ungate_kernel, (length, inner, length, full)),
        grid=(blocks,),
        in_specs=[small, small, rows, rows, rows, one],
        out_specs=[rows, rows, one],
        out_shape=[jax.ShapeDtypeStruct((tokens, inner), bf16)] * 2 + [jax.ShapeDtypeStruct((1, inner), f32)],
        compiler_params=pltpu.CompilerParams(vmem_limit_bytes=VMEM_LIMIT),
        cost_estimate=LIGHT,
        name="gate_backward",
    )(squares, cross, y, zx, dgn, gate_gain[None])


def output_kernel(left_ref, right_ref, cot_ref, out_ref, cross_ref):
    total = dot(left_ref[...], right_ref[...])
    product = (total * cot_ref[...].astype(f32)).astype(bf16)
    row = dot(jnp.ones((8, product.shape[1]), bf16), product, NT)

    @pl.when(pl.program_id(0) == 0)
    def _():
        cross_ref[...] = jnp.zeros_like(cross_ref)

    cross_ref[...] += row
    out_ref[...] = total.astype(bf16)


def run_output(gained, w_out, cotangent):
    tokens, inner = gained.shape
    features = w_out.shape[1]
    tile = min(512, features)
    return pl.pallas_call(
        output_kernel,
        grid=(features // tile,),
        in_specs=[
            pl.BlockSpec((tokens, inner), lambda j: (0, 0), pipeline_mode=pl.Buffered(1)),
            pl.BlockSpec((inner, tile), lambda j: (0, j)),
            pl.BlockSpec((tokens, tile), lambda j: (0, j)),
        ],
        out_specs=[pl.BlockSpec((tokens, tile), lambda j: (0, j)), pl.BlockSpec((8, tokens), lambda j: (0, 0))],
        out_shape=[
            jax.ShapeDtypeStruct((tokens, features), bf16),
            jax.ShapeDtypeStruct((8, tokens), f32),
        ],
        compiler_params=pltpu.CompilerParams(vmem_limit_bytes=VMEM_LIMIT),
        cost_estimate=LIGHT,
        name="output_project",
    )(gained, w_out, cotangent)


def norm_kernel(features, x_ref, cot_ref, gain_ref, wbc_ref, wdt_ref, normed_ref, turned_ref, inv_ref, bc_ref, dtr_ref):
    x = x_ref[...].astype(f32)
    inv = lax.rsqrt(jnp.sum(x * x, axis=1, keepdims=True) / features + epsilon)
    inv_ref[...] = inv
    normed = (x * inv * gain_ref[...]).astype(bf16)
    normed_ref[...] = normed
    turned_ref[0] = jnp.transpose(normed)
    turned_ref[1] = jnp.transpose(cot_ref[...])
    bc_ref[...] = dot(normed, wbc_ref[...])
    dtr_ref[...] = dot(normed, wdt_ref[...], NT)


def run_norm(x_in, cotangent, norm_gain, w_bc, w_dt_t, length):
    tokens, features = x_in.shape
    wide = w_bc.shape[1]
    heads = w_dt_t.shape[0]
    rows = lambda width: pl.BlockSpec((length, width), lambda b: (b, 0))
    whole = lambda shape: pl.BlockSpec(shape, lambda b: (0, 0), pipeline_mode=pl.Buffered(1))
    turned = pl.BlockSpec((2, features, length), lambda b: (0, 0, b))
    return pl.pallas_call(
        functools.partial(norm_kernel, features),
        grid=(tokens // length,),
        in_specs=[rows(features), rows(features), whole((1, features)), whole(w_bc.shape), whole(w_dt_t.shape)],
        out_specs=[rows(features), turned, rows(1), rows(wide), rows(heads)],
        out_shape=[
            jax.ShapeDtypeStruct((tokens, features), bf16),
            jax.ShapeDtypeStruct((2, features, tokens), bf16),
            jax.ShapeDtypeStruct((tokens, 1), f32),
            jax.ShapeDtypeStruct((tokens, wide), f32),
            jax.ShapeDtypeStruct((tokens, heads), f32),
        ],
        compiler_params=pltpu.CompilerParams(vmem_limit_bytes=VMEM_LIMIT),
        cost_estimate=LIGHT,
        name="input_norm",
    )(x_in, cotangent, norm_gain[None], w_bc, w_dt_t)


def fetch_left(share, which, place_ref, mine_ref, theirs_ref, left_s, sem):
    tokens = mine_ref.shape[2]
    count = left_s.shape[0] // share
    copies = []
    for i in range(count):
        src = pl.ds(pl.multiple_of(place_ref[i] * share, share), share)
        for side, ref in enumerate((mine_ref, theirs_ref)):
            copies.append(
                pltpu.make_async_copy(
                    ref.at[which, src, :],
                    left_s.at[pl.ds(i * share, share), pl.ds(side * tokens, tokens)],
                    sem.at[2 * i + side],
                )
            )
    return copies


def gather_right(refs, right_s):
    at = 0
    for ref in refs:
        size = ref.shape[0]
        right_s[at : at + size, :] = ref[...]
        at += size


def load_left(share, which, place_ref, mine_ref, theirs_ref, left_s, sem):
    copies = fetch_left(share, which, place_ref, mine_ref, theirs_ref, left_s, sem)
    for copy in copies:
        copy.start()
    for copy in copies:
        copy.wait()


def grad_kernel(share, which, pieces, scaled, outs, place_ref, mine_ref, theirs_ref, *rest):
    rights = rest[:pieces]
    rest = rest[pieces:]
    if scaled:
        scale_ref = rest[0]
        rest = rest[1:]
    out_refs = rest[:outs]
    left_s, right_s, sem = rest[outs:]

    @pl.when(pl.program_id(0) == 0)
    def _():
        load_left(share, which, place_ref, mine_ref, theirs_ref, left_s, sem)
        if scaled:
            rows_at = left_s.shape[0] // 8

            def apply(i, carry):
                at = pl.ds(pl.multiple_of(i * rows_at, rows_at), rows_at)
                left_s[at, :] = (left_s[at, :].astype(f32) * scale_ref[...]).astype(bf16)
                return carry

            lax.fori_loop(0, 8, apply, 0)

    gather_right(rights, right_s)
    total = dot(left_s[...], right_s[...])
    size = out_refs[0].shape[0]
    for i, ref in enumerate(out_refs):
        ref[...] = total[i * size : (i + 1) * size].astype(bf16)


def run_grad(places, which, mine, theirs, rights, share, first, width, outs, scale=None):
    tokens = mine.shape[2]
    count = places.shape[0]
    rows = count * share
    tile = 256 if width % 256 == 0 and first % 256 == 0 else 128
    anywhere = pl.BlockSpec(memory_space=pl.ANY)
    columns = [
        pl.BlockSpec((right.shape[0], tile), lambda j, *_: (0, first // tile + j)) for right in rights
    ]
    extra = [] if scale is None else [pl.BlockSpec(scale.shape, lambda j, *_: (0, 0))]
    return pl.pallas_call(
        functools.partial(grad_kernel, share, which, len(rights), scale is not None, outs),
        grid_spec=pltpu.PrefetchScalarGridSpec(
            num_scalar_prefetch=1,
            grid=(width // tile,),
            in_specs=[anywhere, anywhere] + columns + extra,
            out_specs=[pl.BlockSpec((rows // outs, tile), lambda j, *_: (0, j))] * outs,
            scratch_shapes=[
                pltpu.VMEM((rows, 2 * tokens), bf16),
                pltpu.VMEM((2 * tokens, tile), bf16),
                pltpu.SemaphoreType.DMA((2 * count,)),
            ],
        ),
        out_shape=[jax.ShapeDtypeStruct((rows // outs, width), bf16)] * outs,
        compiler_params=pltpu.CompilerParams(vmem_limit_bytes=VMEM_LIMIT),
        cost_estimate=LIGHT,
        name="weight_grad",
    )(places, mine, theirs, *rights, *([] if scale is None else [scale]))


def input_kernel(heads, dz_ref, dx_ref, dbc_ref, ddt_ref, wz_ref, wx_ref, wbc_ref, wdt_ref, x_ref, inv_ref, out_ref, gain_ref):
    total = dot(dz_ref[...], wz_ref[...], NT) + dot(dx_ref[...], wx_ref[...], NT)
    total = total + dot(dbc_ref[...], wbc_ref[...], NT)
    total = total + dot(ddt_ref[:, :heads], wdt_ref[...], NN)
    out_ref[...] = total.astype(bf16)
    gain_ref[...] = jnp.sum(total * (x_ref[...].astype(f32) * inv_ref[...]), axis=0, keepdims=True)


def run_input(dz, dx, dbc, ddt, w_cat, w_bc, w_dt_t, x_in, inv_rms, at, tokens):
    inner = dz.shape[1]
    features = x_in.shape[1]
    wide = w_bc.shape[1]
    heads = w_dt_t.shape[0]
    tile = 256
    side = lambda width: pl.BlockSpec((tokens, width), lambda j: (at, 0), pipeline_mode=pl.Buffered(1))
    return pl.pallas_call(
        functools.partial(input_kernel, heads),
        grid=(features // tile,),
        in_specs=[
            side(inner),
            side(inner),
            side(wide),
            side(ddt.shape[1]),
            pl.BlockSpec((tile, inner), lambda j: (j, 0)),
            pl.BlockSpec((tile, inner), lambda j: (j, 1)),
            pl.BlockSpec((tile, wide), lambda j: (j, 0)),
            pl.BlockSpec((heads, tile), lambda j: (0, j)),
            pl.BlockSpec((tokens, tile), lambda j: (at, j)),
            pl.BlockSpec((tokens, 1), lambda j: (at, 0)),
        ],
        out_specs=[pl.BlockSpec((tokens, tile), lambda j: (0, j)), pl.BlockSpec((1, tile), lambda j: (0, j))],
        out_shape=[jax.ShapeDtypeStruct((tokens, features), bf16), jax.ShapeDtypeStruct((1, features), f32)],
        compiler_params=pltpu.CompilerParams(vmem_limit_bytes=VMEM_LIMIT),
        cost_estimate=LIGHT,
        name="input_grad",
    )(dz, dx, dbc, ddt, w_cat, w_cat, w_bc, w_dt_t, x_in, inv_rms)


def conv_back(ext, kern, inputs, length, window):
    total = kern[window - 1 : window, :] * ext[:length, :]
    sums = [None] * (window + 1)
    sums[window] = jnp.sum(ext[:length, :], axis=0, keepdims=True)
    sums[window - 1] = jnp.sum(inputs * ext[:length, :], axis=0, keepdims=True)
    for shift in range(1, window):
        moved = ext[shift : shift + length, :]
        total = total + kern[window - 1 - shift : window - shift, :] * moved
        sums[window - 1 - shift] = jnp.sum(inputs * moved, axis=0, keepdims=True)
    return total, jnp.concatenate(sums, axis=0)


def backward_kernel(
    sizes,
    par_ref,
    dy_ref,
    xc_ref,
    pre_ref,
    xp_ref,
    hs_ref,
    bcc_ref,
    bcp_ref,
    bc_ref,
    dtr_ref,
    kx_ref,
    kbc_ref,
    bias_ref,
    alog_ref,
    skip_ref,
    sel_ref,
    selt_ref,
    *rest,
):
    length, inner, heads, head_dim, lanes, blocks, window, start, count = sizes
    last_chunk = start + count == blocks
    if not last_chunk:
        ds_prev, nx_prev, nbc_prev = rest[:3]
        rest = rest[3:]
    dxp_ref, dbc_ref, ddt_ref, gkx_ref, gkbc_ref, gskip_ref, ghead_ref = rest[:7]
    rest = rest[7:]
    if start:
        ds_next, nx_next, nbc_next = rest[:3]
        rest = rest[3:]
    (
        d_state,
        next_x,
        next_bc,
        lhs_s,
        cum_s,
        cumt_s,
        score_s,
        dscore_s,
        db_s,
        dc_s,
        red_s,
        cross_s,
        inner_s,
    ) = rest
    state = bcc_ref.shape[1] // 2
    b = start + count - 1 - pl.program_id(0)
    par = par_ref[b]
    slot = jnp.where(par >= 0, par, blocks)

    @pl.when(pl.program_id(0) == 0)
    def _():
        if last_chunk:
            d_state[...] = jnp.zeros_like(d_state)
            next_x[...] = jnp.zeros_like(next_x)
            next_bc[...] = jnp.zeros_like(next_bc)
        else:
            pltpu.sync_copy(ds_prev, d_state.at[: start + count])
            next_x[: start + count] = nx_prev[...]
            next_bc[: start + count] = nbc_prev[...]
            d_state[blocks] = jnp.zeros(d_state.shape[1:], f32)
            next_x[blocks] = jnp.zeros(next_x.shape[1:], f32)
            next_bc[blocks] = jnp.zeros(next_bc.shape[1:], f32)
        cum_s[...] = jnp.zeros_like(cum_s)
        cross_s[...] = jnp.zeros_like(cross_s)
        gkx_ref[...] = jnp.zeros_like(gkx_ref)
        gkbc_ref[...] = jnp.zeros_like(gkbc_ref)
        gskip_ref[...] = jnp.zeros_like(gskip_ref)
        ghead_ref[...] = jnp.zeros_like(ghead_ref)

    bcc = bcc_ref[...]
    c_rows = bcc[:, state:]
    b_rows = bcc[:, :state]
    row, col = tri_mask(length)
    score_s[...] = jnp.where(row >= col, dot(c_rows, b_rows, NT), 0.0)
    dtr, dt, rate, cum, from_start, to_end = step_values(dtr_ref, bias_ref, alog_ref, length)
    hi, lo = split_low(jnp.concatenate([dt, from_start, to_end], axis=0))
    lhs_s[...] = jnp.concatenate([hi, lo], axis=1)
    store_columns(cum, cum_s, cumt_s, heads)
    dscore_s[...] = jnp.zeros_like(dscore_s)
    db_s[...] = jnp.zeros_like(db_s)
    dc_s[...] = jnp.zeros_like(dc_s)
    red_s[...] = jnp.zeros_like(red_s)
    first = head_masks(length, head_dim)
    group = lanes // head_dim
    pair = 2 * head_dim
    before = (row < col).astype(bf16)
    following = (row >= col).astype(f32)

    def body(g, carry):
        sl = pl.ds(pl.multiple_of(g * lanes, lanes), lanes)
        wide = dot(lhs_s[...], sel_ref[:, sl])
        dt_l = wide[:length]
        start_l = wide[length : 2 * length]
        end_l = wide[2 * length :]
        last_l = start_l[length - 1 : length, :]
        dyb = dy_ref[:, sl]
        dy = dyb.astype(f32)
        xc = xc_ref[:, sl]
        xcf = xc.astype(f32)
        xd = dt_l * xcf
        xdb = xd.astype(bf16)
        gx = (end_l * xd).astype(bf16)
        hb = hs_ref[0, :, sl]
        d_end = d_state[b, :, sl]
        d_endb = d_end.astype(bf16)
        sdy = (start_l * dy).astype(bf16)
        carried = start_l * dot(c_rows, hb)
        local = end_l * dot(b_rows, d_endb)
        dc_s[...] += dot(sdy, hb, NT)
        db_s[...] += dot(gx, d_endb, NT)
        d_state[slot, :, sl] += last_l * d_end + dot(c_rows, sdy, TN)
        carry_end = jnp.sum(d_end * hb.astype(f32), axis=0, keepdims=True) * last_l
        cols = pltpu.roll(cum_s[...], cum_s.shape[1] - g * group, 1)
        rows = cumt_s[pl.ds(pl.multiple_of(g * group, 8), max(group, 8)), :]
        score = score_s[...]
        dscore = dscore_s[...]
        crossings = []
        for q in range(lanes // pair):
            at = slice(q * pair, (q + 1) * pair)
            dy2 = pair_stack(dyb[:, at], first)
            dw2 = dot(dy2, xdb[:, at], NT)
            weights, terms = [], []
            for half in range(2):
                h_at = 2 * q + half
                gap = jnp.minimum(cols[:, h_at : h_at + 1] - rows[h_at : h_at + 1, :], 0.0)
                decay = jnp.exp(gap)
                weights.append((score * decay).astype(bf16))
                t = dw2[half * length : (half + 1) * length] * decay
                dscore = dscore + t
                terms.append((t * score).astype(bf16))
            inner_s[:, at] = dot(jnp.concatenate(weights, axis=0), dy2, TN)
            crossed = dot(jnp.concatenate(terms, axis=0), before)
            for half in range(2):
                part = crossed[half * length : (half + 1) * length] * following
                crossings.append(jnp.sum(part, axis=0, keepdims=True))
        dscore_s[...] = dscore
        cross_s[pl.ds(pl.multiple_of(g * group, 8), group), :] = jnp.concatenate(crossings, axis=0)
        dxd = inner_s[...] + local
        products = jnp.concatenate(
            [(dy * carried).astype(bf16), (local * xd).astype(bf16), (dxd * xcf).astype(bf16),
             jnp.broadcast_to(carry_end, (16, lanes)).astype(bf16)], axis=0
        )
        red_s[...] += dot(products, selt_ref[sl, :])
        gskip_ref[:, sl] += jnp.sum(dy * xcf, axis=0, keepdims=True)
        dx = dt_l * dxd + skip_ref[:, sl] * dy
        pre = pre_ref[:, sl].astype(f32)
        sig = sigmoid(pre)
        d_pre = dx * (sig + pre * sig * (1.0 - sig))
        ext = jnp.concatenate([d_pre, next_x[b, :, sl]], axis=0)
        next_x[slot, :, sl] += d_pre[:8, :]
        xpv = xp_ref[:, sl].astype(f32)
        dxp, sums = conv_back(ext, kx_ref[:, sl], xpv, length, window)
        dxp_ref[:, sl] = dxp.astype(bf16)
        gkx_ref[:, sl] += sums
        return carry

    lax.fori_loop(0, inner // lanes, body, 0)

    red = red_s[...]
    carried_t = red[:length, :heads]
    local_t = red[length : 2 * length, :heads]
    ddt = red[2 * length : 3 * length, :heads]
    end_t = red[3 * length : 3 * length + 1, :heads]
    suffix = (row <= col).astype(f32)
    prefix = (row > col).astype(f32)
    d_rate = (
        dot(suffix, carried_t, NN, highest)
        + dot(prefix, local_t, NN, highest)
        + end_t
        + jnp.transpose(cross_s[...])[:, :heads]
    )
    ddt = ddt + d_rate * rate
    ddtr = ddt * sigmoid(dtr)
    ghead_ref[0:1, :] += jnp.sum(ddtr, axis=0, keepdims=True)
    ghead_ref[1:2, :] += jnp.sum(d_rate * rate * dt, axis=0, keepdims=True)

    dscore = jnp.where(row >= col, dscore_s[...], 0.0).astype(bf16)
    d_c = dc_s[...] + dot(dscore, b_rows)
    d_b = db_s[...] + dot(dscore, c_rows, TN)
    pre = bcp_ref[...]
    sig = sigmoid(pre)
    d_pre = jnp.concatenate([d_b, d_c], axis=1) * (sig + pre * sig * (1.0 - sig))
    ext = jnp.concatenate([d_pre, next_bc[b]], axis=0)
    next_bc[slot] += d_pre[:8, :]
    dbcp, sums = conv_back(ext, kbc_ref[...], bc_ref[...], length, window)
    gkbc_ref[...] += sums
    dbc_ref[...] = dbcp.astype(bf16)
    ddt_ref[...] = jnp.zeros_like(ddt_ref)
    ddt_ref[:, :heads] = ddtr.astype(bf16)

    if start:

        @pl.when(b == start)
        def _():
            pltpu.sync_copy(d_state.at[:start], ds_next)
            nx_next[...] = next_x[:start]
            nbc_next[...] = next_bc[:start]


def run_backward(
    start, count, parent, dy, xc, pre, zx, hs, bcc, bcp, bc_pre, dt_raw, conv_x, conv_bc, dt_bias, a_log, skip_l,
    sel, sel_t, small, carry
):
    inner = conv_x.shape[1]
    heads = dt_raw.shape[1]
    head_dim = inner // heads
    blocks = parent.shape[0]
    length = dy.shape[0] // blocks
    tokens = count * length
    window = conv_x.shape[0] - 1
    wide = bcc.shape[1]
    state = wide // 2
    lanes = min(512, inner)
    anywhere = pl.BlockSpec(memory_space=pl.ANY)
    sizes = (length, inner, heads, head_dim, lanes, blocks, window, start, count)
    top = count - 1
    later = lambda width: pl.BlockSpec((length, width), lambda b, *_: (start + top - b, 0))
    whole = lambda shape: pl.BlockSpec(shape, lambda b, *_: (0,) * len(shape))
    rows = lambda width: pl.BlockSpec((length, width), lambda b, *_: (top - b, 0))
    carry_specs = [anywhere, whole(carry[1].shape), whole(carry[2].shape)] if carry else []
    next_specs, next_shapes = [], []
    if start:
        shapes = [(start, state, inner), (start, 8, inner), (start, 8, wide)]
        next_specs = [anywhere, whole(shapes[1]), whole(shapes[2])]
        next_shapes = [jax.ShapeDtypeStruct(shape, f32) for shape in shapes]
    grid_spec = pltpu.PrefetchScalarGridSpec(
        num_scalar_prefetch=1,
        grid=(count,),
        in_specs=[
            later(inner),
            later(inner),
            later(inner),
            pl.BlockSpec((length, inner), lambda b, *_: (start + top - b, 1)),
            pl.BlockSpec((1, state, inner), lambda b, *_: (start + top - b, 0, 0)),
            later(wide),
            later(wide),
            later(wide),
            later(heads),
            whole(conv_x.shape),
            whole(conv_bc.shape),
            whole((1, heads)),
            whole((1, heads)),
            whole((1, inner)),
            whole(sel.shape),
            whole(sel_t.shape),
        ]
        + carry_specs,
        out_specs=[
            rows(inner),
            rows(wide),
            rows(small - wide),
            whole(conv_x.shape),
            whole(conv_bc.shape),
            whole((1, inner)),
            whole((2, heads)),
        ]
        + next_specs,
        scratch_shapes=[
            pltpu.VMEM((blocks + 1, state, inner), f32),
            pltpu.VMEM((blocks + 1, 8, inner), f32),
            pltpu.VMEM((blocks + 1, 8, wide), f32),
            pltpu.VMEM((3 * length, 2 * heads), bf16),
            pltpu.VMEM((length, length), f32),
            pltpu.VMEM((length, length), f32),
            pltpu.VMEM((length, length), f32),
            pltpu.VMEM((length, length), f32),
            pltpu.VMEM((length, state), f32),
            pltpu.VMEM((length, state), f32),
            pltpu.VMEM((3 * length + 16, sel_t.shape[1]), f32),
            pltpu.VMEM((length, length), f32),
            pltpu.VMEM((length, lanes), f32),
        ],
    )
    return pl.pallas_call(
        functools.partial(backward_kernel, sizes),
        grid_spec=grid_spec,
        out_shape=[
            jax.ShapeDtypeStruct((tokens, inner), bf16),
            jax.ShapeDtypeStruct((tokens, wide), bf16),
            jax.ShapeDtypeStruct((tokens, small - wide), bf16),
            jax.ShapeDtypeStruct(conv_x.shape, f32),
            jax.ShapeDtypeStruct(conv_bc.shape, f32),
            jax.ShapeDtypeStruct((1, inner), f32),
            jax.ShapeDtypeStruct((2, heads), f32),
        ]
        + next_shapes,
        compiler_params=pltpu.CompilerParams(vmem_limit_bytes=VMEM_LIMIT),
        cost_estimate=LIGHT,
        name="ssd_backward",
    )(
        parent, dy, xc, pre, zx, hs, bcc, bcp, bc_pre, dt_raw, conv_x, conv_bc,
        dt_bias[None], a_log[None], skip_l, sel, sel_t, *carry,
    )


def add_kernel(terms, *refs):
    out_refs = refs[terms:]
    size = out_refs[0].shape[0]
    for i, out in enumerate(out_refs):
        rows = slice(i * size, (i + 1) * size)
        total = refs[0][rows, :].astype(f32)
        for ref in refs[1:terms]:
            total = total + ref[rows, :].astype(f32)
        out[...] = total.astype(out.dtype)


def run_add(values, pieces, kind):
    rows, width = values[0].shape
    tile = width // 2 if rows * width > 65536 and width % 256 == 0 else width
    spec = lambda size: pl.BlockSpec((size, tile), lambda j: (0, j))
    size = rows // pieces
    return pl.pallas_call(
        functools.partial(add_kernel, len(values)),
        grid=(width // tile,),
        in_specs=[spec(rows)] * len(values),
        out_specs=[spec(size)] * pieces,
        out_shape=[jax.ShapeDtypeStruct((size, width), kind)] * pieces,
        compiler_params=pltpu.CompilerParams(vmem_limit_bytes=VMEM_LIMIT),
        cost_estimate=LIGHT,
        name="add_parts",
    )(*values)


def mixed_kernel(full, terms, sq_ref, x_ref, *refs):
    length = x_ref.shape[0]
    inv = lax.rsqrt(token_column(sq_ref, pl.program_id(0), length)[:, :1] / full + epsilon)
    total = refs[0][...].astype(f32)
    for ref in refs[1:terms]:
        total = total + ref[...].astype(f32)
    refs[terms][...] = (x_ref[...].astype(f32) + inv * total).astype(bf16)


def run_mixed(squares, x_in, values, full):
    tokens, features = x_in.shape
    blocks, length = squares.shape
    rows = pl.BlockSpec((length, features), lambda b: (b, 0))
    return pl.pallas_call(
        functools.partial(mixed_kernel, full, len(values)),
        grid=(blocks,),
        in_specs=[pl.BlockSpec((blocks, length), lambda b: (0, 0)), rows] + [rows] * len(values),
        out_specs=rows,
        out_shape=jax.ShapeDtypeStruct((tokens, features), bf16),
        compiler_params=pltpu.CompilerParams(vmem_limit_bytes=VMEM_LIMIT),
        cost_estimate=LIGHT,
        name="layer_output",
    )(squares, x_in, *values)


def finish_kernel(terms, x_ref, cot_ref, inv_ref, gain_ref, *refs):
    x = x_ref[...].astype(f32)
    inv = inv_ref[...]
    total = refs[0][...].astype(f32)
    for ref in refs[1:terms]:
        total = total + ref[...].astype(f32)
    gained = total * gain_ref[...]
    spread = inv * inv * inv * jnp.sum(gained * x, axis=1, keepdims=True) / x.shape[1]
    refs[-1][...] = (cot_ref[...].astype(f32) + inv * gained - x * spread).astype(bf16)


def run_finish(values, x_in, cotangent, inv_rms, norm_gain, first, length, into):
    tokens, features = x_in.shape
    count = values[0].shape[0] // length
    later = lambda width: pl.BlockSpec((length, width), lambda b: (first + b, 0))
    rows = pl.BlockSpec((length, features), lambda b: (b, 0))
    extra = [] if into is None else [into]
    return pl.pallas_call(
        functools.partial(finish_kernel, len(values)),
        grid=(count,),
        in_specs=[later(features), later(features), later(1), pl.BlockSpec((1, features), lambda b: (0, 0))]
        + [rows] * len(values)
        + [pl.BlockSpec(memory_space=pl.ANY)] * len(extra),
        out_specs=later(features),
        out_shape=jax.ShapeDtypeStruct((tokens, features), bf16),
        input_output_aliases={} if into is None else {4 + len(values): 0},
        compiler_params=pltpu.CompilerParams(vmem_limit_bytes=VMEM_LIMIT),
        cost_estimate=LIGHT,
        name="input_grad_finish",
    )(x_in, cotangent, inv_rms, norm_gain[None], *values, *extra)


def over_columns(left, right):
    return lax.dot_general(left, right, (((1,), (1,)), ((), ())), preferred_element_type=f32)


def after(value, *others):
    return lax.optimization_barrier((value,) + others)[0]


def from_side(value):
    return lax.ppermute(value, "tensor", [(0, 1), (1, 0)])


def side_start(value):
    if lax.axis_size("tensor") == 2:
        return value, from_side(value)
    return None, lax.psum(value, "tensor")


def present(pair):
    return [value for value in pair if value is not None]


def side_total(pair):
    value, got = pair
    return got.astype(f32) if value is None else value.astype(f32) + got.astype(f32)


def pair_up(value, bit):
    size = lax.axis_size("dp")
    return lax.ppermute(value, "dp", [(i, i ^ bit) for i in range(size)])


def dealt_order(bits):
    order = [0]
    for bit in reversed(bits):
        order = order + [j | bit for j in order]
    return order


class Order:
    def __init__(self):
        self.pending = []

    def first(self, value):
        return after(value, *self.pending) if self.pending else value

    def then(self, value):
        self.pending = [value]
        return value

    def wait(self, value):
        self.pending = self.pending + [value]


def send_pieces(pieces, bit):
    return pieces[0], pair_up(pieces[1], bit)


def add_all(order, sent, kind=bf16):
    kept, got = sent
    return order.then(run_add([order.first(kept), got], 1, kind)[0])


def add_send(order, sent, bit):
    kept, got = sent
    pieces = run_add([order.first(kept), got], 2, bf16)
    order.then(pieces[0])
    return send_pieces(pieces, bit)


def add_last(order, sent, bits):
    for bit in bits:
        sent = add_send(order, sent, bit)
    return add_all(order, sent)


def send_same(value, bit):
    return value, pair_up(value, bit)


def local(
    x_in,
    norm_gain,
    w_zx,
    w_bc,
    w_dt,
    conv_x,
    conv_bc,
    dt_bias,
    a_log,
    d_skip,
    gate_gain,
    w_out,
    cotangent,
    block_parent,
):
    tokens, features = x_in.shape
    heads = w_dt.shape[1]
    inner = w_zx.shape[2]
    head_dim = inner // heads
    sides = lax.axis_size("tensor")
    dp = lax.axis_size("dp")
    full = inner * sides
    blocks = block_parent.shape[0]
    length = tokens // blocks
    wide = w_bc.shape[1]
    small = -(-(wide + heads) // 128) * 128
    window = conv_x.shape[0] - 1
    share = features // dp
    me = lax.axis_index("dp")

    near = []
    bit = 2
    while bit < dp:
        near.append(bit)
        bit *= 2
    far = near[1:] + near[:1]

    def places(bits):
        return lax.bitwise_xor(me, jnp.asarray(dealt_order(bits), jnp.int32)).astype(jnp.int32)

    place_near, place_far = places(near), places(far)

    head_of = jnp.arange(inner, dtype=jnp.int32) // head_dim
    one_hot = (jnp.arange(heads, dtype=jnp.int32)[:, None] == head_of[None, :]).astype(bf16)
    sel = jnp.concatenate([one_hot, one_hot], axis=0)
    sel_t = (jnp.arange(128, dtype=jnp.int32)[None, :] == head_of[:, None]).astype(bf16)
    skip_l = jnp.repeat(d_skip, head_dim)[None]

    count = blocks // 2
    step = count * length
    w_dt_t = w_dt.T
    join = lambda values: jnp.concatenate(values, axis=0)

    order = Order()
    normed, turned, inv_rms, bc_pre, dt_raw = run_norm(x_in, cotangent, norm_gain, w_bc, w_dt_t, length)
    turned_near = pair_up(turned, 1)
    w_cat = w_zx.reshape(features, 2 * inner)
    zx = jnp.dot(normed, w_cat, preferred_element_type=f32).astype(bf16)
    y, xc, pre, gg, bcc, bcp, hs, sq = run_forward(
        block_parent, bc_pre, dt_raw, zx, conv_x, conv_bc, dt_bias, a_log, skip_l, gate_gain, sel
    )
    gg_near = pair_up(gg, 1)
    out, cross = run_output(gg, w_out, cotangent)
    sums = side_total(side_start(join([sq[:, 0, :], cross[0].reshape(blocks, length)])))
    got_out = side_start(after(out, sums))
    dgn = over_columns(after(cotangent, out), w_out).astype(bf16)
    squares, crosses = sums[:blocks], sums[blocks:]
    inv_gate = lax.rsqrt(squares / full + epsilon)
    scale = inv_gate.reshape(1, tokens)
    scale = jnp.concatenate([scale, pair_up(scale, 1)], axis=1)
    dz, dy, gg_grad = run_ungate(squares, crosses, y, zx, dgn, gate_gain, full)
    order.then(dz)
    dz_near = pair_up(dz, 1)
    rights = [order.first(gg), gg_near]
    pieces = run_grad(place_near, 1, turned, turned_near, rights, share, 0, inner, 2, scale)
    order.then(pieces[0])
    w_out_1 = send_pieces(pieces, near[0])
    rights = [order.first(dz), dz_near]
    pieces = run_grad(place_near, 0, turned, turned_near, rights, share, 0, inner, 2)
    order.then(pieces[0])
    w_z_1 = send_pieces(pieces, near[0])

    tail = (conv_x, conv_bc, dt_bias, a_log, skip_l, sel, sel_t, small)
    back = run_backward(
        0, blocks, block_parent, order.first(dy), xc, pre, zx, hs, bcc, bcp, bc_pre, dt_raw, *tail, ()
    )
    dx, dbc, ddt, gkx, gkbc, gskip, ghead = back
    order.then(dx)
    order.wait(got_out[1])
    order.wait(w_out_1[1])
    w_out_2 = add_send(order, w_out_1, near[1])
    dx_near = pair_up(dx, 1)
    got_bc = side_start(dbc)
    low_1, gain_1 = run_input(dz, order.first(dx), dbc, ddt, w_cat, w_bc, w_dt_t, x_in, inv_rms, 0, step)
    order.then(low_1)
    got_low_1 = side_start(low_1)
    w_out_3 = add_send(order, w_out_2, near[2])
    got_bc = tuple(None if value is None else order.first(value) for value in got_bc)
    d_small = jnp.concatenate([side_total(got_bc).astype(bf16), ddt], axis=1)
    order.then(d_small)
    small_near = pair_up(d_small, 1)
    order.wait(dx_near)
    low_2, gain_2 = run_input(dz, order.first(dx), dbc, ddt, w_cat, w_bc, w_dt_t, x_in, inv_rms, 1, step)
    order.then(low_2)
    order.wait(small_near)
    got_low_2 = side_start(low_2)
    w_z_2 = add_send(order, w_z_1, near[1])
    edge = inner * 5 // 8 // 256 * 256
    pieces = run_grad(place_near, 0, turned, turned_near, [order.first(dx), dx_near], share, 0, edge, 2)
    order.then(pieces[1])
    sent_a = send_pieces(pieces, near[0])
    w_out_grad = add_last(order, w_out_3, near[3:])
    pieces = run_grad(place_near, 0, turned, turned_near, [order.first(d_small), small_near], share, 0, small, 2)
    order.then(pieces[1])
    sent_s = send_pieces(pieces, near[0])
    pieces = run_grad(place_far, 0, turned, turned_near, [order.first(dx), dx_near], share, edge, inner - edge, 2)
    order.then(pieces[1])
    w_z_3 = add_send(order, w_z_2, near[2])

    def finish(part, got, into):
        values = present(got)
        values = [order.first(values[0])] + values[1:]
        return order.then(
            run_finish(values, x_in, cotangent, inv_rms, norm_gain, part * count, length, into)
        )

    def spread_rows(sent, bit):
        kept, got = sent
        places_s.extend([j ^ bit for j in places_s])
        return order.then(join([order.first(kept), got]))

    places_s = [0]
    input_grad = finish(0, got_low_1, None)
    sent_b = send_pieces(pieces, far[0])
    sent_a = add_send(order, sent_a, near[1])
    sent_s = add_send(order, sent_s, near[1])
    mixed = order.then(run_mixed(squares, order.first(x_in), present(got_out), full))
    w_z_grad = add_last(order, w_z_3, near[3:])
    gain_1, gain_2, gkbc, gskip, gkx, ghead, gg_grad = order.first((gain_1, gain_2, gkbc, gskip, gkx, ghead, gg_grad))
    shared = jnp.concatenate([(gain_1 + gain_2).reshape(-1), gkbc.reshape(-1)])
    d_skip_part = jnp.sum(gskip.reshape(heads, head_dim), axis=1)
    own = jnp.concatenate(
        [gkx.reshape(-1), ghead.reshape(-1), d_skip_part, gg_grad.reshape(-1)]
    )
    n_shared, n_own = shared.shape[0], own.shape[0]
    pad_shared = -(-n_shared // 1024) * 1024
    pad_own = -(-n_own // 1024) * 1024
    shared = jnp.concatenate([shared, jnp.zeros((pad_shared - n_shared,), f32)]).reshape(-1, 128)
    own = jnp.concatenate([own, jnp.zeros((pad_own - n_own,), f32)]).reshape(-1, 128)
    packed = join([shared, own])

    order.then(packed)
    packed = send_same(packed, 1)
    sent_b = add_send(order, sent_b, far[1])
    packed = send_same(add_all(order, packed, f32), near[0])
    sent_a = add_send(order, sent_a, near[2])
    sent_s = add_send(order, sent_s, near[2])
    packed = send_same(add_all(order, packed, f32), near[1])
    order.wait(got_low_2[1])
    input_grad = finish(1, got_low_2, input_grad)
    w_s = add_last(order, sent_s, near[3:])
    rows_bc = send_same(w_s[:, :wide], near[2])
    sent_b = add_send(order, sent_b, far[2])
    packed = send_same(add_all(order, packed, f32), near[2])
    rows_bc = send_same(spread_rows(rows_bc, near[2]), near[1])
    w_x_a = add_last(order, sent_a, near[3:])
    packed = add_all(order, packed, f32)
    for bit in near[3:]:
        packed = add_all(order, send_same(packed, bit), f32)
    got_shared = side_start(packed[: pad_shared // 128])
    rows_bc = send_same(spread_rows(rows_bc, near[1]), near[0])
    w_x_b = add_last(order, sent_b, far[3:])
    rows_bc = spread_rows(rows_bc, near[0])
    for bit in near[3:]:
        rows_bc = spread_rows(send_same(rows_bc, bit), bit)
    rows_bc = spread_rows(send_same(rows_bc, 1), 1)
    chunks = rows_bc.reshape(dp, share, wide)
    back_to = jnp.asarray([places_s.index(j) for j in range(dp)], jnp.int32)
    w_bc_grad = jnp.take(chunks, back_to[lax.bitwise_xor(me, jnp.arange(dp, dtype=jnp.int32))], axis=0)
    w_bc_grad = w_bc_grad.reshape(features, wide).astype(f32)
    w_dt_grad = w_s[:, wide : wide + heads].astype(f32)
    w_x_grad = jnp.concatenate([w_x_a, w_x_b], axis=1)
    shared = side_total(got_shared).reshape(-1)
    own = packed[pad_shared // 128 :].reshape(-1)

    edge = (window + 1) * inner
    w_zx_grad = jnp.stack([w_z_grad, w_x_grad], axis=1).astype(f32)
    return (
        mixed,
        input_grad,
        shared[:features],
        w_zx_grad,
        w_bc_grad,
        w_dt_grad,
        own[:edge].reshape(window + 1, inner),
        shared[features:n_shared].reshape(window + 1, wide),
        own[edge : edge + heads],
        own[edge + heads : edge + 2 * heads],
        own[edge + 2 * heads : edge + 3 * heads],
        own[edge + 3 * heads : n_own],
        w_out_grad.astype(f32).T,
    )


def solution(mesh):
    return jax.shard_map(
        local,
        mesh=mesh,
        in_specs=(
            P("dp", None),
            P(),
            P(None, None, "tensor"),
            P(),
            P(None, "tensor"),
            P(None, "tensor"),
            P(),
            P("tensor"),
            P("tensor"),
            P("tensor"),
            P("tensor"),
            P("tensor", None),
            P("dp", None),
            P("dp"),
        ),
        out_specs=(
            P("dp", None),
            P("dp", None),
            P(),
            P("dp", None, "tensor"),
            P(),
            P("dp", "tensor"),
            P(None, "tensor"),
            P(),
            P("tensor"),
            P("tensor"),
            P("tensor"),
            P("tensor"),
            P("tensor", "dp"),
        ),
        check_vma=False,
    )
```

time: 1190 us -> 464 us (0.39)
  matrix products: 397 us -> 36.8 us
  Pallas kernels: 0 us -> 285 us
  waiting for transfers between devices: 280 us -> 39.9 us
  other arithmetic: 188 us -> 11.2 us
  local copies, waits for them, and re-layouts: 181 us -> 40.5 us
  blocking collectives: 112 us -> 0 us
  starting transfers between devices: 0.29 us -> 46.3 us
  between operations: 17.3 us -> 1.13 us
    dot_general x59 -> x1, matrix products: 331 us -> 22.9 us  [local(): zx = jnp.dot(normed, w_cat, preferred_element_type=f32).astype(bf16)]
    pallas_call x0 -> x34, Pallas kernels: none -> 285 us  [the longest x5 61.2 us: run_grad(): pl.pallas_call(functools.partial(grad_kernel, share, which, len(rights),...]
    reduce_scatter x2 -> x0, waiting for transfers between devices: 202 us -> none  [the longest x1 183 us: local(): lax.psum_scatter(w_zx_part.astype(jnp.bfloat16), 'dp', scatter_dimension=...]
    psum x4 -> x0, blocking collectives: 112 us -> none  [the longest x1 59.2 us: local(): lax.psum((conv_x_part, dt_bias_part, a_log_part, d_skip_part, gate_gain_p...]
    reshape x6 -> x7, local copies, waits for them, and re-layouts: 68.4 us -> 2.22 us  [the longest x1 0.81 us: local(): own = packed[pad_shared // 128:].reshape(-1)]
    reduce_sum x9 -> x1, other arithmetic: 56.6 us -> 0.11 us  [local(): d_skip_part = jnp.sum(gskip.reshape(heads, head_dim), axis=1)]
    all_gather x1 -> x0, waiting for transfers between devices: 56.4 us -> none  [local(): lax.all_gather(d_input.astype(jnp.bfloat16), 'tensor', axis=0, tiled=True)]
    dot_general x5 -> x1, matrix products: 66 us -> 13.9 us  [over_columns(): lax.dot_general(left, right, (((1,), (1,)), ((), ())), preferred_element_...]
  transfers between devices with their start and end apart: 7 -> 35, of which waited for: 4 -> 8; matrix products, arithmetic and copies ran while one was open for 38% -> 17% of each run, Pallas kernels for 0% -> 59%
where the time goes in v1:
time: 464 us; the launch traced here: 461 us
  Pallas kernels  285 us (61%)
  starting transfers between devices  46.3 us (10%)
  local copies, waits for them, and re-layouts  40.5 us (9%)
  waiting for transfers between devices  39.9 us (9%)
  matrix products  36.8 us (8%)
  other arithmetic  11.2 us (2%)
    pallas_call x5, Pallas kernels, run_grad(): pl.pallas_call(functools.partial(grad_kernel, share, which, len(rights),...  61.2 us
    pallas_call x1, Pallas kernels, run_backward(): pl.pallas_call(functools.partial(backward_kernel, sizes), grid_spec=grid_...  55 us
    ppermute x29, starting transfers between devices, pair_up(): return lax.ppermute(value, 'dp', [(i, i ^ bit) for i in range(size)])  42 us
    ppermute x29, waiting for transfers between devices, pair_up(): return lax.ppermute(value, 'dp', [(i, i ^ bit) for i in range(size)])  39.9 us
    pallas_call x19, Pallas kernels, run_add(): pl.pallas_call(functools.partial(add_kernel, len(values)), grid=(width //...  39.3 us
    pallas_call x2, Pallas kernels, run_input(): pl.pallas_call(functools.partial(input_kernel, heads), grid=(features //...  33.5 us
    pallas_call x1, Pallas kernels, run_forward(): pl.pallas_call(functools.partial(forward_kernel, sizes), grid_spec=grid_s...  32.2 us
    unnamed x71, local copies, waits for them, and re-layouts  31.4 us
  transfers between devices with their start and end apart: 35, of which 8 were waited for; matrix products, arithmetic and copies ran while one was open for 17% of the time, Pallas kernels for 59%

profile of v1, /device:TPU:1, one launch (start us, length us, event | category | flops | bytes accessed | tf_op | source)
XLA Modules:
  0.0 460.8 jit_solution(12261238494445448207)
XLA Ops:
  0.6 11.7 %input_norm.1 = (bf16[1024,2048]{1,0:T(8,128)(2,1)}, bf16[2,2048,1024]{2,1,0:T(8,128)(2,1)}, f32[1024,1]{1,0:T(8,128)}, f32[1024,256]{1,0:T(8,128)}, f32[1024,32]{1,0:T(8,128)}) custom-call(bf16[1024,2048]{1,0:T(8,128)(2,1)} %x_ref.10, bf16[1024,2048]{1,0:T(8,128)(2,1)} %cot_ref.7, f32[1,2048]{1,0:T(1,128)} %bitcast.54, bf16[2048,256]{1,0:T(8,128)(2,1)} %wbc_ref.5, ...), custom_call_target="tpu_custom_call" | custom-call | flops 1000 | bytes 1000 | tf_op jit(solution)/shard_map/input_norm/pallas_call | solution.py:366
  12.5 17.3 %copy.39 = bf16[256,8,2,2048]{3,1,2,0:T(8,128)(2,1)} copy(bf16[256,8,2,2048]{3,2,1,0:T(2,128)(2,1)} %bitcast.47) | data formatting | bytes 33554432
  31.3 22.9 %convolution_convert_fusion.z_ref.xp_ref = bf16[1024,4096]{1,0:T(8,128)(2,1)} fusion(bf16[1024,2048]{1,0:T(8,128)(2,1)} %get-tuple-element.119, bf16[2048,4096]{1,0:T(8,128)(2,1)} %bitcast.42), kind=kOutput, calls=%fused_computation.2 | convolution fusion | flops 17184063488 | bytes 29360128 | tf_op jit(solution)/shard_map/dot_general | solution.py:1046
  54.2 32.2 %ssd_forward.1 = (bf16[1024,2048]{1,0:T(8,128)(2,1)}, bf16[1024,2048]{1,0:T(8,128)(2,1)}, bf16[1024,2048]{1,0:T(8,128)(2,1)}, bf16[1024,2048]{1,0:T(8,128)(2,1)}...) custom-call(s32[8]{0:T(128)} %par_ref.3, ...), custom_call_target="tpu_custom_call" | custom-call | flops 1000 | bytes 1000 | tf_op jit(solution)/shard_map/ssd_forward/pallas_call | solution.py:244
  86.9 15.5 %output_project.1 = (bf16[1024,2048]{1,0:T(8,128)(2,1)}, f32[8,1024]{1,0:T(8,128)}) custom-call(bf16[1024,2048]{1,0:T(8,128)(2,1)} %get-tuple-element.129.left_ref.rest_0_, bf16[2048,2048]{1,0:T(8,128)(2,1)} %right_ref.1, bf16[1024,2048]{1,0:T(8,128)(2,1)} %cot_ref.7), custom_call_target="tpu_custom_call" | custom-call | flops 1000 | bytes 1000 | tf_op jit(solution)/shard_map/output_project/pallas_call | solution.py:328
  105.5 13.9 %convolution_convert_fusion.1.dgn_ref = bf16[1024,2048]{1,0:T(8,128)(2,1)} fusion(bf16[1024,2048]{1,0:T(8,128)(2,1)} %cot_ref.7, bf16[2048,2048]{1,0:T(8,128)(2,1)} %right_ref.1), kind=kOutput, calls=%fused_computation.3 | convolution fusion | flops 8592031744 | bytes 16777216 | tf_op jit(solution)/shard_map/dot_general | solution.py:909
  120.0 14.5 %gate_backward.1 = (bf16[1024,2048]{1,0:T(8,128)(2,1)}, bf16[1024,2048]{1,0:T(8,128)(2,1)}, f32[1,2048]{1,0:T(1,128)}) custom-call(f32[8,128]{1,0:T(8,128)} %get-tuple-element.252.sq_ref, f32[8,128]{1,0:T(8,128)} %get-tuple-element.251.cross_ref, bf16[1024,2048]{1,0:T(8,128)(2,1)} %get-tuple-element.124.y_ref, ...), custom_call_target="tpu_custom_call" | custom-call | flops 1000 | bytes 1000 | tf_op jit(solution)/shard_map/gate_backward/pallas_call | solution.py:299
  136.0 5.1 %collective-permute-done.3 = f32[1,1024]{1,0:T(1,128)S(1)} collective-permute-done((f32[1,1024]{1,0:T(1,128)S(1)}, f32[1,1024]{1,0:T(1,128)S(1)}, u32[]{:S(2)}, u32[]{:S(2)}) %collective-permute-start.3) | collective-permute-done | bytes 4128 | tf_op jit(solution)/shard_map/ppermute | solution.py:937
  141.6 16.1 %weight_grad.5 = (bf16[512,2048]{1,0:T(8,128)(2,1)}, bf16[512,2048]{1,0:T(8,128)(2,1)}) custom-call(s32[8]{0:T(128)} %broadcast_xor_fusion.1.place_ref, bf16[2,2048,1024]{2,1,0:T(8,128)(2,1)} %get-tuple-element.123.mine_ref, bf16[2,2048,1024]{2,1,0:T(8,128)(2,1)} %collective-permute-done.1.theirs_ref, ...), custom_call_target="tpu_custom_call" | custom-call | flops 1000 | bytes 1000 | tf_op jit(solution)/shard_map/weight_grad/pallas_call | solution.py:456
  161.1 15.5 %weight_grad.6 = (bf16[512,2048]{1,0:T(8,128)(2,1)}, bf16[512,2048]{1,0:T(8,128)(2,1)}) custom-call(s32[8]{0:T(128)} %broadcast_xor_fusion.1.place_ref, bf16[2,2048,1024]{2,1,0:T(8,128)(2,1)} %get-tuple-element.123.mine_ref, bf16[2,2048,1024]{2,1,0:T(8,128)(2,1)} %collective-permute-done.1.theirs_ref, bf16[1024,2048]{1,0:T(8,128)(2,1)} %get-tuple-element.131.rest_0_.dz_ref, ...), custom_call_target="tpu_custom_call" | custom-call | flops 1000 | bytes 1000 | tf_op jit(solution)/shard_map/weight_grad/pallas_call | solution.py:456
  176.5 55.0 %ssd_backward.1 = (bf16[1024,2048]{1,0:T(8,128)(2,1)}, bf16[1024,256]{1,0:T(8,128)(2,1)}, bf16[1024,128]{1,0:T(8,128)(2,1)}, f32[5,2048]{1,0:T(8,128)}, f32[5,25...) custom-call(s32[8]{0:T(128)} %par_ref.3, bf16[1024,2048]{1,0:T(8,128)(2,1)} %get-tuple-element.133.dy_ref, ...), custom_call_target="tpu_custom_call" | custom-call | flops 1000 | bytes 1000 | tf_op jit(solution)/shard_map/ssd_backward/pallas_call | solution.py:801
  238.9 16.7 %input_grad.2 = (bf16[512,2048]{1,0:T(8,128)(2,1)}, f32[1,2048]{1,0:T(1,128)}) custom-call(bf16[1024,2048]{1,0:T(8,128)(2,1)} %get-tuple-element.131.rest_0_.dz_ref, bf16[1024,2048]{1,0:T(8,128)(2,1)} %get-tuple-element.167.dx_ref.rest_0_, bf16[1024,256]{1,0:T(8,128)(2,1)} %get-tuple-element.152.dbc_ref, bf16[1024,128]{1,0:T(8,128)(2,1)} %get-tuple-element.146.ddt_ref, ...), custom_call_target="tpu_custom_call" | custom-call | flops 1000 | bytes 1000 | tf_op jit(solution)/shard_map/input_grad/pallas_call | solution.py:491
  256.7 5.3 %collective-permute-done.7.refs_1_ = bf16[256,2048]{1,0:T(8,128)(2,1)} collective-permute-done((bf16[256,2048]{1,0:T(8,128)(2,1)}, bf16[256,2048]{1,0:T(8,128)(2,1)}, u32[]{:S(2)}, u32[]{:S(2)}) %collective-permute-start.7) | collective-permute-done | bytes 1048608 | tf_op jit(solution)/shard_map/ppermute | solution.py:937
  266.6 16.7 %input_grad.3 = (bf16[512,2048]{1,0:T(8,128)(2,1)}, f32[1,2048]{1,0:T(1,128)}) custom-call(bf16[1024,2048]{1,0:T(8,128)(2,1)} %get-tuple-element.131.rest_0_.dz_ref, bf16[1024,2048]{1,0:T(8,128)(2,1)} %get-tuple-element.167.dx_ref.rest_0_, bf16[1024,256]{1,0:T(8,128)(2,1)} %get-tuple-element.152.dbc_ref, bf16[1024,128]{1,0:T(8,128)(2,1)} %get-tuple-element.146.ddt_ref, ...), custom_call_target="tpu_custom_call" | custom-call | flops 1000 | bytes 1000 | tf_op jit(solution)/shard_map/input_grad/pallas_call | solution.py:491
  290.3 11.7 %weight_grad.7 = (bf16[512,1280]{1,0:T(8,128)(2,1)}, bf16[512,1280]{1,0:T(8,128)(2,1)}) custom-call(s32[8]{0:T(128)} %broadcast_xor_fusion.1.place_ref, bf16[2,2048,1024]{2,1,0:T(8,128)(2,1)} %get-tuple-element.123.mine_ref, bf16[2,2048,1024]{2,1,0:T(8,128)(2,1)} %collective-permute-done.1.theirs_ref, bf16[1024,2048]{1,0:T(8,128)(2,1)} %get-tuple-element.167.dx_ref.rest_0_, ...), custom_call_target="tpu_custom_call" | custom-call | flops 1000 | bytes 1000 | tf_op jit(solution)/shard_map/weight_grad/pallas_call | solution.py:456
  305.6 17.6 %collective-permute-done.12.refs_1_ = bf16[128,2048]{1,0:T(8,128)(2,1)S(1)} collective-permute-done((bf16[128,2048]{1,0:T(8,128)(2,1)S(1)}, bf16[128,2048]{1,0:T(8,128)(2,1)S(1)}, u32[]{:S(2)}, u32[]{:S(2)}) %collective-permute-start.12) | collective-permute-done | bytes 524320 | tf_op jit(solution)/shard_map/ppermute | solution.py:937
  325.9 8.8 %weight_grad.8 = (bf16[512,384]{1,0:T(8,128)(2,1)}, bf16[512,384]{1,0:T(8,128)(2,1)}) custom-call(s32[8]{0:T(128)} %broadcast_xor_fusion.1.place_ref, bf16[2,2048,1024]{2,1,0:T(8,128)(2,1)} %get-tuple-element.123.mine_ref, bf16[2,2048,1024]{2,1,0:T(8,128)(2,1)} %collective-permute-done.1.theirs_ref, bf16[1024,384]{1,0:T(8,128)(2,1)} %copy-done.1, ...), custom_call_target="tpu_custom_call" | custom-call | flops 1000 | bytes 1000 | tf_op jit(solution)/shard_map/weight_grad/pallas_call | solution.py:456
  334.7 9.2 %weight_grad.9 = (bf16[512,768]{1,0:T(8,128)(2,1)}, bf16[512,768]{1,0:T(8,128)(2,1)}) custom-call(s32[8]{0:T(128)} %broadcast_xor_fusion.place_ref, bf16[2,2048,1024]{2,1,0:T(8,128)(2,1)} %get-tuple-element.123.mine_ref, bf16[2,2048,1024]{2,1,0:T(8,128)(2,1)} %collective-permute-done.1.theirs_ref, bf16[1024,2048]{1,0:T(8,128)(2,1)} %get-tuple-element.167.dx_ref.rest_0_, ...), custom_call_target="tpu_custom_call" | custom-call | flops 1000 | bytes 1000 | tf_op jit(solution)/shard_map/weight_grad/pallas_call | solution.py:456
  355.2 6.4 %input_grad_finish.2.refs_2_ = bf16[1024,2048]{1,0:T(8,128)(2,1)} custom-call(bf16[1024,2048]{1,0:T(8,128)(2,1)} %x_ref.10, bf16[1024,2048]{1,0:T(8,128)(2,1)} %cot_ref.7, f32[1024,1]{1,0:T(8,128)} %get-tuple-element.147.inv_ref, f32[1,2048]{1,0:T(1,128)} %bitcast.55, bf16[512,2048]{1,0:T(8,128)(2,1)} %get-tuple-element.172.refs_0_, ...), custom_call_target="tpu_custom_call" | custom-call | flops 1000 | bytes 1000 | tf_op jit(solution)/shard_map/input_grad_finish/pallas_call | solution.py:893
  367.0 9.5 %layer_output.1 = bf16[1024,2048]{1,0:T(8,128)(2,1)} custom-call(f32[8,128]{1,0:T(8,128)} %get-tuple-element.252.sq_ref, bf16[1024,2048]{1,0:T(8,128)(2,1)} %x_ref.10, bf16[1024,2048]{1,0:T(8,128)(2,1)} %get-tuple-element.141.refs_0_, bf16[1024,2048]{1,0:T(8,128)(2,1)} %collective-permute-done.5.refs_1_), custom_call_target="tpu_custom_call" | custom-call | flops 1000 | bytes 1000 | tf_op jit(solution)/shard_map/layer_output/pallas_call | solution.py:864
  394.1 6.6 %collective-permute-done.21.refs_1_ = bf16[256,384]{1,0:T(8,128)(2,1)} collective-permute-done((bf16[256,384]{1,0:T(8,128)(2,1)}, bf16[256,384]{1,0:T(8,128)(2,1)}, u32[]{:S(2)}, u32[]{:S(2)}) %collective-permute-start.21) | collective-permute-done | bytes 196640 | tf_op jit(solution)/shard_map/ppermute | solution.py:937
  402.4 4.4 collective-permute-start.24
  413.6 6.4 %input_grad_finish.3 = bf16[1024,2048]{1,0:T(8,128)(2,1)} custom-call(bf16[1024,2048]{1,0:T(8,128)(2,1)} %x_ref.10, bf16[1024,2048]{1,0:T(8,128)(2,1)} %cot_ref.7, f32[1024,1]{1,0:T(8,128)} %get-tuple-element.147.inv_ref, f32[1,2048]{1,0:T(1,128)} %bitcast.56, bf16[512,2048]{1,0:T(8,128)(2,1)} %get-tuple-element.205.refs_0_, ...), custom_call_target="tpu_custom_call", output_to_operand_aliasing={{}: (6, {})} | custom-call | flops 1000 | bytes 1000 | tf_op jit(solution)/shard_map/input_grad_finish/pallas_call | solution.py:893
  446.4 6.0 %collective-permute-start.34 = (bf16[1024,256]{1,0:T(8,128)(2,1)S(1)}, bf16[1024,256]{1,0:T(8,128)(2,1)S(1)}, u32[]{:S(2)}, u32[]{:S(2)}) collective-permute-start(bf16[1024,256]{1,0:T(8,128)(2,1)S(1)} %constant_dynamic-update-slice_fusion.4), channel_id=1, source_target_pairs={{0,2},{2,0},{4,6},{6,4},{8,10},{10,8},{12,14},{14,12},{16,18},{18,... | collective-permute-start | bytes 1572872 | tf_op jit(solution)/shard_map/ppermute | solution.py:937
  (212 shorter events, 115.0 us)
Async XLA Ops:
  12.4 129.3 %collective-permute-start.1 = (bf16[2,2048,1024]{2,1,0:T(8,128)(2,1)}, bf16[2,2048,1024]{2,1,0:T(8,128)(2,1)}, u32[]{:S(2)}, u32[]{:S(2)}) collective-permute-start(bf16[2,2048,1024]{2,1,0:T(8,128)(2,1)} %get-tuple-element.123.mine_ref), channel_id=1, source_target_pairs={{0,2},{2,0},{4,6},{6,4},{8,10},{10,8},{12,14},{14,12},{16,18},{18,... | collective-permute-start | bytes 25165832 | tf_op jit(solution)/shard_map/ppermute | solution.py:937
  86.4 55.3 %collective-permute-start.2 = (bf16[1024,2048]{1,0:T(8,128)(2,1)}, bf16[1024,2048]{1,0:T(8,128)(2,1)}, u32[]{:S(2)}, u32[]{:S(2)}) collective-permute-start(bf16[1024,2048]{1,0:T(8,128)(2,1)} %get-tuple-element.129.left_ref.rest_0_), channel_id=1, source_target_pairs={{0,2},{2,0},{4,6},{6,4},{8,10},{10,8},{12,14},{14,12},{16,18},{18,... | collective-permute-start | bytes 12582920 | tf_op jit(solution)/shard_map/ppermute | solution.py:937
  103.1 16.2 %collective-permute-start = (f32[16,128]{1,0:T(8,128)S(1)}, f32[16,128]{1,0:T(8,128)S(1)}, u32[]{:S(2)}, u32[]{:S(2)}) collective-permute-start(f32[16,128]{1,0:T(8,128)S(1)} %pad_maximum_fusion.3), channel_id=1, source_target_pairs={{0,1},{1,0},{2,3},{3,2},{4,5},{5,4},{6,7},{7,6},{8,9},{9,8},{10,11... | collective-permute-start | bytes 24584 | tf_op jit(solution)/shard_map/ppermute | solution.py:917
  134.5 26.6 %collective-permute-start.4 = (bf16[1024,2048]{1,0:T(8,128)(2,1)}, bf16[1024,2048]{1,0:T(8,128)(2,1)}, u32[]{:S(2)}, u32[]{:S(2)}) collective-permute-start(bf16[1024,2048]{1,0:T(8,128)(2,1)} %get-tuple-element.131.rest_0_.dz_ref), channel_id=1, source_target_pairs={{0,2},{2,0},{4,6},{6,4},{8,10},{10,8},{12,14},{14,12},{16,18},{18,... | collective-permute-start | bytes 12582920 | tf_op jit(solution)/shard_map/ppermute | solution.py:937
  135.3 97.0 %collective-permute-start.5 = (bf16[1024,2048]{1,0:T(8,128)(2,1)}, bf16[1024,2048]{1,0:T(8,128)(2,1)}, u32[]{:S(2)}, u32[]{:S(2)}) collective-permute-start(bf16[1024,2048]{1,0:T(8,128)(2,1)} %get-tuple-element.141.refs_0_), channel_id=1, source_target_pairs={{0,1},{1,0},{2,3},{3,2},{4,5},{5,4},{6,7},{7,6},{8,9},{9,8},{10,11... | collective-permute-start | bytes 12582920 | tf_op jit(solution)/shard_map/ppermute | solution.py:917
  157.7 74.6 %collective-permute-start.6 = (bf16[512,2048]{1,0:T(8,128)(2,1)}, bf16[512,2048]{1,0:T(8,128)(2,1)S(1)}, u32[]{:S(2)}, u32[]{:S(2)}) collective-permute-start(bf16[512,2048]{1,0:T(8,128)(2,1)} %get-tuple-element.142), channel_id=1, source_target_pairs={{0,4},{2,6},{4,0},{6,2},{8,12},{10,14},{12,8},{14,10},{16,20},{18,... | collective-permute-start | bytes 6291464 | tf_op jit(solution)/shard_map/ppermute | solution.py:937
  231.6 35.0 %collective-permute-start.9 = (bf16[1024,2048]{1,0:T(8,128)(2,1)}, bf16[1024,2048]{1,0:T(8,128)(2,1)}, u32[]{:S(2)}, u32[]{:S(2)}) collective-permute-start(bf16[1024,2048]{1,0:T(8,128)(2,1)} %get-tuple-element.167.dx_ref.rest_0_), channel_id=1, source_target_pairs={{0,2},{2,0},{4,6},{6,4},{8,10},{10,8},{12,14},{14,12},{16,18},{18,... | collective-permute-start | bytes 12582920 | tf_op jit(solution)/shard_map/ppermute | solution.py:937
  236.9 25.1 %collective-permute-start.7 = (bf16[256,2048]{1,0:T(8,128)(2,1)}, bf16[256,2048]{1,0:T(8,128)(2,1)}, u32[]{:S(2)}, u32[]{:S(2)}) collective-permute-start(bf16[256,2048]{1,0:T(8,128)(2,1)} %get-tuple-element.150), channel_id=1, source_target_pairs={{0,8},{2,10},{4,12},{6,14},{8,0},{10,2},{12,4},{14,6},{16,24},{18,... | collective-permute-start | bytes 3145736 | tf_op jit(solution)/shard_map/ppermute | solution.py:937
  238.2 47.2 %collective-permute-start.11 = (bf16[512,2048]{1,0:T(8,128)(2,1)}, bf16[512,2048]{1,0:T(8,128)(2,1)S(1)}, u32[]{:S(2)}, u32[]{:S(2)}) collective-permute-start(bf16[512,2048]{1,0:T(8,128)(2,1)} %get-tuple-element.157), channel_id=1, source_target_pairs={{0,4},{2,6},{4,0},{6,2},{8,12},{10,14},{12,8},{14,10},{16,20},{18,... | collective-permute-start | bytes 6291464 | tf_op jit(solution)/shard_map/ppermute | solution.py:937
  238.6 25.9 %collective-permute-start.8 = (bf16[1024,256]{1,0:T(8,128)(2,1)}, bf16[1024,256]{1,0:T(8,128)(2,1)S(1)}, u32[]{:S(2)}, u32[]{:S(2)}) collective-permute-start(bf16[1024,256]{1,0:T(8,128)(2,1)} %get-tuple-element.152.dbc_ref), channel_id=1, source_target_pairs={{0,1},{1,0},{2,3},{3,2},{4,5},{5,4},{6,7},{7,6},{8,9},{9,8},{10,11... | collective-permute-start | bytes 1572872 | tf_op jit(solution)/shard_map/ppermute | solution.py:917
  255.7 95.1 %collective-permute-start.14 = (bf16[512,2048]{1,0:T(8,128)(2,1)}, bf16[512,2048]{1,0:T(8,128)(2,1)}, u32[]{:S(2)}, u32[]{:S(2)}) collective-permute-start(bf16[512,2048]{1,0:T(8,128)(2,1)} %get-tuple-element.172.refs_0_), channel_id=1, source_target_pairs={{0,1},{1,0},{2,3},{3,2},{4,5},{5,4},{6,7},{7,6},{8,9},{9,8},{10,11... | collective-permute-start | bytes 6291464 | tf_op jit(solution)/shard_map/ppermute | solution.py:917
  265.7 17.6 %collective-permute-start.10 = (bf16[1024,384]{1,0:T(8,128)(2,1)S(1)}, bf16[1024,384]{1,0:T(8,128)(2,1)S(1)}, u32[]{:S(2)}, u32[]{:S(2)}) collective-permute-start(bf16[1024,384]{1,0:T(8,128)(2,1)S(1)} %pad_maximum_fusion.1.rest_0_), channel_id=1, source_target_pairs={{0,2},{2,0},{4,6},{6,4},{8,10},{10,8},{12,14},{14,12},{16,18},{18,... | collective-permute-start | bytes 2359304 | tf_op jit(solution)/shard_map/ppermute | solution.py:937
  290.1 53.8 %collective-permute-start.13 = (bf16[256,2048]{1,0:T(8,128)(2,1)}, bf16[256,2048]{1,0:T(8,128)(2,1)}, u32[]{:S(2)}, u32[]{:S(2)}) collective-permute-start(bf16[256,2048]{1,0:T(8,128)(2,1)} %get-tuple-element.170), channel_id=1, source_target_pairs={{0,8},{2,10},{4,12},{6,14},{8,0},{10,2},{12,4},{14,6},{16,24},{18,... | collective-permute-start | bytes 3145736 | tf_op jit(solution)/shard_map/ppermute | solution.py:937
  302.0 59.6 %collective-permute-start.15 = (bf16[512,1280]{1,0:T(8,128)(2,1)}, bf16[512,1280]{1,0:T(8,128)(2,1)}, u32[]{:S(2)}, u32[]{:S(2)}) collective-permute-start(bf16[512,1280]{1,0:T(8,128)(2,1)} %get-tuple-element.160), channel_id=1, source_target_pairs={{0,4},{2,6},{4,0},{6,2},{8,12},{10,14},{12,8},{14,10},{16,20},{18,... | collective-permute-start | bytes 3932168 | tf_op jit(solution)/shard_map/ppermute | solution.py:937
  302.4 20.8 %collective-permute-start.12 = (bf16[128,2048]{1,0:T(8,128)(2,1)S(1)}, bf16[128,2048]{1,0:T(8,128)(2,1)S(1)}, u32[]{:S(2)}, u32[]{:S(2)}) collective-permute-start(bf16[128,2048]{1,0:T(8,128)(2,1)S(1)} %copy-done.27), channel_id=1, source_target_pairs={{0,16},{2,18},{4,20},{6,22},{8,24},{10,26},{12,28},{14,30},{16,0},... | collective-permute-start | bytes 1572872 | tf_op jit(solution)/shard_map/ppermute | solution.py:937
  304.6 109.0 %collective-permute-start.23 = (bf16[512,2048]{1,0:T(8,128)(2,1)S(1)}, bf16[512,2048]{1,0:T(8,128)(2,1)}, u32[]{:S(2)}, u32[]{:S(2)}) collective-permute-start(bf16[512,2048]{1,0:T(8,128)(2,1)S(1)} %copy-done.3), channel_id=1, source_target_pairs={{0,1},{1,0},{2,3},{3,2},{4,5},{5,4},{6,7},{7,6},{8,9},{9,8},{10,11... | collective-permute-start | bytes 6291464 | tf_op jit(solution)/shard_map/ppermute | solution.py:917
  346.4 31.5 %collective-permute-start.17 = (bf16[128,2048]{1,0:T(8,128)(2,1)}, bf16[128,2048]{1,0:T(8,128)(2,1)}, u32[]{:S(2)}, u32[]{:S(2)}) collective-permute-start(bf16[128,2048]{1,0:T(8,128)(2,1)} %get-tuple-element.186), channel_id=1, source_target_pairs={{0,16},{2,18},{4,20},{6,22},{8,24},{10,26},{12,28},{14,30},{16,0},... | collective-permute-start | bytes 1572872 | tf_op jit(solution)/shard_map/ppermute | solution.py:937
  350.8 34.7 %collective-permute-start.18 = (bf16[512,768]{1,0:T(8,128)(2,1)}, bf16[512,768]{1,0:T(8,128)(2,1)S(1)}, u32[]{:S(2)}, u32[]{:S(2)}) collective-permute-start(bf16[512,768]{1,0:T(8,128)(2,1)} %get-tuple-element.168), channel_id=1, source_target_pairs={{0,8},{2,10},{4,12},{6,14},{8,0},{10,2},{12,4},{14,6},{16,24},{18,... | collective-permute-start | bytes 2359304 | tf_op jit(solution)/shard_map/ppermute | solution.py:937
  364.2 27.8 %collective-permute-start.20 = (bf16[256,1280]{1,0:T(8,128)(2,1)}, bf16[256,1280]{1,0:T(8,128)(2,1)}, u32[]{:S(2)}, u32[]{:S(2)}) collective-permute-start(bf16[256,1280]{1,0:T(8,128)(2,1)} %get-tuple-element.199), channel_id=1, source_target_pairs={{0,8},{2,10},{4,12},{6,14},{8,0},{10,2},{12,4},{14,6},{16,24},{18,... | collective-permute-start | bytes 1966088 | tf_op jit(solution)/shard_map/ppermute | solution.py:937
  376.5 24.2 %collective-permute-start.21 = (bf16[256,384]{1,0:T(8,128)(2,1)}, bf16[256,384]{1,0:T(8,128)(2,1)}, u32[]{:S(2)}, u32[]{:S(2)}) collective-permute-start(bf16[256,384]{1,0:T(8,128)(2,1)} %get-tuple-element.202), channel_id=1, source_target_pairs={{0,8},{2,10},{4,12},{6,14},{8,0},{10,2},{12,4},{14,6},{16,24},{18,... | collective-permute-start | bytes 589832 | tf_op jit(solution)/shard_map/ppermute | solution.py:937
  391.0 30.6 %collective-permute-start.25 = (bf16[256,768]{1,0:T(8,128)(2,1)}, bf16[256,768]{1,0:T(8,128)(2,1)S(1)}, u32[]{:S(2)}, u32[]{:S(2)}) collective-permute-start(bf16[256,768]{1,0:T(8,128)(2,1)} %get-tuple-element.209), channel_id=1, source_target_pairs={{0,16},{2,18},{4,20},{6,22},{8,24},{10,26},{12,28},{14,30},{16,0},... | collective-permute-start | bytes 1179656 | tf_op jit(solution)/shard_map/ppermute | solution.py:937
  402.4 17.6 %collective-permute-start.24 = (bf16[128,384]{1,0:T(8,128)(2,1)}, bf16[128,384]{1,0:T(8,128)(2,1)}, u32[]{:S(2)}, u32[]{:S(2)}) collective-permute-start(bf16[128,384]{1,0:T(8,128)(2,1)} %get-tuple-element.207), channel_id=1, source_target_pairs={{0,16},{2,18},{4,20},{6,22},{8,24},{10,26},{12,28},{14,30},{16,0},... | collective-permute-start | bytes 294920 | tf_op jit(solution)/shard_map/ppermute | solution.py:937
  408.9 18.6 %collective-permute-start.26 = (f32[136,128]{1,0:T(8,128)}, f32[136,128]{1,0:T(8,128)}, u32[]{:S(2)}, u32[]{:S(2)}) collective-permute-start(f32[136,128]{1,0:T(8,128)} %add_parts.31.refs_0_), channel_id=1, source_target_pairs={{0,8},{2,10},{4,12},{6,14},{8,0},{10,2},{12,4},{14,6},{16,24},{18,... | collective-permute-start | bytes 208904 | tf_op jit(solution)/shard_map/ppermute | solution.py:937
  413.6 22.0 %collective-permute-start.28 = (bf16[128,1280]{1,0:T(8,128)(2,1)}, bf16[128,1280]{1,0:T(8,128)(2,1)S(1)}, u32[]{:S(2)}, u32[]{:S(2)}) collective-permute-start(bf16[128,1280]{1,0:T(8,128)(2,1)} %get-tuple-element.214), channel_id=1, source_target_pairs={{0,16},{2,18},{4,20},{6,22},{8,24},{10,26},{12,28},{14,30},{16,0},... | collective-permute-start | bytes 983048 | tf_op jit(solution)/shard_map/ppermute | solution.py:937
  (44 other events, 439.7 us)

commit v2 on v1

--- a/solution.py
+++ b/solution.py
@@ -81,6 +81,7 @@
     dtr_ref,
     z_ref,
     xp_ref,
+    dgn_ref,
     kx_ref,
     kbc_ref,
     bias_ref,
@@ -104,6 +105,7 @@
     cumt_s,
     score_s,
     acc_s,
+    cross_s,
 ):
     length, inner, heads, head_dim, lanes, blocks, window = sizes
     state = bcc_ref.shape[1] // 2
@@ -134,6 +136,7 @@
     lhs_s[...] = jnp.concatenate([hi, lo], axis=1)
     store_columns(cum, cum_s, cumt_s, heads)
     acc_s[...] = jnp.zeros_like(acc_s)
+    cross_s[...] = jnp.zeros_like(cross_s)
     first = head_masks(length, head_dim)
     group = lanes // head_dim
     pair = 2 * head_dim
@@ -168,6 +171,8 @@
         zv = z_ref[:, sl].astype(f32)
         gate = zv * sigmoid(zv)
         acc = acc_s[...]
+        cross = cross_s[...]
+        dgn = dgn_ref[:, sl].astype(f32)
         for q in range(lanes // pair):
             at = slice(q * pair, (q + 1) * pair)
             weights = []
@@ -182,14 +187,18 @@
             gained = gated * gain[:, at]
             gg_ref[:, out] = gained.astype(bf16)
             acc = acc + gated * gated
+            cross = cross + dgn[:, at] * gained
         acc_s[...] = acc
+        cross_s[...] = cross
         return carry
 
     lax.fori_loop(0, inner // lanes, body, 0)
-    sq_ref[0] = dot(jnp.ones((8, pair), f32), acc_s[...], NT, highest)
-
-
-def run_forward(parent, bc_pre, dt_raw, zx, conv_x, conv_bc, dt_bias, a_log, skip_l, gate_gain, sel):
+    ones = jnp.ones((8, pair), f32)
+    sq_ref[0, :8, :] = dot(ones, acc_s[...], NT, highest)
+    sq_ref[0, 8:, :] = dot(ones, cross_s[...], NT, highest)
+
+
+def run_forward(parent, bc_pre, dt_raw, zx, dgn, conv_x, conv_bc, dt_bias, a_log, skip_l, gate_gain, sel):
     tokens = zx.shape[0]
     inner = conv_x.shape[1]
     heads = dt_raw.shape[1]
@@ -212,6 +221,7 @@
             rows(heads),
             rows(inner),
             pl.BlockSpec((length, inner), lambda b, *_: (b, 1)),
+            rows(inner),
             whole(conv_x.shape),
             whole(conv_bc.shape),
             whole((1, heads)),
@@ -228,7 +238,7 @@
             rows(wide),
             rows(wide),
             block((state, inner)),
-            block((8, length)),
+            block((16, length)),
         ],
         scratch_shapes=[
             pltpu.VMEM((blocks + 1, state, inner), f32),
@@ -238,6 +248,7 @@
             pltpu.VMEM((length, length), f32),
             pltpu.VMEM((length, length), f32),
             pltpu.VMEM((length, length), f32),
+            pltpu.VMEM((length, 2 * head_dim), f32),
             pltpu.VMEM((length, 2 * head_dim), f32),
         ],
     )
@@ -249,12 +260,12 @@
             jax.ShapeDtypeStruct((tokens, wide), bf16),
             jax.ShapeDtypeStruct((tokens, wide), f32),
             jax.ShapeDtypeStruct((blocks, state, inner), bf16),
-            jax.ShapeDtypeStruct((blocks, 8, length), f32),
+            jax.ShapeDtypeStruct((blocks, 16, length), f32),
         ],
         compiler_params=pltpu.CompilerParams(vmem_limit_bytes=VMEM_LIMIT),
         cost_estimate=LIGHT,
         name="ssd_forward",
-    )(parent, bc_pre, dt_raw, zx, zx, conv_x, conv_bc, dt_bias[None], a_log[None], skip_l, gate_gain[None], sel)
+    )(parent, bc_pre, dt_raw, zx, zx, dgn, conv_x, conv_bc, dt_bias[None], a_log[None], skip_l, gate_gain[None], sel)
 
 
 def token_column(row_ref, at, length):
@@ -306,42 +317,6 @@
         cost_estimate=LIGHT,
         name="gate_backward",
     )(squares, cross, y, zx, dgn, gate_gain[None])
-
-
-def output_kernel(left_ref, right_ref, cot_ref, out_ref, cross_ref):
-    total = dot(left_ref[...], right_ref[...])
-    product = (total * cot_ref[...].astype(f32)).astype(bf16)
-    row = dot(jnp.ones((8, product.shape[1]), bf16), product, NT)
-
-    @pl.when(pl.program_id(0) == 0)
-    def _():
-        cross_ref[...] = jnp.zeros_like(cross_ref)
-
-    cross_ref[...] += row
-    out_ref[...] = total.astype(bf16)
-
-
-def run_output(gained, w_out, cotangent):
-    tokens, inner = gained.shape
-    features = w_out.shape[1]
-    tile = min(512, features)
-    return pl.pallas_call(
-        output_kernel,
-        grid=(features // tile,),
-        in_specs=[
-            pl.BlockSpec((tokens, inner), lambda j: (0, 0), pipeline_mode=pl.Buffered(1)),
-            pl.BlockSpec((inner, tile), lambda j: (0, j)),
-            pl.BlockSpec((tokens, tile), lambda j: (0, j)),
-        ],
-        out_specs=[pl.BlockSpec((tokens, tile), lambda j: (0, j)), pl.BlockSpec((8, tokens), lambda j: (0, 0))],
-        out_shape=[
-            jax.ShapeDtypeStruct((tokens, features), bf16),
-            jax.ShapeDtypeStruct((8, tokens), f32),
-        ],
-        compiler_params=pltpu.CompilerParams(vmem_limit_bytes=VMEM_LIMIT),
-        cost_estimate=LIGHT,
-        name="output_project",
-    )(gained, w_out, cotangent)
 
 
 def norm_kernel(features, x_ref, cot_ref, gain_ref, wbc_ref, wdt_ref, normed_ref, turned_ref, inv_ref, bc_ref, dtr_ref):
@@ -506,7 +481,7 @@
         out_specs=[pl.BlockSpec((tokens, tile), lambda j: (0, j)), pl.BlockSpec((1, tile), lambda j: (0, j))],
         out_shape=[jax.ShapeDtypeStruct((tokens, features), bf16), jax.ShapeDtypeStruct((1, features), f32)],
         compiler_params=pltpu.CompilerParams(vmem_limit_bytes=VMEM_LIMIT),
-        cost_estimate=LIGHT,
+        cost_estimate=pl.CostEstimate(flops=27 * 900_000_000, bytes_accessed=1000, transcendentals=0),
         name="input_grad",
     )(dz, dx, dbc, ddt, w_cat, w_cat, w_bc, w_dt_t, x_in, inv_rms)
 
@@ -884,25 +859,20 @@
     refs[-1][...] = (cot_ref[...].astype(f32) + inv * gained - x * spread).astype(bf16)
 
 
-def run_finish(values, x_in, cotangent, inv_rms, norm_gain, first, length, into):
+def run_finish(values, x_in, cotangent, inv_rms, norm_gain, length):
     tokens, features = x_in.shape
-    count = values[0].shape[0] // length
-    later = lambda width: pl.BlockSpec((length, width), lambda b: (first + b, 0))
-    rows = pl.BlockSpec((length, features), lambda b: (b, 0))
-    extra = [] if into is None else [into]
+    rows = lambda width: pl.BlockSpec((length, width), lambda b: (b, 0))
     return pl.pallas_call(
         functools.partial(finish_kernel, len(values)),
-        grid=(count,),
-        in_specs=[later(features), later(features), later(1), pl.BlockSpec((1, features), lambda b: (0, 0))]
-        + [rows] * len(values)
-        + [pl.BlockSpec(memory_space=pl.ANY)] * len(extra),
-        out_specs=later(features),
+        grid=(tokens // length,),
+        in_specs=[rows(features), rows(features), rows(1), pl.BlockSpec((1, features), lambda b: (0, 0))]
+        + [rows(features)] * len(values),
+        out_specs=rows(features),
         out_shape=jax.ShapeDtypeStruct((tokens, features), bf16),
-        input_output_aliases={} if into is None else {4 + len(values): 0},
         compiler_params=pltpu.CompilerParams(vmem_limit_bytes=VMEM_LIMIT),
         cost_estimate=LIGHT,
         name="input_grad_finish",
-    )(x_in, cotangent, inv_rms, norm_gain[None], *values, *extra)
+    )(x_in, cotangent, inv_rms, norm_gain[None], *values)
 
 
 def over_columns(left, right):
@@ -1044,14 +1014,15 @@
     turned_near = pair_up(turned, 1)
     w_cat = w_zx.reshape(features, 2 * inner)
     zx = jnp.dot(normed, w_cat, preferred_element_type=f32).astype(bf16)
+    dgn = over_columns(after(cotangent, zx), w_out).astype(bf16)
     y, xc, pre, gg, bcc, bcp, hs, sq = run_forward(
-        block_parent, bc_pre, dt_raw, zx, conv_x, conv_bc, dt_bias, a_log, skip_l, gate_gain, sel
+        block_parent, bc_pre, dt_raw, zx, dgn, conv_x, conv_bc, dt_bias, a_log, skip_l, gate_gain, sel
     )
+    sums = side_start(join([sq[:, 0, :], sq[:, 8, :]]))
+    out = jnp.dot(gg, w_out, preferred_element_type=f32).astype(bf16)
+    sums = side_total((None if sums[0] is None else after(sums[0], out), sums[1]))
     gg_near = pair_up(gg, 1)
-    out, cross = run_output(gg, w_out, cotangent)
-    sums = side_total(side_start(join([sq[:, 0, :], cross[0].reshape(blocks, length)])))
     got_out = side_start(after(out, sums))
-    dgn = over_columns(after(cotangent, out), w_out).astype(bf16)
     squares, crosses = sums[:blocks], sums[blocks:]
     inv_gate = lax.rsqrt(squares / full + epsilon)
     scale = inv_gate.reshape(1, tokens)
@@ -1079,38 +1050,27 @@
     w_out_2 = add_send(order, w_out_1, near[1])
     dx_near = pair_up(dx, 1)
     got_bc = side_start(dbc)
-    low_1, gain_1 = run_input(dz, order.first(dx), dbc, ddt, w_cat, w_bc, w_dt_t, x_in, inv_rms, 0, step)
-    order.then(low_1)
-    got_low_1 = side_start(low_1)
+    low, low_gain = run_input(dz, order.first(dx), dbc, ddt, w_cat, w_bc, w_dt_t, x_in, inv_rms, 0, tokens)
+    order.then(low)
+    got_low = side_start(low)
+    order.wait(w_z_1[1])
     w_out_3 = add_send(order, w_out_2, near[2])
+    w_z_2 = add_send(order, w_z_1, near[1])
     got_bc = tuple(None if value is None else order.first(value) for value in got_bc)
     d_small = jnp.concatenate([side_total(got_bc).astype(bf16), ddt], axis=1)
     order.then(d_small)
     small_near = pair_up(d_small, 1)
-    order.wait(dx_near)
-    low_2, gain_2 = run_input(dz, order.first(dx), dbc, ddt, w_cat, w_bc, w_dt_t, x_in, inv_rms, 1, step)
-    order.then(low_2)
-    order.wait(small_near)
-    got_low_2 = side_start(low_2)
-    w_z_2 = add_send(order, w_z_1, near[1])
     edge = inner * 5 // 8 // 256 * 256
     pieces = run_grad(place_near, 0, turned, turned_near, [order.first(dx), dx_near], share, 0, edge, 2)
     order.then(pieces[1])
     sent_a = send_pieces(pieces, near[0])
-    w_out_grad = add_last(order, w_out_3, near[3:])
     pieces = run_grad(place_near, 0, turned, turned_near, [order.first(d_small), small_near], share, 0, small, 2)
     order.then(pieces[1])
     sent_s = send_pieces(pieces, near[0])
     pieces = run_grad(place_far, 0, turned, turned_near, [order.first(dx), dx_near], share, edge, inner - edge, 2)
     order.then(pieces[1])
-    w_z_3 = add_send(order, w_z_2, near[2])
-
-    def finish(part, got, into):
-        values = present(got)
-        values = [order.first(values[0])] + values[1:]
-        return order.then(
-            run_finish(values, x_in, cotangent, inv_rms, norm_gain, part * count, length, into)
-        )
+    w_out_grad = add_last(order, w_out_3, near[3:])
+    sent_b = send_pieces(pieces, far[0])
 
     def spread_rows(sent, bit):
         kept, got = sent
@@ -1118,14 +1078,12 @@
         return order.then(join([order.first(kept), got]))
 
     places_s = [0]
-    input_grad = finish(0, got_low_1, None)
-    sent_b = send_pieces(pieces, far[0])
     sent_a = add_send(order, sent_a, near[1])
     sent_s = add_send(order, sent_s, near[1])
+    w_z_3 = add_send(order, w_z_2, near[2])
     mixed = order.then(run_mixed(squares, order.first(x_in), present(got_out), full))
-    w_z_grad = add_last(order, w_z_3, near[3:])
-    gain_1, gain_2, gkbc, gskip, gkx, ghead, gg_grad = order.first((gain_1, gain_2, gkbc, gskip, gkx, ghead, gg_grad))
-    shared = jnp.concatenate([(gain_1 + gain_2).reshape(-1), gkbc.reshape(-1)])
+    low_gain, gkbc, gskip, gkx, ghead, gg_grad = order.first((low_gain, gkbc, gskip, gkx, ghead, gg_grad))
+    shared = jnp.concatenate([low_gain.reshape(-1), gkbc.reshape(-1)])
     d_skip_part = jnp.sum(gskip.reshape(heads, head_dim), axis=1)
     own = jnp.concatenate(
         [gkx.reshape(-1), ghead.reshape(-1), d_skip_part, gg_grad.reshape(-1)]
@@ -1144,8 +1102,7 @@
     sent_a = add_send(order, sent_a, near[2])
     sent_s = add_send(order, sent_s, near[2])
     packed = send_same(add_all(order, packed, f32), near[1])
-    order.wait(got_low_2[1])
-    input_grad = finish(1, got_low_2, input_grad)
+    w_z_grad = add_last(order, w_z_3, near[3:])
     w_s = add_last(order, sent_s, near[3:])
     rows_bc = send_same(w_s[:, :wide], near[2])
     sent_b = add_send(order, sent_b, far[2])
@@ -1157,6 +1114,10 @@
         packed = add_all(order, send_same(packed, bit), f32)
     got_shared = side_start(packed[: pad_shared // 128])
     rows_bc = send_same(spread_rows(rows_bc, near[1]), near[0])
+    values = present(got_low)
+    input_grad = order.then(
+        run_finish([order.first(values[0])] + values[1:], x_in, cotangent, inv_rms, norm_gain, length)
+    )
     w_x_b = add_last(order, sent_b, far[3:])
     rows_bc = spread_rows(rows_bc, near[0])
     for bit in near[3:]:

time: 464 us -> 463 us (level)
  waiting for transfers between devices: 39.9 us -> 64.3 us
  Pallas kernels: 285 us -> 264 us
  matrix products: 36.8 us -> 47.5 us
  starting transfers between devices: 46.3 us -> 37.1 us
    ppermute x29, waiting for transfers between devices: 39.9 us -> 64.3 us  [pair_up(): return lax.ppermute(value, 'dp', [(i, i ^ bit) for i in range(size)])]
    pallas_call x3 -> x1, Pallas kernels: 28.3 us -> 11.4 us  [run_finish(): pl.pallas_call(functools.partial(finish_kernel, len(values)), grid=(token...]
    dot_general x0 -> x1, matrix products: none -> 13.8 us  [local(): out = jnp.dot(gg, w_out, preferred_element_type=f32).astype(bf16)]
    ppermute x29, starting transfers between devices: 42 us -> 32.5 us  [pair_up(): return lax.ppermute(value, 'dp', [(i, i ^ bit) for i in range(size)])]
    pallas_call x2 -> x1, Pallas kernels: 33.5 us -> 27.3 us  [run_input(): pl.pallas_call(functools.partial(input_kernel, heads), grid=(features //...]
    unnamed x71 -> x83, local copies, waits for them, and re-layouts: 31.4 us -> 30.1 us
  transfers between devices with their start and end apart: 35 -> 34, of which waited for: 8 -> 6; matrix products, arithmetic and copies ran while one was open for 17% -> 17% of each run, Pallas kernels for 59% -> 55%
where the time goes in v2:
time: 463 us; the launch traced here: 460 us
  Pallas kernels  264 us (57%)
  waiting for transfers between devices  64.3 us (14%)
  matrix products  47.5 us (10%)
  local copies, waits for them, and re-layouts  37.8 us (8%)
  starting transfers between devices  37.1 us (8%)
  other arithmetic  8.89 us (2%)
    ppermute x29, waiting for transfers between devices, pair_up(): return lax.ppermute(value, 'dp', [(i, i ^ bit) for i in range(size)])  64.3 us
    pallas_call x5, Pallas kernels, run_grad(): pl.pallas_call(functools.partial(grad_kernel, share, which, len(rights),...  60.6 us
    pallas_call x1, Pallas kernels, run_backward(): pl.pallas_call(functools.partial(backward_kernel, sizes), grid_spec=grid_...  55 us
    pallas_call x19, Pallas kernels, run_add(): pl.pallas_call(functools.partial(add_kernel, len(values)), grid=(width //...  39.3 us
    pallas_call x1, Pallas kernels, run_forward(): pl.pallas_call(functools.partial(forward_kernel, sizes), grid_spec=grid_s...  34.4 us
    ppermute x29, starting transfers between devices, pair_up(): return lax.ppermute(value, 'dp', [(i, i ^ bit) for i in range(size)])  32.5 us
    unnamed x83, local copies, waits for them, and re-layouts  30.1 us
    pallas_call x1, Pallas kernels, run_input(): pl.pallas_call(functools.partial(input_kernel, heads), grid=(features //...  27.3 us
  transfers between devices with their start and end apart: 34, of which 6 were waited for; matrix products, arithmetic and copies ran while one was open for 17% of the time, Pallas kernels for 55%

profile of v2, /device:TPU:1, one launch (start us, length us, event | category | flops | bytes accessed | tf_op | source)
XLA Modules:
  0.0 460.5 jit_solution(13805782358380553816)
XLA Ops:
  0.6 11.7 %input_norm.1 = (bf16[1024,2048]{1,0:T(8,128)(2,1)}, bf16[2,2048,1024]{2,1,0:T(8,128)(2,1)}, f32[1024,1]{1,0:T(8,128)}, f32[1024,256]{1,0:T(8,128)}, f32[1024,32]{1,0:T(8,128)}) custom-call(bf16[1024,2048]{1,0:T(8,128)(2,1)} %x_ref.6, bf16[1024,2048]{1,0:T(8,128)(2,1)} %cot_ref.3, f32[1,2048]{1,0:T(1,128)} %bitcast.56, bf16[2048,256]{1,0:T(8,128)(2,1)} %wbc_ref.3, ...), custom_call_target="tpu_custom_call" | custom-call | flops 1000 | bytes 1000 | tf_op jit(solution)/shard_map/input_norm/pallas_call | solution.py:341
  12.5 12.3 %copy.40 = bf16[256,8,2,2048]{3,1,2,0:T(8,128)(2,1)S(1)} copy(bf16[256,8,2,2048]{3,2,1,0:T(2,128)(2,1)} %bitcast.45) | data formatting | bytes 33554432
  24.9 19.8 %convolution_convert_fusion.z_ref.xp_ref = bf16[1024,4096]{1,0:T(8,128)(2,1)} fusion(bf16[1024,2048]{1,0:T(8,128)(2,1)S(1)} %copy-done.32, bf16[2048,4096]{1,0:T(8,128)(2,1)S(1)} %bitcast.46), kind=kOutput, calls=%fused_computation.2 | convolution fusion | flops 17184063488 | bytes 29360128 | tf_op jit(solution)/shard_map/dot_general | solution.py:1016
  46.2 13.9 %convolution_convert_fusion.2.dgn_ref = bf16[1024,2048]{1,0:T(8,128)(2,1)} fusion(bf16[1024,2048]{1,0:T(8,128)(2,1)} %cot_ref.3, bf16[2048,2048]{1,0:T(8,128)(2,1)} %param.28), kind=kOutput, calls=%fused_computation.4 | convolution fusion | flops 8592031744 | bytes 16777216 | tf_op jit(solution)/shard_map/dot_general | solution.py:879
  60.0 34.4 %ssd_forward.1 = (bf16[1024,2048]{1,0:T(8,128)(2,1)}, bf16[1024,2048]{1,0:T(8,128)(2,1)}, bf16[1024,2048]{1,0:T(8,128)(2,1)}, bf16[1024,2048]{1,0:T(8,128)(2,1)}...) custom-call(s32[8]{0:T(128)} %par_ref.3, ...), custom_call_target="tpu_custom_call" | custom-call | flops 1000 | bytes 1000 | tf_op jit(solution)/shard_map/ssd_forward/pallas_call | solution.py:255
  98.4 13.8 %convolution_convert_fusion.1.refs_0_ = bf16[1024,2048]{1,0:T(8,128)(2,1)} fusion(bf16[1024,2048]{1,0:T(8,128)(2,1)} %get-tuple-element.121.rest_0_, bf16[2048,2048]{1,0:T(8,128)(2,1)} %param.28), kind=kOutput, calls=%fused_computation.3 | convolution fusion | flops 8592031744 | bytes 16777216 | tf_op jit(solution)/shard_map/dot_general | solution.py:1022
  112.8 14.5 %gate_backward.1 = (bf16[1024,2048]{1,0:T(8,128)(2,1)}, bf16[1024,2048]{1,0:T(8,128)(2,1)}, f32[1,2048]{1,0:T(1,128)}) custom-call(f32[8,128]{1,0:T(8,128)} %get-tuple-element.242.sq_ref, f32[8,128]{1,0:T(8,128)} %get-tuple-element.241.cross_ref, bf16[1024,2048]{1,0:T(8,128)(2,1)} %get-tuple-element.119.y_ref, ...), custom_call_target="tpu_custom_call" | custom-call | flops 1000 | bytes 1000 | tf_op jit(solution)/shard_map/gate_backward/pallas_call | solution.py:310
  128.6 5.4 %collective-permute-done.3 = f32[1,1024]{1,0:T(1,128)S(1)} collective-permute-done((f32[1,1024]{1,0:T(1,128)S(1)}, f32[1,1024]{1,0:T(1,128)S(1)}, u32[]{:S(2)}, u32[]{:S(2)}) %collective-permute-start.3) | collective-permute-done | bytes 4128 | tf_op jit(solution)/shard_map/ppermute | solution.py:907
  134.7 15.9 %weight_grad.5 = (bf16[512,2048]{1,0:T(8,128)(2,1)}, bf16[512,2048]{1,0:T(8,128)(2,1)}) custom-call(s32[8]{0:T(128)} %broadcast_xor_fusion.1.place_ref, bf16[2,2048,1024]{2,1,0:T(8,128)(2,1)} %get-tuple-element.118.mine_ref, bf16[2,2048,1024]{2,1,0:T(8,128)(2,1)} %collective-permute-done.1.theirs_ref, bf16[1024,2048]{1,0:T(8,128)(2,1)} %get-tuple-element.121.rest_0_, ...), custom_call_target="tpu_custom_call" | custom-call | flops 1000 | bytes 1000 | tf_op jit(solution)/shard_map/weight_grad/pallas_call | solution.py:431
  153.3 15.4 %weight_grad.6 = (bf16[512,2048]{1,0:T(8,128)(2,1)}, bf16[512,2048]{1,0:T(8,128)(2,1)}) custom-call(s32[8]{0:T(128)} %broadcast_xor_fusion.1.place_ref, bf16[2,2048,1024]{2,1,0:T(8,128)(2,1)} %get-tuple-element.118.mine_ref, bf16[2,2048,1024]{2,1,0:T(8,128)(2,1)} %collective-permute-done.1.theirs_ref, bf16[1024,2048]{1,0:T(8,128)(2,1)} %get-tuple-element.123.rest_0_.dz_ref, ...), custom_call_target="tpu_custom_call" | custom-call | flops 1000 | bytes 1000 | tf_op jit(solution)/shard_map/weight_grad/pallas_call | solution.py:431
  168.8 55.0 %ssd_backward.1 = (bf16[1024,2048]{1,0:T(8,128)(2,1)}, bf16[1024,256]{1,0:T(8,128)(2,1)}, bf16[1024,128]{1,0:T(8,128)(2,1)}, f32[5,2048]{1,0:T(8,128)}, f32[5,25...) custom-call(s32[8]{0:T(128)} %par_ref.3, bf16[1024,2048]{1,0:T(8,128)(2,1)} %get-tuple-element.126.dy_ref, ...), custom_call_target="tpu_custom_call" | custom-call | flops 1000 | bytes 1000 | tf_op jit(solution)/shard_map/ssd_backward/pallas_call | solution.py:776
  226.2 3.4 add_parts.19
  231.1 27.3 %input_grad.1 = (bf16[1024,2048]{1,0:T(8,128)(2,1)}, f32[1,2048]{1,0:T(1,128)}) custom-call(bf16[1024,2048]{1,0:T(8,128)(2,1)} %get-tuple-element.123.rest_0_.dz_ref, bf16[1024,2048]{1,0:T(8,128)(2,1)} %get-tuple-element.156.dx_ref.rest_0_, bf16[1024,256]{1,0:T(8,128)(2,1)} %get-tuple-element.148.dbc_ref, bf16[1024,128]{1,0:T(8,128)(2,1)} %get-tuple-element.139.ddt_ref, ...), custom_call_target="tpu_custom_call" | custom-call | flops 24299999232 | bytes 1000 | tf_op jit(solution)/shard_map/input_grad/pallas_call | solution.py:466
  259.6 12.6 %collective-permute-done.7.refs_1_ = bf16[512,2048]{1,0:T(8,128)(2,1)} collective-permute-done((bf16[512,2048]{1,0:T(8,128)(2,1)}, bf16[512,2048]{1,0:T(8,128)(2,1)}, u32[]{:S(2)}, u32[]{:S(2)}) %collective-permute-start.7) | collective-permute-done | bytes 2097184 | tf_op jit(solution)/shard_map/ppermute | solution.py:907
  279.2 11.6 %weight_grad.7 = (bf16[512,1280]{1,0:T(8,128)(2,1)}, bf16[512,1280]{1,0:T(8,128)(2,1)}) custom-call(s32[8]{0:T(128)} %broadcast_xor_fusion.1.place_ref, bf16[2,2048,1024]{2,1,0:T(8,128)(2,1)} %get-tuple-element.118.mine_ref, bf16[2,2048,1024]{2,1,0:T(8,128)(2,1)} %collective-permute-done.1.theirs_ref, bf16[1024,2048]{1,0:T(8,128)(2,1)} %get-tuple-element.156.dx_ref.rest_0_, ...), custom_call_target="tpu_custom_call" | custom-call | flops 1000 | bytes 1000 | tf_op jit(solution)/shard_map/weight_grad/pallas_call | solution.py:431
  297.0 8.8 %weight_grad.8 = (bf16[512,384]{1,0:T(8,128)(2,1)}, bf16[512,384]{1,0:T(8,128)(2,1)}) custom-call(s32[8]{0:T(128)} %broadcast_xor_fusion.1.place_ref, bf16[2,2048,1024]{2,1,0:T(8,128)(2,1)} %get-tuple-element.118.mine_ref, bf16[2,2048,1024]{2,1,0:T(8,128)(2,1)} %collective-permute-done.1.theirs_ref, bf16[1024,384]{1,0:T(8,128)(2,1)} %copy-done.2, ...), custom_call_target="tpu_custom_call" | custom-call | flops 1000 | bytes 1000 | tf_op jit(solution)/shard_map/weight_grad/pallas_call | solution.py:431
  307.1 8.8 %weight_grad.9 = (bf16[512,768]{1,0:T(8,128)(2,1)}, bf16[512,768]{1,0:T(8,128)(2,1)}) custom-call(s32[8]{0:T(128)} %broadcast_xor_fusion.place_ref, bf16[2,2048,1024]{2,1,0:T(8,128)(2,1)} %get-tuple-element.118.mine_ref, bf16[2,2048,1024]{2,1,0:T(8,128)(2,1)} %collective-permute-done.1.theirs_ref, bf16[1024,2048]{1,0:T(8,128)(2,1)} %get-tuple-element.156.dx_ref.rest_0_, ...), custom_call_target="tpu_custom_call" | custom-call | flops 1000 | bytes 1000 | tf_op jit(solution)/shard_map/weight_grad/pallas_call | solution.py:431
  315.9 11.7 %collective-permute-done.12.refs_1_ = bf16[128,2048]{1,0:T(8,128)(2,1)} collective-permute-done((bf16[128,2048]{1,0:T(8,128)(2,1)}, bf16[128,2048]{1,0:T(8,128)(2,1)}, u32[]{:S(2)}, u32[]{:S(2)}) %collective-permute-start.12) | collective-permute-done | bytes 524320 | tf_op jit(solution)/shard_map/ppermute | solution.py:907
  342.8 9.5 %layer_output.1 = bf16[1024,2048]{1,0:T(8,128)(2,1)} custom-call(f32[8,128]{1,0:T(8,128)} %get-tuple-element.242.sq_ref, bf16[1024,2048]{1,0:T(8,128)(2,1)} %x_ref.6, bf16[1024,2048]{1,0:T(8,128)(2,1)} %convolution_convert_fusion.1.refs_0_, bf16[1024,2048]{1,0:T(8,128)(2,1)} %collective-permute-done.5.refs_1_), custom_call_target="tpu_custom_call" | custom-call | flops 1000 | bytes 1000 | tf_op jit(solution)/shard_map/layer_output/pallas_call | solution.py:839
  367.8 3.5 collective-permute-done.19.refs_1_
  379.8 16.2 %collective-permute-done.21.refs_1_ = bf16[128,2048]{1,0:T(8,128)(2,1)S(1)} collective-permute-done((bf16[128,2048]{1,0:T(8,128)(2,1)}, bf16[128,2048]{1,0:T(8,128)(2,1)S(1)}, u32[]{:S(2)}, u32[]{:S(2)}) %collective-permute-start.21) | collective-permute-done | bytes 524320 | tf_op jit(solution)/shard_map/ppermute | solution.py:907
  398.8 14.8 %collective-permute-done.22.refs_1_ = bf16[128,384]{1,0:T(8,128)(2,1)S(1)} collective-permute-done((bf16[128,384]{1,0:T(8,128)(2,1)}, bf16[128,384]{1,0:T(8,128)(2,1)S(1)}, u32[]{:S(2)}, u32[]{:S(2)}) %collective-permute-start.22) | collective-permute-done | bytes 98336 | tf_op jit(solution)/shard_map/ppermute | solution.py:907
  431.8 11.4 %input_grad_finish.1 = bf16[1024,2048]{1,0:T(8,128)(2,1)} custom-call(bf16[1024,2048]{1,0:T(8,128)(2,1)} %x_ref.6, bf16[1024,2048]{1,0:T(8,128)(2,1)} %cot_ref.3, f32[1024,1]{1,0:T(8,128)} %get-tuple-element.140.inv_ref, f32[1,2048]{1,0:T(1,128)} %bitcast.57, bf16[1024,2048]{1,0:T(8,128)(2,1)} %get-tuple-element.204.refs_0_, ...), custom_call_target="tpu_custom_call" | custom-call | flops 1000 | bytes 1000 | tf_op jit(solution)/shard_map/input_grad_finish/pallas_call | solution.py:865
  447.2 4.9 %collective-permute-start.33 = (bf16[1024,256]{1,0:T(8,128)(2,1)S(1)}, bf16[1024,256]{1,0:T(8,128)(2,1)S(1)}, u32[]{:S(2)}, u32[]{:S(2)}) collective-permute-start(bf16[1024,256]{1,0:T(8,128)(2,1)S(1)} %constant_dynamic-update-slice_fusion.4), channel_id=1, source_target_pairs={{0,2},{2,0},{4,6},{6,4},{8,10},{10,8},{12,14},{14,12},{16,18},{18,... | collective-permute-start | bytes 1572872 | tf_op jit(solution)/shard_map/ppermute | solution.py:907
  (218 shorter events, 102.6 us)
Async XLA Ops:
  12.4 122.3 %collective-permute-start.1 = (bf16[2,2048,1024]{2,1,0:T(8,128)(2,1)}, bf16[2,2048,1024]{2,1,0:T(8,128)(2,1)}, u32[]{:S(2)}, u32[]{:S(2)}) collective-permute-start(bf16[2,2048,1024]{2,1,0:T(8,128)(2,1)} %get-tuple-element.118.mine_ref), channel_id=1, source_target_pairs={{0,2},{2,0},{4,6},{6,4},{8,10},{10,8},{12,14},{14,12},{16,18},{18,... | collective-permute-start | bytes 25165832 | tf_op jit(solution)/shard_map/ppermute | solution.py:907
  95.3 16.9 %collective-permute-start = (f32[16,128]{1,0:T(8,128)S(1)}, f32[16,128]{1,0:T(8,128)S(1)}, u32[]{:S(2)}, u32[]{:S(2)}) collective-permute-start(f32[16,128]{1,0:T(8,128)S(1)} %pad_maximum_fusion.3), channel_id=1, source_target_pairs={{0,1},{1,0},{2,3},{3,2},{4,5},{5,4},{6,7},{7,6},{8,9},{9,8},{10,11... | collective-permute-start | bytes 24584 | tf_op jit(solution)/shard_map/ppermute | solution.py:887
  98.1 36.6 %collective-permute-start.2 = (bf16[1024,2048]{1,0:T(8,128)(2,1)}, bf16[1024,2048]{1,0:T(8,128)(2,1)}, u32[]{:S(2)}, u32[]{:S(2)}) collective-permute-start(bf16[1024,2048]{1,0:T(8,128)(2,1)} %get-tuple-element.121.rest_0_), channel_id=1, source_target_pairs={{0,2},{2,0},{4,6},{6,4},{8,10},{10,8},{12,14},{14,12},{16,18},{18,... | collective-permute-start | bytes 12582920 | tf_op jit(solution)/shard_map/ppermute | solution.py:907
  127.4 26.0 %collective-permute-start.4 = (bf16[1024,2048]{1,0:T(8,128)(2,1)}, bf16[1024,2048]{1,0:T(8,128)(2,1)}, u32[]{:S(2)}, u32[]{:S(2)}) collective-permute-start(bf16[1024,2048]{1,0:T(8,128)(2,1)} %get-tuple-element.123.rest_0_.dz_ref), channel_id=1, source_target_pairs={{0,2},{2,0},{4,6},{6,4},{8,10},{10,8},{12,14},{14,12},{16,18},{18,... | collective-permute-start | bytes 12582920 | tf_op jit(solution)/shard_map/ppermute | solution.py:907
  127.6 97.3 %collective-permute-start.5 = (bf16[1024,2048]{1,0:T(8,128)(2,1)}, bf16[1024,2048]{1,0:T(8,128)(2,1)}, u32[]{:S(2)}, u32[]{:S(2)}) collective-permute-start(bf16[1024,2048]{1,0:T(8,128)(2,1)} %convolution_convert_fusion.1.refs_0_), channel_id=1, source_target_pairs={{0,1},{1,0},{2,3},{3,2},{4,5},{5,4},{6,7},{7,6},{8,9},{9,8},{10,11... | collective-permute-start | bytes 12582920 | tf_op jit(solution)/shard_map/ppermute | solution.py:887
  150.6 74.2 %collective-permute-start.6 = (bf16[512,2048]{1,0:T(8,128)(2,1)}, bf16[512,2048]{1,0:T(8,128)(2,1)S(1)}, u32[]{:S(2)}, u32[]{:S(2)}) collective-permute-start(bf16[512,2048]{1,0:T(8,128)(2,1)} %get-tuple-element.134), channel_id=1, source_target_pairs={{0,4},{2,6},{4,0},{6,2},{8,12},{10,14},{12,8},{14,10},{16,20},{18,... | collective-permute-start | bytes 6291464 | tf_op jit(solution)/shard_map/ppermute | solution.py:907
  223.8 55.4 %collective-permute-start.10 = (bf16[1024,2048]{1,0:T(8,128)(2,1)}, bf16[1024,2048]{1,0:T(8,128)(2,1)}, u32[]{:S(2)}, u32[]{:S(2)}) collective-permute-start(bf16[1024,2048]{1,0:T(8,128)(2,1)} %get-tuple-element.156.dx_ref.rest_0_), channel_id=1, source_target_pairs={{0,2},{2,0},{4,6},{6,4},{8,10},{10,8},{12,14},{14,12},{16,18},{18,... | collective-permute-start | bytes 12582920 | tf_op jit(solution)/shard_map/ppermute | solution.py:907
  224.7 47.5 %collective-permute-start.7 = (bf16[512,2048]{1,0:T(8,128)(2,1)}, bf16[512,2048]{1,0:T(8,128)(2,1)}, u32[]{:S(2)}, u32[]{:S(2)}) collective-permute-start(bf16[512,2048]{1,0:T(8,128)(2,1)} %get-tuple-element.142), channel_id=1, source_target_pairs={{0,4},{2,6},{4,0},{6,2},{8,12},{10,14},{12,8},{14,10},{16,20},{18,... | collective-permute-start | bytes 6291464 | tf_op jit(solution)/shard_map/ppermute | solution.py:907
  224.7 54.2 %collective-permute-start.9 = (bf16[1024,256]{1,0:T(8,128)(2,1)}, bf16[1024,256]{1,0:T(8,128)(2,1)S(1)}, u32[]{:S(2)}, u32[]{:S(2)}) collective-permute-start(bf16[1024,256]{1,0:T(8,128)(2,1)} %get-tuple-element.148.dbc_ref), channel_id=1, source_target_pairs={{0,1},{1,0},{2,3},{3,2},{4,5},{5,4},{6,7},{7,6},{8,9},{9,8},{10,11... | collective-permute-start | bytes 1572872 | tf_op jit(solution)/shard_map/ppermute | solution.py:887
  229.6 42.6 %collective-permute-start.8 = (bf16[256,2048]{1,0:T(8,128)(2,1)}, bf16[256,2048]{1,0:T(8,128)(2,1)S(1)}, u32[]{:S(2)}, u32[]{:S(2)}) collective-permute-start(bf16[256,2048]{1,0:T(8,128)(2,1)} %get-tuple-element.144), channel_id=1, source_target_pairs={{0,8},{2,10},{4,12},{6,14},{8,0},{10,2},{12,4},{14,6},{16,24},{18,... | collective-permute-start | bytes 3145736 | tf_op jit(solution)/shard_map/ppermute | solution.py:907
  258.4 173.5 %collective-permute-start.29 = (bf16[1024,2048]{1,0:T(8,128)(2,1)}, bf16[1024,2048]{1,0:T(8,128)(2,1)}, u32[]{:S(2)}, u32[]{:S(2)}) collective-permute-start(bf16[1024,2048]{1,0:T(8,128)(2,1)} %get-tuple-element.204.refs_0_), channel_id=1, source_target_pairs={{0,1},{1,0},{2,3},{3,2},{4,5},{5,4},{6,7},{7,6},{8,9},{9,8},{10,11... | collective-permute-start | bytes 12582920 | tf_op jit(solution)/shard_map/ppermute | solution.py:887
  290.8 42.1 %collective-permute-start.13 = (bf16[512,1280]{1,0:T(8,128)(2,1)}, bf16[512,1280]{1,0:T(8,128)(2,1)S(1)}, u32[]{:S(2)}, u32[]{:S(2)}) collective-permute-start(bf16[512,1280]{1,0:T(8,128)(2,1)} %get-tuple-element.151), channel_id=1, source_target_pairs={{0,4},{2,6},{4,0},{6,2},{8,12},{10,14},{12,8},{14,10},{16,20},{18,... | collective-permute-start | bytes 3932168 | tf_op jit(solution)/shard_map/ppermute | solution.py:907
  292.0 47.4 %collective-permute-start.15 = (bf16[256,2048]{1,0:T(8,128)(2,1)}, bf16[256,2048]{1,0:T(8,128)(2,1)S(1)}, u32[]{:S(2)}, u32[]{:S(2)}) collective-permute-start(bf16[256,2048]{1,0:T(8,128)(2,1)} %get-tuple-element.165), channel_id=1, source_target_pairs={{0,8},{2,10},{4,12},{6,14},{8,0},{10,2},{12,4},{14,6},{16,24},{18,... | collective-permute-start | bytes 3145736 | tf_op jit(solution)/shard_map/ppermute | solution.py:907
  293.5 34.1 %collective-permute-start.12 = (bf16[128,2048]{1,0:T(8,128)(2,1)}, bf16[128,2048]{1,0:T(8,128)(2,1)}, u32[]{:S(2)}, u32[]{:S(2)}) collective-permute-start(bf16[128,2048]{1,0:T(8,128)(2,1)} %get-tuple-element.159), channel_id=1, source_target_pairs={{0,16},{2,18},{4,20},{6,22},{8,24},{10,26},{12,28},{14,30},{16,0},... | collective-permute-start | bytes 1572872 | tf_op jit(solution)/shard_map/ppermute | solution.py:907
  305.8 30.9 %collective-permute-start.14 = (bf16[512,384]{1,0:T(8,128)(2,1)}, bf16[512,384]{1,0:T(8,128)(2,1)S(1)}, u32[]{:S(2)}, u32[]{:S(2)}) collective-permute-start(bf16[512,384]{1,0:T(8,128)(2,1)} %get-tuple-element.155), channel_id=1, source_target_pairs={{0,4},{2,6},{4,0},{6,2},{8,12},{10,14},{12,8},{14,10},{16,20},{18,... | collective-permute-start | bytes 1179656 | tf_op jit(solution)/shard_map/ppermute | solution.py:907
  327.7 29.2 %collective-permute-start.16 = (bf16[512,768]{1,0:T(8,128)(2,1)}, bf16[512,768]{1,0:T(8,128)(2,1)S(1)}, u32[]{:S(2)}, u32[]{:S(2)}) collective-permute-start(bf16[512,768]{1,0:T(8,128)(2,1)} %get-tuple-element.157), channel_id=1, source_target_pairs={{0,8},{2,10},{4,12},{6,14},{8,0},{10,2},{12,4},{14,6},{16,24},{18,... | collective-permute-start | bytes 2359304 | tf_op jit(solution)/shard_map/ppermute | solution.py:907
  336.6 26.7 %collective-permute-start.18 = (bf16[256,1280]{1,0:T(8,128)(2,1)}, bf16[256,1280]{1,0:T(8,128)(2,1)}, u32[]{:S(2)}, u32[]{:S(2)}) collective-permute-start(bf16[256,1280]{1,0:T(8,128)(2,1)} %get-tuple-element.185), channel_id=1, source_target_pairs={{0,8},{2,10},{4,12},{6,14},{8,0},{10,2},{12,4},{14,6},{16,24},{18,... | collective-permute-start | bytes 1966088 | tf_op jit(solution)/shard_map/ppermute | solution.py:907
  355.1 16.2 %collective-permute-start.19 = (bf16[256,384]{1,0:T(8,128)(2,1)S(1)}, bf16[256,384]{1,0:T(8,128)(2,1)S(1)}, u32[]{:S(2)}, u32[]{:S(2)}) collective-permute-start(bf16[256,384]{1,0:T(8,128)(2,1)S(1)} %copy-done.34), channel_id=1, source_target_pairs={{0,8},{2,10},{4,12},{6,14},{8,0},{10,2},{12,4},{14,6},{16,24},{18,... | collective-permute-start | bytes 589832 | tf_op jit(solution)/shard_map/ppermute | solution.py:907
  359.9 36.1 %collective-permute-start.21 = (bf16[128,2048]{1,0:T(8,128)(2,1)}, bf16[128,2048]{1,0:T(8,128)(2,1)S(1)}, u32[]{:S(2)}, u32[]{:S(2)}) collective-permute-start(bf16[128,2048]{1,0:T(8,128)(2,1)} %get-tuple-element.192), channel_id=1, source_target_pairs={{0,16},{2,18},{4,20},{6,22},{8,24},{10,26},{12,28},{14,30},{16,0},... | collective-permute-start | bytes 1572872 | tf_op jit(solution)/shard_map/ppermute | solution.py:907
  363.4 52.5 %collective-permute-start.23 = (bf16[256,768]{1,0:T(8,128)(2,1)}, bf16[256,768]{1,0:T(8,128)(2,1)S(1)}, u32[]{:S(2)}, u32[]{:S(2)}) collective-permute-start(bf16[256,768]{1,0:T(8,128)(2,1)} %get-tuple-element.196), channel_id=1, source_target_pairs={{0,16},{2,18},{4,20},{6,22},{8,24},{10,26},{12,28},{14,30},{16,0},... | collective-permute-start | bytes 1179656 | tf_op jit(solution)/shard_map/ppermute | solution.py:907
  373.7 39.9 %collective-permute-start.22 = (bf16[128,384]{1,0:T(8,128)(2,1)}, bf16[128,384]{1,0:T(8,128)(2,1)S(1)}, u32[]{:S(2)}, u32[]{:S(2)}) collective-permute-start(bf16[128,384]{1,0:T(8,128)(2,1)} %get-tuple-element.194), channel_id=1, source_target_pairs={{0,16},{2,18},{4,20},{6,22},{8,24},{10,26},{12,28},{14,30},{16,0},... | collective-permute-start | bytes 294920 | tf_op jit(solution)/shard_map/ppermute | solution.py:907
  376.2 43.2 %collective-permute-start.24 = (f32[136,128]{1,0:T(8,128)}, f32[136,128]{1,0:T(8,128)S(1)}, u32[]{:S(2)}, u32[]{:S(2)}) collective-permute-start(f32[136,128]{1,0:T(8,128)} %add_parts.30.refs_0_), channel_id=1, source_target_pairs={{0,8},{2,10},{4,12},{6,14},{8,0},{10,2},{12,4},{14,6},{16,24},{18,... | collective-permute-start | bytes 208904 | tf_op jit(solution)/shard_map/ppermute | solution.py:907
  398.8 27.9 %collective-permute-start.26 = (bf16[128,1280]{1,0:T(8,128)(2,1)S(1)}, bf16[128,1280]{1,0:T(8,128)(2,1)S(1)}, u32[]{:S(2)}, u32[]{:S(2)}) collective-permute-start(bf16[128,1280]{1,0:T(8,128)(2,1)S(1)} %copy-done.33), channel_id=1, source_target_pairs={{0,16},{2,18},{4,20},{6,22},{8,24},{10,26},{12,28},{14,30},{16,0},... | collective-permute-start | bytes 983048 | tf_op jit(solution)/shard_map/ppermute | solution.py:907
  424.8 18.4 %collective-permute-start.31 = (bf16[128,768]{1,0:T(8,128)(2,1)}, bf16[128,768]{1,0:T(8,128)(2,1)S(1)}, u32[]{:S(2)}, u32[]{:S(2)}) collective-permute-start(bf16[128,768]{1,0:T(8,128)(2,1)} %get-tuple-element.206), channel_id=1, source_target_pairs={{0,4},{2,6},{4,0},{6,2},{8,12},{10,14},{12,8},{14,10},{16,20},{18,... | collective-permute-start | bytes 589832 | tf_op jit(solution)/shard_map/ppermute | solution.py:907
  (49 other events, 446.1 us)

commit v3 on v2

--- a/solution.py
+++ b/solution.py
@@ -1053,9 +1053,7 @@
     low, low_gain = run_input(dz, order.first(dx), dbc, ddt, w_cat, w_bc, w_dt_t, x_in, inv_rms, 0, tokens)
     order.then(low)
     got_low = side_start(low)
-    order.wait(w_z_1[1])
     w_out_3 = add_send(order, w_out_2, near[2])
-    w_z_2 = add_send(order, w_z_1, near[1])
     got_bc = tuple(None if value is None else order.first(value) for value in got_bc)
     d_small = jnp.concatenate([side_total(got_bc).astype(bf16), ddt], axis=1)
     order.then(d_small)
@@ -1063,6 +1061,7 @@
     edge = inner * 5 // 8 // 256 * 256
     pieces = run_grad(place_near, 0, turned, turned_near, [order.first(dx), dx_near], share, 0, edge, 2)
     order.then(pieces[1])
+    w_z_2 = add_send(order, w_z_1, near[1])
     sent_a = send_pieces(pieces, near[0])
     pieces = run_grad(place_near, 0, turned, turned_near, [order.first(d_small), small_near], share, 0, small, 2)
     order.then(pieces[1])

time: 463 us -> 453 us (0.978)
  waiting for transfers between devices: 64.3 us -> 53.3 us
    ppermute x29, waiting for transfers between devices: 64.3 us -> 53.3 us  [pair_up(): return lax.ppermute(value, 'dp', [(i, i ^ bit) for i in range(size)])]
  transfers between devices with their start and end apart: 34 -> 34, of which waited for: 6 -> 6; matrix products, arithmetic and copies ran while one was open for 17% -> 18% of each run, Pallas kernels for 55% -> 56%
where the time goes in v3:
time: 453 us; the launch traced here: 450 us
  Pallas kernels  264 us (58%)
  waiting for transfers between devices  53.3 us (12%)
  matrix products  47.5 us (10%)
  local copies, waits for them, and re-layouts  36.8 us (8%)
  starting transfers between devices  36.5 us (8%)
  other arithmetic  10.9 us (2%)
    pallas_call x5, Pallas kernels, run_grad(): pl.pallas_call(functools.partial(grad_kernel, share, which, len(rights),...  60.7 us
    pallas_call x1, Pallas kernels, run_backward(): pl.pallas_call(functools.partial(backward_kernel, sizes), grid_spec=grid_...  55.1 us
    ppermute x29, waiting for transfers between devices, pair_up(): return lax.ppermute(value, 'dp', [(i, i ^ bit) for i in range(size)])  53.3 us
    pallas_call x19, Pallas kernels, run_add(): pl.pallas_call(functools.partial(add_kernel, len(values)), grid=(width //...  39.3 us
    pallas_call x1, Pallas kernels, run_forward(): pl.pallas_call(functools.partial(forward_kernel, sizes), grid_spec=grid_s...  34.4 us
    ppermute x29, starting transfers between devices, pair_up(): return lax.ppermute(value, 'dp', [(i, i ^ bit) for i in range(size)])  31.8 us
    unnamed x83, local copies, waits for them, and re-layouts  29.1 us
    pallas_call x1, Pallas kernels, run_input(): pl.pallas_call(functools.partial(input_kernel, heads), grid=(features //...  27.2 us
  transfers between devices with their start and end apart: 34, of which 6 were waited for; matrix products, arithmetic and copies ran while one was open for 18% of the time, Pallas kernels for 56%

profile of v3, /device:TPU:1, one launch (start us, length us, event | category | flops | bytes accessed | tf_op | source)
XLA Modules:
  0.0 450.1 jit_solution(14909933036885787309)
XLA Ops:
  0.6 11.7 %input_norm.1 = (bf16[1024,2048]{1,0:T(8,128)(2,1)}, bf16[2,2048,1024]{2,1,0:T(8,128)(2,1)}, f32[1024,1]{1,0:T(8,128)}, f32[1024,256]{1,0:T(8,128)}, f32[1024,32]{1,0:T(8,128)}) custom-call(bf16[1024,2048]{1,0:T(8,128)(2,1)} %x_ref.6, bf16[1024,2048]{1,0:T(8,128)(2,1)} %cot_ref.3, f32[1,2048]{1,0:T(1,128)} %bitcast.56, bf16[2048,256]{1,0:T(8,128)(2,1)} %wbc_ref.3, ...), custom_call_target="tpu_custom_call" | custom-call | flops 1000 | bytes 1000 | tf_op jit(solution)/shard_map/input_norm/pallas_call | solution.py:341
  12.5 12.3 %copy.40 = bf16[256,8,2,2048]{3,1,2,0:T(8,128)(2,1)S(1)} copy(bf16[256,8,2,2048]{3,2,1,0:T(2,128)(2,1)} %bitcast.45) | data formatting | bytes 33554432
  24.9 19.8 %convolution_convert_fusion.z_ref.xp_ref = bf16[1024,4096]{1,0:T(8,128)(2,1)} fusion(bf16[1024,2048]{1,0:T(8,128)(2,1)S(1)} %copy-done.32, bf16[2048,4096]{1,0:T(8,128)(2,1)S(1)} %bitcast.46), kind=kOutput, calls=%fused_computation.2 | convolution fusion | flops 17184063488 | bytes 29360128 | tf_op jit(solution)/shard_map/dot_general | solution.py:1016
  46.2 13.9 %convolution_convert_fusion.2.dgn_ref = bf16[1024,2048]{1,0:T(8,128)(2,1)} fusion(bf16[1024,2048]{1,0:T(8,128)(2,1)} %cot_ref.3, bf16[2048,2048]{1,0:T(8,128)(2,1)} %param.28), kind=kOutput, calls=%fused_computation.4 | convolution fusion | flops 8592031744 | bytes 16777216 | tf_op jit(solution)/shard_map/dot_general | solution.py:879
  60.0 34.4 %ssd_forward.1 = (bf16[1024,2048]{1,0:T(8,128)(2,1)}, bf16[1024,2048]{1,0:T(8,128)(2,1)}, bf16[1024,2048]{1,0:T(8,128)(2,1)}, bf16[1024,2048]{1,0:T(8,128)(2,1)}...) custom-call(s32[8]{0:T(128)} %par_ref.3, ...), custom_call_target="tpu_custom_call" | custom-call | flops 1000 | bytes 1000 | tf_op jit(solution)/shard_map/ssd_forward/pallas_call | solution.py:255
  98.4 13.8 %convolution_convert_fusion.1.refs_0_ = bf16[1024,2048]{1,0:T(8,128)(2,1)} fusion(bf16[1024,2048]{1,0:T(8,128)(2,1)} %get-tuple-element.121.rest_0_, bf16[2048,2048]{1,0:T(8,128)(2,1)} %param.28), kind=kOutput, calls=%fused_computation.3 | convolution fusion | flops 8592031744 | bytes 16777216 | tf_op jit(solution)/shard_map/dot_general | solution.py:1022
  112.8 14.5 %gate_backward.1 = (bf16[1024,2048]{1,0:T(8,128)(2,1)}, bf16[1024,2048]{1,0:T(8,128)(2,1)}, f32[1,2048]{1,0:T(1,128)}) custom-call(f32[8,128]{1,0:T(8,128)} %get-tuple-element.242.sq_ref, f32[8,128]{1,0:T(8,128)} %get-tuple-element.241.cross_ref, bf16[1024,2048]{1,0:T(8,128)(2,1)} %get-tuple-element.119.y_ref, ...), custom_call_target="tpu_custom_call" | custom-call | flops 1000 | bytes 1000 | tf_op jit(solution)/shard_map/gate_backward/pallas_call | solution.py:310
  128.7 5.4 %collective-permute-done.3 = f32[1,1024]{1,0:T(1,128)S(1)} collective-permute-done((f32[1,1024]{1,0:T(1,128)S(1)}, f32[1,1024]{1,0:T(1,128)S(1)}, u32[]{:S(2)}, u32[]{:S(2)}) %collective-permute-start.3) | collective-permute-done | bytes 4128 | tf_op jit(solution)/shard_map/ppermute | solution.py:907
  134.7 15.9 %weight_grad.5 = (bf16[512,2048]{1,0:T(8,128)(2,1)}, bf16[512,2048]{1,0:T(8,128)(2,1)}) custom-call(s32[8]{0:T(128)} %broadcast_xor_fusion.1.place_ref, bf16[2,2048,1024]{2,1,0:T(8,128)(2,1)} %get-tuple-element.118.mine_ref, bf16[2,2048,1024]{2,1,0:T(8,128)(2,1)} %collective-permute-done.1.theirs_ref, bf16[1024,2048]{1,0:T(8,128)(2,1)} %get-tuple-element.121.rest_0_, ...), custom_call_target="tpu_custom_call" | custom-call | flops 1000 | bytes 1000 | tf_op jit(solution)/shard_map/weight_grad/pallas_call | solution.py:431
  153.4 15.4 %weight_grad.6 = (bf16[512,2048]{1,0:T(8,128)(2,1)}, bf16[512,2048]{1,0:T(8,128)(2,1)}) custom-call(s32[8]{0:T(128)} %broadcast_xor_fusion.1.place_ref, bf16[2,2048,1024]{2,1,0:T(8,128)(2,1)} %get-tuple-element.118.mine_ref, bf16[2,2048,1024]{2,1,0:T(8,128)(2,1)} %collective-permute-done.1.theirs_ref, bf16[1024,2048]{1,0:T(8,128)(2,1)} %get-tuple-element.123.rest_0_.dz_ref, ...), custom_call_target="tpu_custom_call" | custom-call | flops 1000 | bytes 1000 | tf_op jit(solution)/shard_map/weight_grad/pallas_call | solution.py:431
  168.8 55.1 %ssd_backward.1 = (bf16[1024,2048]{1,0:T(8,128)(2,1)}, bf16[1024,256]{1,0:T(8,128)(2,1)}, bf16[1024,128]{1,0:T(8,128)(2,1)}, f32[5,2048]{1,0:T(8,128)}, f32[5,25...) custom-call(s32[8]{0:T(128)} %par_ref.3, bf16[1024,2048]{1,0:T(8,128)(2,1)} %get-tuple-element.126.dy_ref, ...), custom_call_target="tpu_custom_call" | custom-call | flops 1000 | bytes 1000 | tf_op jit(solution)/shard_map/ssd_backward/pallas_call | solution.py:776
  225.0 3.4 add_parts.19
  229.7 27.2 %input_grad.1 = (bf16[1024,2048]{1,0:T(8,128)(2,1)}, f32[1,2048]{1,0:T(1,128)}) custom-call(bf16[1024,2048]{1,0:T(8,128)(2,1)} %get-tuple-element.123.rest_0_.dz_ref, bf16[1024,2048]{1,0:T(8,128)(2,1)} %get-tuple-element.156.dx_ref.rest_0_, bf16[1024,256]{1,0:T(8,128)(2,1)} %get-tuple-element.145.dbc_ref, bf16[1024,128]{1,0:T(8,128)(2,1)} %get-tuple-element.139.ddt_ref, ...), custom_call_target="tpu_custom_call" | custom-call | flops 24299999232 | bytes 1000 | tf_op jit(solution)/shard_map/input_grad/pallas_call | solution.py:466
  263.8 11.7 %weight_grad.7 = (bf16[512,1280]{1,0:T(8,128)(2,1)}, bf16[512,1280]{1,0:T(8,128)(2,1)}) custom-call(s32[8]{0:T(128)} %broadcast_xor_fusion.1.place_ref, bf16[2,2048,1024]{2,1,0:T(8,128)(2,1)} %get-tuple-element.118.mine_ref, bf16[2,2048,1024]{2,1,0:T(8,128)(2,1)} %collective-permute-done.1.theirs_ref, bf16[1024,2048]{1,0:T(8,128)(2,1)} %get-tuple-element.156.dx_ref.rest_0_, ...), custom_call_target="tpu_custom_call" | custom-call | flops 1000 | bytes 1000 | tf_op jit(solution)/shard_map/weight_grad/pallas_call | solution.py:431
  286.7 8.8 %weight_grad.8 = (bf16[512,384]{1,0:T(8,128)(2,1)}, bf16[512,384]{1,0:T(8,128)(2,1)}) custom-call(s32[8]{0:T(128)} %broadcast_xor_fusion.1.place_ref, bf16[2,2048,1024]{2,1,0:T(8,128)(2,1)} %get-tuple-element.118.mine_ref, bf16[2,2048,1024]{2,1,0:T(8,128)(2,1)} %collective-permute-done.1.theirs_ref, bf16[1024,384]{1,0:T(8,128)(2,1)} %copy-done.2, ...), custom_call_target="tpu_custom_call" | custom-call | flops 1000 | bytes 1000 | tf_op jit(solution)/shard_map/weight_grad/pallas_call | solution.py:431
  295.9 8.8 %weight_grad.9 = (bf16[512,768]{1,0:T(8,128)(2,1)}, bf16[512,768]{1,0:T(8,128)(2,1)}) custom-call(s32[8]{0:T(128)} %broadcast_xor_fusion.place_ref, bf16[2,2048,1024]{2,1,0:T(8,128)(2,1)} %get-tuple-element.118.mine_ref, bf16[2,2048,1024]{2,1,0:T(8,128)(2,1)} %collective-permute-done.1.theirs_ref, bf16[1024,2048]{1,0:T(8,128)(2,1)} %get-tuple-element.156.dx_ref.rest_0_, ...), custom_call_target="tpu_custom_call" | custom-call | flops 1000 | bytes 1000 | tf_op jit(solution)/shard_map/weight_grad/pallas_call | solution.py:431
  304.7 12.5 %collective-permute-done.12.refs_1_ = bf16[128,2048]{1,0:T(8,128)(2,1)S(1)} collective-permute-done((bf16[128,2048]{1,0:T(8,128)(2,1)S(1)}, bf16[128,2048]{1,0:T(8,128)(2,1)S(1)}, u32[]{:S(2)}, u32[]{:S(2)}) %collective-permute-start.12) | collective-permute-done | bytes 524320 | tf_op jit(solution)/shard_map/ppermute | solution.py:907
  317.2 4.4 collective-permute-start.16
  333.2 9.4 %layer_output.1 = bf16[1024,2048]{1,0:T(8,128)(2,1)} custom-call(f32[8,128]{1,0:T(8,128)} %get-tuple-element.242.sq_ref, bf16[1024,2048]{1,0:T(8,128)(2,1)} %x_ref.6, bf16[1024,2048]{1,0:T(8,128)(2,1)} %convolution_convert_fusion.1.refs_0_, bf16[1024,2048]{1,0:T(8,128)(2,1)} %collective-permute-done.5.refs_1_), custom_call_target="tpu_custom_call" | custom-call | flops 1000 | bytes 1000 | tf_op jit(solution)/shard_map/layer_output/pallas_call | solution.py:839
  356.5 5.5 %collective-permute-done.19.refs_1_ = bf16[256,384]{1,0:T(8,128)(2,1)S(1)} collective-permute-done((bf16[256,384]{1,0:T(8,128)(2,1)}, bf16[256,384]{1,0:T(8,128)(2,1)S(1)}, u32[]{:S(2)}, u32[]{:S(2)}) %collective-permute-start.19) | collective-permute-done | bytes 196640 | tf_op jit(solution)/shard_map/ppermute | solution.py:907
  371.6 14.0 %collective-permute-done.21.refs_1_ = bf16[128,2048]{1,0:T(8,128)(2,1)S(1)} collective-permute-done((bf16[128,2048]{1,0:T(8,128)(2,1)}, bf16[128,2048]{1,0:T(8,128)(2,1)S(1)}, u32[]{:S(2)}, u32[]{:S(2)}) %collective-permute-start.21) | collective-permute-done | bytes 524320 | tf_op jit(solution)/shard_map/ppermute | solution.py:907
  388.4 14.8 %collective-permute-done.22.refs_1_ = bf16[128,384]{1,0:T(8,128)(2,1)S(1)} collective-permute-done((bf16[128,384]{1,0:T(8,128)(2,1)}, bf16[128,384]{1,0:T(8,128)(2,1)S(1)}, u32[]{:S(2)}, u32[]{:S(2)}) %collective-permute-start.22) | collective-permute-done | bytes 98336 | tf_op jit(solution)/shard_map/ppermute | solution.py:907
  421.5 11.4 %input_grad_finish.1 = bf16[1024,2048]{1,0:T(8,128)(2,1)} custom-call(bf16[1024,2048]{1,0:T(8,128)(2,1)} %x_ref.6, bf16[1024,2048]{1,0:T(8,128)(2,1)} %cot_ref.3, f32[1024,1]{1,0:T(8,128)} %get-tuple-element.140.inv_ref, f32[1,2048]{1,0:T(1,128)} %bitcast.57, bf16[1024,2048]{1,0:T(8,128)(2,1)} %get-tuple-element.204.refs_0_, ...), custom_call_target="tpu_custom_call" | custom-call | flops 1000 | bytes 1000 | tf_op jit(solution)/shard_map/input_grad_finish/pallas_call | solution.py:865
  436.8 4.9 %collective-permute-start.33 = (bf16[1024,256]{1,0:T(8,128)(2,1)S(1)}, bf16[1024,256]{1,0:T(8,128)(2,1)S(1)}, u32[]{:S(2)}, u32[]{:S(2)}) collective-permute-start(bf16[1024,256]{1,0:T(8,128)(2,1)S(1)} %constant_dynamic-update-slice_fusion.4), channel_id=1, source_target_pairs={{0,2},{2,0},{4,6},{6,4},{8,10},{10,8},{12,14},{14,12},{16,18},{18,... | collective-permute-start | bytes 1572872 | tf_op jit(solution)/shard_map/ppermute | solution.py:907
  (218 shorter events, 99.6 us)
Async XLA Ops:
  12.4 122.3 %collective-permute-start.1 = (bf16[2,2048,1024]{2,1,0:T(8,128)(2,1)}, bf16[2,2048,1024]{2,1,0:T(8,128)(2,1)}, u32[]{:S(2)}, u32[]{:S(2)}) collective-permute-start(bf16[2,2048,1024]{2,1,0:T(8,128)(2,1)} %get-tuple-element.118.mine_ref), channel_id=1, source_target_pairs={{0,2},{2,0},{4,6},{6,4},{8,10},{10,8},{12,14},{14,12},{16,18},{18,... | collective-permute-start | bytes 25165832 | tf_op jit(solution)/shard_map/ppermute | solution.py:907
  95.3 16.9 %collective-permute-start = (f32[16,128]{1,0:T(8,128)S(1)}, f32[16,128]{1,0:T(8,128)S(1)}, u32[]{:S(2)}, u32[]{:S(2)}) collective-permute-start(f32[16,128]{1,0:T(8,128)S(1)} %pad_maximum_fusion.3), channel_id=1, source_target_pairs={{0,1},{1,0},{2,3},{3,2},{4,5},{5,4},{6,7},{7,6},{8,9},{9,8},{10,11... | collective-permute-start | bytes 24584 | tf_op jit(solution)/shard_map/ppermute | solution.py:887
  98.1 36.6 %collective-permute-start.2 = (bf16[1024,2048]{1,0:T(8,128)(2,1)}, bf16[1024,2048]{1,0:T(8,128)(2,1)}, u32[]{:S(2)}, u32[]{:S(2)}) collective-permute-start(bf16[1024,2048]{1,0:T(8,128)(2,1)} %get-tuple-element.121.rest_0_), channel_id=1, source_target_pairs={{0,2},{2,0},{4,6},{6,4},{8,10},{10,8},{12,14},{14,12},{16,18},{18,... | collective-permute-start | bytes 12582920 | tf_op jit(solution)/shard_map/ppermute | solution.py:907
  127.4 26.0 %collective-permute-start.4 = (bf16[1024,2048]{1,0:T(8,128)(2,1)}, bf16[1024,2048]{1,0:T(8,128)(2,1)}, u32[]{:S(2)}, u32[]{:S(2)}) collective-permute-start(bf16[1024,2048]{1,0:T(8,128)(2,1)} %get-tuple-element.123.rest_0_.dz_ref), channel_id=1, source_target_pairs={{0,2},{2,0},{4,6},{6,4},{8,10},{10,8},{12,14},{14,12},{16,18},{18,... | collective-permute-start | bytes 12582920 | tf_op jit(solution)/shard_map/ppermute | solution.py:907
  127.6 97.5 %collective-permute-start.5 = (bf16[1024,2048]{1,0:T(8,128)(2,1)}, bf16[1024,2048]{1,0:T(8,128)(2,1)}, u32[]{:S(2)}, u32[]{:S(2)}) collective-permute-start(bf16[1024,2048]{1,0:T(8,128)(2,1)} %convolution_convert_fusion.1.refs_0_), channel_id=1, source_target_pairs={{0,1},{1,0},{2,3},{3,2},{4,5},{5,4},{6,7},{7,6},{8,9},{9,8},{10,11... | collective-permute-start | bytes 12582920 | tf_op jit(solution)/shard_map/ppermute | solution.py:887
  150.7 74.4 %collective-permute-start.6 = (bf16[512,2048]{1,0:T(8,128)(2,1)}, bf16[512,2048]{1,0:T(8,128)(2,1)}, u32[]{:S(2)}, u32[]{:S(2)}) collective-permute-start(bf16[512,2048]{1,0:T(8,128)(2,1)} %get-tuple-element.135), channel_id=1, source_target_pairs={{0,4},{2,6},{4,0},{6,2},{8,12},{10,14},{12,8},{14,10},{16,20},{18,... | collective-permute-start | bytes 6291464 | tf_op jit(solution)/shard_map/ppermute | solution.py:907
  224.0 39.9 %collective-permute-start.9 = (bf16[1024,2048]{1,0:T(8,128)(2,1)}, bf16[1024,2048]{1,0:T(8,128)(2,1)}, u32[]{:S(2)}, u32[]{:S(2)}) collective-permute-start(bf16[1024,2048]{1,0:T(8,128)(2,1)} %get-tuple-element.156.dx_ref.rest_0_), channel_id=1, source_target_pairs={{0,2},{2,0},{4,6},{6,4},{8,10},{10,8},{12,14},{14,12},{16,18},{18,... | collective-permute-start | bytes 12582920 | tf_op jit(solution)/shard_map/ppermute | solution.py:907
  224.6 37.0 %collective-permute-start.8 = (bf16[1024,256]{1,0:T(8,128)(2,1)}, bf16[1024,256]{1,0:T(8,128)(2,1)}, u32[]{:S(2)}, u32[]{:S(2)}) collective-permute-start(bf16[1024,256]{1,0:T(8,128)(2,1)} %get-tuple-element.145.dbc_ref), channel_id=1, source_target_pairs={{0,1},{1,0},{2,3},{3,2},{4,5},{5,4},{6,7},{7,6},{8,9},{9,8},{10,11... | collective-permute-start | bytes 1572872 | tf_op jit(solution)/shard_map/ppermute | solution.py:887
  224.8 53.6 %collective-permute-start.10 = (bf16[512,2048]{1,0:T(8,128)(2,1)}, bf16[512,2048]{1,0:T(8,128)(2,1)S(1)}, u32[]{:S(2)}, u32[]{:S(2)}) collective-permute-start(bf16[512,2048]{1,0:T(8,128)(2,1)} %get-tuple-element.150), channel_id=1, source_target_pairs={{0,4},{2,6},{4,0},{6,2},{8,12},{10,14},{12,8},{14,10},{16,20},{18,... | collective-permute-start | bytes 6291464 | tf_op jit(solution)/shard_map/ppermute | solution.py:907
  228.4 29.8 %collective-permute-start.7 = (bf16[256,2048]{1,0:T(8,128)(2,1)}, bf16[256,2048]{1,0:T(8,128)(2,1)S(1)}, u32[]{:S(2)}, u32[]{:S(2)}) collective-permute-start(bf16[256,2048]{1,0:T(8,128)(2,1)} %get-tuple-element.143), channel_id=1, source_target_pairs={{0,8},{2,10},{4,12},{6,14},{8,0},{10,2},{12,4},{14,6},{16,24},{18,... | collective-permute-start | bytes 3145736 | tf_op jit(solution)/shard_map/ppermute | solution.py:907
  257.0 164.5 %collective-permute-start.29 = (bf16[1024,2048]{1,0:T(8,128)(2,1)}, bf16[1024,2048]{1,0:T(8,128)(2,1)}, u32[]{:S(2)}, u32[]{:S(2)}) collective-permute-start(bf16[1024,2048]{1,0:T(8,128)(2,1)} %get-tuple-element.204.refs_0_), channel_id=1, source_target_pairs={{0,1},{1,0},{2,3},{3,2},{4,5},{5,4},{6,7},{7,6},{8,9},{9,8},{10,11... | collective-permute-start | bytes 12582920 | tf_op jit(solution)/shard_map/ppermute | solution.py:887
  275.6 48.0 %collective-permute-start.13 = (bf16[512,1280]{1,0:T(8,128)(2,1)}, bf16[512,1280]{1,0:T(8,128)(2,1)}, u32[]{:S(2)}, u32[]{:S(2)}) collective-permute-start(bf16[512,1280]{1,0:T(8,128)(2,1)} %get-tuple-element.148), channel_id=1, source_target_pairs={{0,4},{2,6},{4,0},{6,2},{8,12},{10,14},{12,8},{14,10},{16,20},{18,... | collective-permute-start | bytes 3932168 | tf_op jit(solution)/shard_map/ppermute | solution.py:907
  283.1 46.7 %collective-permute-start.15 = (bf16[256,2048]{1,0:T(8,128)(2,1)}, bf16[256,2048]{1,0:T(8,128)(2,1)S(1)}, u32[]{:S(2)}, u32[]{:S(2)}) collective-permute-start(bf16[256,2048]{1,0:T(8,128)(2,1)} %get-tuple-element.165), channel_id=1, source_target_pairs={{0,8},{2,10},{4,12},{6,14},{8,0},{10,2},{12,4},{14,6},{16,24},{18,... | collective-permute-start | bytes 3145736 | tf_op jit(solution)/shard_map/ppermute | solution.py:907
  283.2 34.0 %collective-permute-start.12 = (bf16[128,2048]{1,0:T(8,128)(2,1)S(1)}, bf16[128,2048]{1,0:T(8,128)(2,1)S(1)}, u32[]{:S(2)}, u32[]{:S(2)}) collective-permute-start(bf16[128,2048]{1,0:T(8,128)(2,1)S(1)} %copy-done.33), channel_id=1, source_target_pairs={{0,16},{2,18},{4,20},{6,22},{8,24},{10,26},{12,28},{14,30},{16,0},... | collective-permute-start | bytes 1572872 | tf_op jit(solution)/shard_map/ppermute | solution.py:907
  295.5 31.6 %collective-permute-start.14 = (bf16[512,384]{1,0:T(8,128)(2,1)}, bf16[512,384]{1,0:T(8,128)(2,1)S(1)}, u32[]{:S(2)}, u32[]{:S(2)}) collective-permute-start(bf16[512,384]{1,0:T(8,128)(2,1)} %get-tuple-element.155), channel_id=1, source_target_pairs={{0,4},{2,6},{4,0},{6,2},{8,12},{10,14},{12,8},{14,10},{16,20},{18,... | collective-permute-start | bytes 1179656 | tf_op jit(solution)/shard_map/ppermute | solution.py:907
  317.2 29.3 %collective-permute-start.16 = (bf16[512,768]{1,0:T(8,128)(2,1)}, bf16[512,768]{1,0:T(8,128)(2,1)S(1)}, u32[]{:S(2)}, u32[]{:S(2)}) collective-permute-start(bf16[512,768]{1,0:T(8,128)(2,1)} %get-tuple-element.157), channel_id=1, source_target_pairs={{0,8},{2,10},{4,12},{6,14},{8,0},{10,2},{12,4},{14,6},{16,24},{18,... | collective-permute-start | bytes 2359304 | tf_op jit(solution)/shard_map/ppermute | solution.py:907
  326.2 26.7 %collective-permute-start.18 = (bf16[256,1280]{1,0:T(8,128)(2,1)}, bf16[256,1280]{1,0:T(8,128)(2,1)S(1)}, u32[]{:S(2)}, u32[]{:S(2)}) collective-permute-start(bf16[256,1280]{1,0:T(8,128)(2,1)} %get-tuple-element.185), channel_id=1, source_target_pairs={{0,8},{2,10},{4,12},{6,14},{8,0},{10,2},{12,4},{14,6},{16,24},{18,... | collective-permute-start | bytes 1966088 | tf_op jit(solution)/shard_map/ppermute | solution.py:907
  349.5 36.1 %collective-permute-start.21 = (bf16[128,2048]{1,0:T(8,128)(2,1)}, bf16[128,2048]{1,0:T(8,128)(2,1)S(1)}, u32[]{:S(2)}, u32[]{:S(2)}) collective-permute-start(bf16[128,2048]{1,0:T(8,128)(2,1)} %get-tuple-element.192), channel_id=1, source_target_pairs={{0,16},{2,18},{4,20},{6,22},{8,24},{10,26},{12,28},{14,30},{16,0},... | collective-permute-start | bytes 1572872 | tf_op jit(solution)/shard_map/ppermute | solution.py:907
  353.0 52.4 %collective-permute-start.23 = (bf16[256,768]{1,0:T(8,128)(2,1)}, bf16[256,768]{1,0:T(8,128)(2,1)S(1)}, u32[]{:S(2)}, u32[]{:S(2)}) collective-permute-start(bf16[256,768]{1,0:T(8,128)(2,1)} %get-tuple-element.196), channel_id=1, source_target_pairs={{0,16},{2,18},{4,20},{6,22},{8,24},{10,26},{12,28},{14,30},{16,0},... | collective-permute-start | bytes 1179656 | tf_op jit(solution)/shard_map/ppermute | solution.py:907
  364.4 38.8 %collective-permute-start.22 = (bf16[128,384]{1,0:T(8,128)(2,1)}, bf16[128,384]{1,0:T(8,128)(2,1)S(1)}, u32[]{:S(2)}, u32[]{:S(2)}) collective-permute-start(bf16[128,384]{1,0:T(8,128)(2,1)} %get-tuple-element.194), channel_id=1, source_target_pairs={{0,16},{2,18},{4,20},{6,22},{8,24},{10,26},{12,28},{14,30},{16,0},... | collective-permute-start | bytes 294920 | tf_op jit(solution)/shard_map/ppermute | solution.py:907
  368.0 40.9 %collective-permute-start.24 = (f32[136,128]{1,0:T(8,128)}, f32[136,128]{1,0:T(8,128)S(1)}, u32[]{:S(2)}, u32[]{:S(2)}) collective-permute-start(f32[136,128]{1,0:T(8,128)} %add_parts.30.refs_0_), channel_id=1, source_target_pairs={{0,8},{2,10},{4,12},{6,14},{8,0},{10,2},{12,4},{14,6},{16,24},{18,... | collective-permute-start | bytes 208904 | tf_op jit(solution)/shard_map/ppermute | solution.py:907
  388.4 26.9 %collective-permute-start.26 = (bf16[128,1280]{1,0:T(8,128)(2,1)S(1)}, bf16[128,1280]{1,0:T(8,128)(2,1)S(1)}, u32[]{:S(2)}, u32[]{:S(2)}) collective-permute-start(bf16[128,1280]{1,0:T(8,128)(2,1)S(1)} %copy-done.34), channel_id=1, source_target_pairs={{0,16},{2,18},{4,20},{6,22},{8,24},{10,26},{12,28},{14,30},{16,0},... | collective-permute-start | bytes 983048 | tf_op jit(solution)/shard_map/ppermute | solution.py:907
  414.4 18.5 %collective-permute-start.31 = (bf16[128,768]{1,0:T(8,128)(2,1)}, bf16[128,768]{1,0:T(8,128)(2,1)S(1)}, u32[]{:S(2)}, u32[]{:S(2)}) collective-permute-start(bf16[128,768]{1,0:T(8,128)(2,1)} %get-tuple-element.206), channel_id=1, source_target_pairs={{0,4},{2,6},{4,0},{6,2},{8,12},{10,14},{12,8},{14,10},{16,20},{18,... | collective-permute-start | bytes 589832 | tf_op jit(solution)/shard_map/ppermute | solution.py:907
  420.2 16.6 %collective-permute-start.32 = (bf16[512,256]{1,0:T(8,128)(2,1)S(1)}, bf16[512,256]{1,0:T(8,128)(2,1)S(1)}, u32[]{:S(2)}, u32[]{:S(2)}) collective-permute-start(bf16[512,256]{1,0:T(8,128)(2,1)S(1)} %constant_dynamic-update-slice_fusion.2), channel_id=1, source_target_pairs={{0,4},{2,6},{4,0},{6,2},{8,12},{10,14},{12,8},{14,10},{16,20},{18,... | collective-permute-start | bytes 786440 | tf_op jit(solution)/shard_map/ppermute | solution.py:907
  (49 other events, 432.7 us)
